TPU v7x, 32 devices: a whole 2x2x4 slice. The times are simulated.
32 devices in a mesh: depth: 8 (over y, x, core), kslab: 4 (over z).
Axes of the slice: x: 2, y: 2, z: 4, core: 2. Of those that a mesh axis runs over, the one named last changes fastest.
Arguments:
- spectra: bfloat16 [8, 2, 512, 1024], P('depth', None, 'kslab'), may hold values from -6 to 6
- green: bfloat16 [8, 8, 2, 512, 1024], P('depth', None, None, 'kslab'), may hold values from -1 to 1, as said below
- contrast: float32 [8, 512, 1024], P('depth', None, 'kslab'), may hold values from 0.3 to 3
Outputs:
- applied: bfloat16 [8, 2, 512, 1024], P('depth', None, None, 'kslab')
Inputs may be any that keep to these rules, and one draw needn't show every extreme that they name: green[t, s] equals green[s, t] for every pair of layers (reciprocity).
All inputs are finite; a program needn't handle non-finite values.
Results may differ from a plain program's by a relative error of at most 0.007.
Values may be sent and summed in bfloat16 or wider, within the bound.
No kernel may reach another device: no remote copies, remote signals or barrier semaphores. Data moves between devices by JAX's collectives and lax.ppermute only.
A program may use at most 128 MiB of HBM per device.

v0:
```python
import math

import jax
import jax.numpy as jnp
from jax import lax
from jax.experimental import pallas as pl
from jax.experimental.pallas import tpu as pltpu
from jax.sharding import PartitionSpec as P


F32 = jnp.float32
BF16 = jnp.bfloat16
ROWS = 16
FINE = 32
MIB = 1 << 20


def fourier_tables(length):
    indices = jnp.arange(length, dtype=jnp.int32)
    products = indices[:, None] * indices[None, :] % length
    angles = products.astype(F32) * (2.0 * math.pi / length)
    factor = 1.0 / math.sqrt(length)
    return (jnp.cos(angles) * factor).astype(BF16), (jnp.sin(angles) * factor).astype(BF16)


def on_any_device(spectra, green, contrast):
    lay_dev, _, kx_dev, ny = spectra.shape
    nx = contrast.shape[1]
    coeffs = green.astype(F32)
    sources = lax.all_gather(spectra, "depth", axis=0, tiled=True).astype(F32)[None]
    real_part = jnp.sum(coeffs[:, :, 0] * sources[:, :, 0] - coeffs[:, :, 1] * sources[:, :, 1], axis=1)
    imag_part = jnp.sum(coeffs[:, :, 0] * sources[:, :, 1] + coeffs[:, :, 1] * sources[:, :, 0], axis=1)
    rounded = jnp.stack([real_part, imag_part], axis=1).astype(BF16)
    table_y = jnp.concatenate(fourier_tables(ny), axis=1)
    rows = lay_dev * kx_dev
    from_real = jnp.dot(rounded[:, 0].reshape(rows, ny), table_y, preferred_element_type=F32)
    from_imag = jnp.dot(rounded[:, 1].reshape(rows, ny), table_y, preferred_element_type=F32)
    halfway_real = (from_real[:, :ny] - from_imag[:, ny:]).reshape(lay_dev, kx_dev, ny)
    halfway_imag = (from_real[:, ny:] + from_imag[:, :ny]).reshape(lay_dev, kx_dev, ny)
    halfway = jnp.stack([halfway_real, halfway_imag], axis=1).astype(BF16)
    table_x = jnp.concatenate(fourier_tables(nx), axis=0)
    stacked = jnp.einsum(
        "ak,nckd->ncad",
        table_x,
        lax.all_to_all(halfway, "kslab", split_axis=3, concat_axis=2, tiled=True),
        preferred_element_type=F32,
    )
    real_part = stacked[:, 0, :nx] - stacked[:, 1, nx:]
    imag_part = stacked[:, 0, nx:] + stacked[:, 1, :nx]
    return (jnp.stack([real_part, imag_part], axis=1) * contrast[:, None]).astype(BF16)


def in_vmem(x):
    return pltpu.with_memory_space_constraint(x, pltpu.VMEM)


def call(body, outs, ins, scratch=(), flops=0, vmem=24 * MIB):
    spec = pl.BlockSpec(memory_space=pltpu.VMEM)
    moved = sum(math.prod(v.shape) * v.dtype.itemsize for v in list(outs) + list(ins))
    return pl.pallas_call(
        body,
        out_shape=[pltpu.VMEM(o.shape, o.dtype) for o in outs],
        in_specs=[spec] * len(ins),
        out_specs=[spec] * len(outs),
        scratch_shapes=list(scratch),
        compiler_params=pltpu.CompilerParams(vmem_limit_bytes=vmem),
        cost_estimate=pl.CostEstimate(flops=flops, bytes_accessed=moved, transcendentals=0),
    )(*[in_vmem(v) for v in ins])


def struct(shape, dtype):
    return jax.ShapeDtypeStruct(shape, dtype)


def modulo(v, length):
    return v & (length - 1) if length & (length - 1) == 0 else lax.rem(v, length)


def fill_table(length, columns, coarse_ref, put):
    width = columns.shape[1]
    step = 2.0 * math.pi / length
    factor = 1.0 / math.sqrt(length)
    rows = lax.broadcasted_iota(jnp.int32, (length // FINE, width), 0) * FINE
    angle = modulo(rows * columns, length).astype(F32) * step
    coarse_ref[0, pl.ds(0, length // FINE)] = jnp.cos(angle) * factor
    coarse_ref[1, pl.ds(0, length // FINE)] = jnp.sin(angle) * factor
    rows = lax.broadcasted_iota(jnp.int32, (FINE, width), 0)
    angle = modulo(rows * columns, length).astype(F32) * step
    coarse_ref[2, pl.ds(0, FINE)] = jnp.cos(angle)
    coarse_ref[3, pl.ds(0, FINE)] = jnp.sin(angle)

    @pl.loop(0, length // FINE)
    def _(block):
        for left in range(0, width, 256):
            cols = pl.ds(left, min(256, width - left))
            cos_c, sin_c = coarse_ref[0, pl.ds(block, 1), cols], coarse_ref[1, pl.ds(block, 1), cols]
            cos_f, sin_f = coarse_ref[2, pl.ds(0, FINE), cols], coarse_ref[3, pl.ds(0, FINE), cols]
            row = pl.ds(pl.multiple_of(block * FINE, FINE), FINE)
            put(row, left, cols, cos_c * cos_f - sin_c * sin_f, sin_c * cos_f + cos_c * sin_f)


def split_rows(own, parts):
    planes, _, ny = own.shape

    def body(own_ref, *refs):
        outs, sems = refs[:-1], refs[-1]
        copies = [
            pltpu.make_async_copy(own_ref.at[:, pl.ds(start, size)], ref, sems.at[i])
            for i, ((start, size), ref) in enumerate(zip(parts, outs))
        ]
        for copy in copies:
            copy.start()
        for copy in copies:
            copy.wait()

    return pl.pallas_call(
        body,
        out_shape=[pltpu.VMEM((planes, size, ny), own.dtype) for _, size in parts],
        in_specs=[pl.BlockSpec(memory_space=pl.ANY)],
        out_specs=[pl.BlockSpec(memory_space=pltpu.VMEM)] * len(parts),
        scratch_shapes=[pltpu.SemaphoreType.DMA((len(parts),))],
        compiler_params=pltpu.CompilerParams(vmem_limit_bytes=8 * MIB),
        cost_estimate=pl.CostEstimate(flops=0, bytes_accessed=MIB, transcendentals=0),
        name="split_rows",
    )(pltpu.with_memory_space_constraint(own, pltpu.HBM))


def prepare(green, contrast, kx_dev, parts, slabs):
    ny, nx = green.shape[3], contrast.shape[0]
    args = [green, contrast]

    def body(*refs):
        given, (ty_ref, *tx_refs) = refs[:2], refs[2 : 3 + len(parts)]
        kept, (coarse_y, coarse_x, sems) = refs[3 + len(parts) : -3], refs[-3:]
        copies = [pltpu.make_async_copy(a, b, sems.at[i]) for i, (a, b) in enumerate(zip(given, kept))]
        for copy in copies:
            copy.start()
        z = lax.axis_index("kslab")
        wide = ny // slabs
        lane = lax.broadcasted_iota(jnp.int32, (1, ny), 1)
        columns = jnp.bitwise_xor(lane // wide, z) * wide + lane % wide

        def put_y(row, left, cols, cos, sin):
            ty_ref[0, row, cols] = cos.astype(BF16)
            ty_ref[1, row, cols] = sin.astype(BF16)

        fill_table(ny, columns, coarse_y, put_y)
        for (start, size), tx_ref in zip(parts, tx_refs):
            lane = lax.broadcasted_iota(jnp.int32, (1, slabs * size), 1)
            columns = jnp.bitwise_xor(lane // size, z) * kx_dev + start + lane % size

            def put_x(row, left, cols, cos, sin):
                tx_ref[0, row, cols] = cos.astype(BF16)
                tx_ref[1, row, cols] = sin.astype(BF16)

            fill_table(nx, columns, coarse_x.at[:, :, pl.ds(0, slabs * size)], put_x)
        for copy in copies:
            copy.wait()

    outs = [struct((2, ny, ny), BF16)]
    outs += [struct((2, nx, slabs * size), BF16) for _, size in parts]
    outs += [struct(v.shape, v.dtype) for v in args]
    most = max(size for _, size in parts)
    anywhere, vmem = pl.BlockSpec(memory_space=pl.ANY), pl.BlockSpec(memory_space=pltpu.VMEM)
    made = pl.pallas_call(
        body,
        out_shape=[pltpu.VMEM(o.shape, o.dtype) for o in outs],
        in_specs=[anywhere] * 2,
        out_specs=[vmem] * len(outs),
        scratch_shapes=[
            pltpu.VMEM((4, max(ny // FINE, FINE), ny), F32),
            pltpu.VMEM((4, max(nx // FINE, FINE), slabs * most), F32),
            pltpu.SemaphoreType.DMA((2,)),
        ],
        compiler_params=pltpu.CompilerParams(vmem_limit_bytes=24 * MIB),
        cost_estimate=pl.CostEstimate(flops=8 * ny * ny, bytes_accessed=8 * MIB, transcendentals=0),
        name="prepare",
    )(*[pltpu.with_memory_space_constraint(v, pltpu.HBM) for v in args])
    return made[0], made[1 : 1 + len(parts)], made[1 + len(parts) :]


def add_sources(total, green_ref, sources, step, start, cols):
    real, imag = total
    whole = pl.ds(pl.multiple_of(start + step * ROWS, ROWS), ROWS)
    for ref, at, layer in sources:
        row = pl.ds(pl.multiple_of(at + step * ROWS, ROWS), ROWS)
        g_real, g_imag = green_ref[layer, 0, whole, cols].astype(F32), green_ref[layer, 1, whole, cols].astype(F32)
        s_real, s_imag = ref[0, row, cols].astype(F32), ref[1, row, cols].astype(F32)
        p_real = g_real * s_real - g_imag * s_imag
        p_imag = g_real * s_imag + g_imag * s_real
        real = p_real if real is None else real + p_real
        imag = p_imag if imag is None else imag + p_imag
    return real, imag


def early_sum(green, arrays, offsets, layers, start, size):
    ny = arrays[0].shape[2]

    def body(green_ref, *refs):
        total_ref = refs[-1]
        sources = list(zip(refs[:-1], offsets, layers()))

        @pl.loop(0, size // ROWS)
        def _(step):
            row = pl.ds(pl.multiple_of(step * ROWS, ROWS), ROWS)
            for left in range(0, ny, 256):
                cols = pl.ds(left, 256)
                total_ref[0, row, cols], total_ref[1, row, cols] = add_sources(
                    (None, None), green_ref, sources, step, start, cols
                )

    return call(body, [struct((2, size, ny), F32)], [green, *arrays], flops=8 * len(arrays) * size * ny)[0]


def finish_rows(green, total, arrays, layers, table_y, start, slabs, groups):
    _, size, ny = arrays[0].shape
    wide = ny // slabs

    def body(green_ref, total_ref, table_ref, *refs):
        ins, outs, left_ref = refs[: len(arrays)], refs[len(arrays) : -1], refs[-1]
        sources = [(ref, 0, layer) for ref, layer in zip(ins, layers())]

        @pl.loop(0, size // ROWS)
        def _(step):
            row = pl.ds(pl.multiple_of(step * ROWS, ROWS), ROWS)
            low = pl.ds(pl.multiple_of(size + step * ROWS, ROWS), ROWS)
            for left in range(0, ny, 256):
                cols = pl.ds(left, 256)
                begun = total_ref[0, row, cols], total_ref[1, row, cols]
                real, imag = add_sources(begun, green_ref, sources, step, start, cols)
                left_ref[row, pl.ds(left, 256)] = real.astype(BF16)
                left_ref[row, pl.ds(ny + left, 256)] = (-imag).astype(BF16)
                left_ref[low, pl.ds(left, 256)] = imag.astype(BF16)
                left_ref[low, pl.ds(ny + left, 256)] = real.astype(BF16)

        for group, out_ref in zip(groups, outs):
            for i, m in enumerate(group):
                cols = pl.ds(m * wide, wide)
                both = jnp.dot(left_ref[:, pl.ds(0, ny)], table_ref[0, :, cols], preferred_element_type=F32)
                both += jnp.dot(left_ref[:, pl.ds(ny, ny)], table_ref[1, :, cols], preferred_element_type=F32)
                out_ref[2 * i] = both[:size].astype(BF16)
                out_ref[2 * i + 1] = both[size:].astype(BF16)

    outs = [struct((2 * len(group), size, wide), BF16) for group in groups]
    flops = 8 * size * ny * ny
    return call(body, outs, [green, total, table_y, *arrays], [pltpu.VMEM((2 * size, 2 * ny), BF16)], flops)


def second_half(pair):
    count = pair.shape[0] // 2

    def body(pair_ref, out_ref):
        out_ref[...] = pair_ref[count:]

    return call(body, [struct((count, *pair.shape[1:]), pair.dtype)], [pair])[0]


def transform_x(table_x, blocks, size, total=None, contrast=None):
    arrays = []
    for array, _ in blocks:
        if not any(array is other for other in arrays):
            arrays.append(array)
    at = [next(i for i, other in enumerate(arrays) if other is array) for array, _ in blocks]
    wide = arrays[0].shape[2]
    nx = table_x.shape[1]
    half = len(blocks) * size
    tall = min(nx, 128)

    def fill(ins, right_ref):
        for m, (_, place) in enumerate(blocks):
            real, imag = ins[at[m]][place], ins[at[m]][place + 1]
            top, low = pl.ds(m * size, size), pl.ds(half + m * size, size)
            right_ref[top, pl.ds(0, wide)] = real
            right_ref[top, pl.ds(wide, wide)] = imag
            right_ref[low, pl.ds(0, wide)] = -imag
            right_ref[low, pl.ds(wide, wide)] = real

    def product(table_ref, right_ref, row):
        part = jnp.dot(table_ref[0, row, :], right_ref[pl.ds(0, half), :], preferred_element_type=F32)
        return part + jnp.dot(table_ref[1, row, :], right_ref[pl.ds(half, half), :], preferred_element_type=F32)

    def body(table_ref, *refs):
        ins, (out_ref, right_ref) = refs[:-2], refs[-2:]
        fill(ins, right_ref)
        for x in range(0, nx, tall):
            row = pl.ds(x, tall)
            part = product(table_ref, right_ref, row)
            out_ref[row, :] = part if total is None else part + ins[-1][row, :]

    def last_body(table_ref, *refs):
        ins, (out_ref, right_ref, kept_ref, sems) = refs[:-4], refs[-4:]
        total_ref, contrast_ref = ins[-2:]
        fill(ins, right_ref)
        copies = []
        for i, x in enumerate(range(0, nx, tall)):
            row = pl.ds(x, tall)
            part = product(table_ref, right_ref, row) + total_ref[row, :]
            scale = contrast_ref[row, :]
            kept_ref[0, row, :] = (part[:, :wide] * scale).astype(BF16)
            kept_ref[1, row, :] = (part[:, wide:] * scale).astype(BF16)
            copies.append(pltpu.make_async_copy(kept_ref.at[:, row], out_ref.at[:, row], sems.at[i]))
            copies[-1].start()
        for copy in copies:
            copy.wait()

    scratch = [pltpu.VMEM((2 * half, 2 * wide), BF16)]
    flops = 8 * nx * half * wide
    if contrast is None:
        ins = [table_x, *arrays] + ([] if total is None else [total])
        return call(body, [struct((nx, 2 * wide), F32)], ins, scratch, flops)[0]
    ins = [table_x, *arrays, total, contrast]
    return pl.pallas_call(
        last_body,
        out_shape=struct((2, nx, wide), BF16),
        in_specs=[pl.BlockSpec(memory_space=pltpu.VMEM)] * len(ins),
        out_specs=pl.BlockSpec(memory_space=pl.ANY),
        scratch_shapes=scratch + [pltpu.VMEM((2, nx, wide), BF16), pltpu.SemaphoreType.DMA((nx // tall,))],
        compiler_params=pltpu.CompilerParams(vmem_limit_bytes=24 * MIB),
        cost_estimate=pl.CostEstimate(flops=flops, bytes_accessed=4 * MIB, transcendentals=0),
        name="transform_x_last",
    )(*[in_vmem(v) for v in ins])


def on_cube_device(slabs, spectra, green, contrast):
    _, _, kx_dev, _ = spectra.shape
    parts = [(0, kx_dev // 2), (kx_dev // 2, kx_dev // 2)]
    own, green, contrast = spectra[0], green[0], contrast[0]

    swap = [(i, i ^ 1) for i in range(8)]
    out = [(i, i ^ 2 if i % 2 == 0 else i ^ 4) for i in range(8)]

    def send(v, route):
        return lax.ppermute(v, "depth", route)

    def layers(masks):
        def at():
            me = lax.axis_index("depth")
            c = lax.rem(me, 2)
            return [jnp.bitwise_xor(me, jnp.where(c == 0, m0, m1)) for m0, m1 in masks]

        return at

    owns = split_rows(own, parts)
    near = [send(v, out) for v in owns]
    own_swap = send(own, swap)
    table_y, table_x, (green, contrast) = prepare(green, contrast, kx_dev, parts, slabs)
    near_swap = [send(v, swap) for v in near]
    far = [send(own_swap[:, s : s + n], out) for s, n in parts]
    across = [send(v, out) for v in near_swap]
    field = None
    results = []
    for i, (start, size) in enumerate(parts):
        far_swap, across_swap = send(far[i], swap), send(across[i], swap)
        total = early_sum(
            green, [owns[i], own_swap, near[i], near_swap[i], far[i], far_swap], [0, start, 0, 0, 0, 0],
            layers([(0, 0), (1, 1), (2, 4), (5, 3), (3, 5), (4, 2)]), start, size,
        )
        relay = slabs == 4 and i < len(parts) - 1
        groups = [[0], [1], [2, 3]] if relay else [[m] for m in range(slabs)]
        halves = finish_rows(
            green, total, [across[i], across_swap], layers([(7, 7), (6, 6)]), table_y, start, slabs, groups
        )

        def hop(m, v):
            return lax.ppermute(v, "kslab", [(k, k ^ m) for k in range(slabs)])

        if relay:
            two, one = hop(2, halves[2]), hop(1, halves[1])
            results.append([(halves[0], 0), (one, 0), (two, 0), (two, 2)])
        else:
            results.append([(halves[0], 0)] + [(hop(m, halves[m]), 0) for m in range(1, slabs)])
    for result in results[:-1]:
        if slabs == 4:
            passed = second_half(result[3][0])
            result[3] = (lax.ppermute(passed, "kslab", [(k, k ^ 1) for k in range(slabs)]), 0)
    for i, (start, size) in enumerate(parts):
        field = transform_x(table_x[i], results[i], size, field, contrast if i == len(parts) - 1 else None)
    return field[None]


def solution(mesh):
    in_specs = (
        P("depth", None, "kslab", None),
        P("depth", None, None, "kslab", None),
        P("depth", None, "kslab"),
    )
    out_specs = P("depth", None, None, "kslab")
    depth, slabs = mesh.shape["depth"], mesh.shape["kslab"]

    def on_device(spectra, green, contrast):
        cube = depth == 8 and spectra.shape[0] == 1 and slabs & (slabs - 1) == 0
        if cube and spectra.shape[2] % 64 == 0 and (spectra.shape[3] // slabs) % 128 == 0:
            return on_cube_device(slabs, spectra, green, contrast)
        return on_any_device(spectra, green, contrast)

    return jax.shard_map(on_device, mesh=mesh, in_specs=in_specs, out_specs=out_specs, check_vma=False)
```

profile of v0, /device:TPU:0, one launch (start us, length us, event | category | flops | bytes accessed | tf_op | source)
XLA Modules:
  0.0 53.8 jit_solution(5986881112922957442)
XLA Ops:
  0.5 1.0 %split_rows.1 = (bf16[2,64,1024]{2,1,0:T(8,128)(2,1)S(1)}, bf16[2,64,1024]{2,1,0:T(8,128)(2,1)S(1)}) custom-call(bf16[2,128,1024]{2,1,0:T(8,128)(2,1)} %bitcast.7), custom_call_target="tpu_custom_call" | custom-call | bytes 1048576 | tf_op jit(solution)/shard_map/split_rows/pallas_call | solution.py:116
  1.5 2.5 %collective-permute-start.10 = (bf16[2,64,1024]{2,1,0:T(8,128)(2,1)S(1)}, bf16[2,64,1024]{2,1,0:T(8,128)(2,1)S(1)}, u32[]{:S(2)}, u32[]{:S(2)}) collective-permute-start(bf16[2,64,1024]{2,1,0:T(8,128)(2,1)S(1)} %get-tuple-element.28.refs_0_), channel_id=1, source_target_pairs={{0,8},{4,20},{8,0},{12,28},{16,24},{20,4},{24,16},{28,12},{1,9},{5... | collective-permute-start | bytes 786440 | tf_op jit(solution)/shard_map/ppermute | solution.py:333
  4.2 4.3 %collective-permute-done.10.refs_2_ = bf16[2,64,1024]{2,1,0:T(8,128)(2,1)S(1)} collective-permute-done((bf16[2,64,1024]{2,1,0:T(8,128)(2,1)S(1)}, bf16[2,64,1024]{2,1,0:T(8,128)(2,1)S(1)}, u32[]{:S(2)}, u32[]{:S(2)}) %collective-permute-start.10) | collective-permute-done | bytes 262176 | tf_op jit(solution)/shard_map/ppermute | solution.py:333
  8.4 2.8 %collective-permute-done.1.refs_2_ = bf16[2,64,1024]{2,1,0:T(8,128)(2,1)S(1)} collective-permute-done((bf16[2,64,1024]{2,1,0:T(8,128)(2,1)S(1)}, bf16[2,64,1024]{2,1,0:T(8,128)(2,1)S(1)}, u32[]{:S(2)}, u32[]{:S(2)}) %collective-permute-start.1) | collective-permute-done | bytes 262176 | tf_op jit(solution)/shard_map/ppermute | solution.py:333
  11.3 2.1 %collective-permute-start.12 = (bf16[2,64,1024]{2,1,0:T(8,128)(2,1)S(1)}, bf16[2,64,1024]{2,1,0:T(8,128)(2,1)S(1)}, u32[]{:S(2)}, u32[]{:S(2)}) collective-permute-start(bf16[2,64,1024]{2,1,0:T(8,128)(2,1)S(1)} %get-tuple-element.33), channel_id=1, source_target_pairs={{0,8},{4,20},{8,0},{12,28},{16,24},{20,4},{24,16},{28,12},{1,9},{5... | collective-permute-start | bytes 786440 | tf_op jit(solution)/shard_map/ppermute | solution.py:333
  13.5 1.9 %collective-permute-start.3 = (bf16[2,64,1024]{2,1,0:T(8,128)(2,1)S(1)}, bf16[2,64,1024]{2,1,0:T(8,128)(2,1)S(1)}, u32[]{:S(2)}, u32[]{:S(2)}) collective-permute-start(bf16[2,64,1024]{2,1,0:T(8,128)(2,1)S(1)} %get-tuple-element.34), channel_id=1, source_target_pairs={{0,8},{4,20},{8,0},{12,28},{16,24},{20,4},{24,16},{28,12},{1,9},{5... | collective-permute-start | bytes 786440 | tf_op jit(solution)/shard_map/ppermute | solution.py:333
  15.5 2.2 %collective-permute-done.12.refs_4_ = bf16[2,64,1024]{2,1,0:T(8,128)(2,1)S(1)} collective-permute-done((bf16[2,64,1024]{2,1,0:T(8,128)(2,1)S(1)}, bf16[2,64,1024]{2,1,0:T(8,128)(2,1)S(1)}, u32[]{:S(2)}, u32[]{:S(2)}) %collective-permute-start.12) | collective-permute-done | bytes 262176 | tf_op jit(solution)/shard_map/ppermute | solution.py:333
  17.7 2.8 %collective-permute-done.14.refs_0_ = bf16[2,64,1024]{2,1,0:T(8,128)(2,1)S(1)} collective-permute-done((bf16[2,64,1024]{2,1,0:T(8,128)(2,1)S(1)}, bf16[2,64,1024]{2,1,0:T(8,128)(2,1)S(1)}, u32[]{:S(2)}, u32[]{:S(2)}) %collective-permute-start.14) | collective-permute-done | bytes 262176 | tf_op jit(solution)/shard_map/ppermute | solution.py:333
  20.5 2.8 %collective-permute-done.3.refs_4_ = bf16[2,64,1024]{2,1,0:T(8,128)(2,1)S(1)} collective-permute-done((bf16[2,64,1024]{2,1,0:T(8,128)(2,1)S(1)}, bf16[2,64,1024]{2,1,0:T(8,128)(2,1)S(1)}, u32[]{:S(2)}, u32[]{:S(2)}) %collective-permute-start.3) | collective-permute-done | bytes 262176 | tf_op jit(solution)/shard_map/ppermute | solution.py:333
  23.4 2.8 %collective-permute-done.5.refs_0_ = bf16[2,64,1024]{2,1,0:T(8,128)(2,1)S(1)} collective-permute-done((bf16[2,64,1024]{2,1,0:T(8,128)(2,1)S(1)}, bf16[2,64,1024]{2,1,0:T(8,128)(2,1)S(1)}, u32[]{:S(2)}, u32[]{:S(2)}) %collective-permute-start.5) | collective-permute-done | bytes 262176 | tf_op jit(solution)/shard_map/ppermute | solution.py:333
  26.2 3.0 %prepare.1 = (bf16[2,1024,1024]{2,1,0:T(8,128)(2,1)S(1)}, bf16[2,512,256]{2,1,0:T(8,128)(2,1)S(1)}, bf16[2,512,256]{2,1,0:T(8,128)(2,1)S(1)}, bf16[8,2,128,1024]{3,2,1,0:T(8,128)(2,1)S(1)}, f32[512,256]{1,0:T(8,128)S(1)}) custom-call(bf16[8,2,128,1024]{3,2,1,0:T(8,128)(2,1)} %bitcast.4, f32[512,256]{1,0:T(8,128)} %bitcast.5), custom_call_target="tpu_custom_call" | custom-call | flops 8388608 | bytes 8388608 | tf_op jit(solution)/shard_map/prepare/pallas_call | solution.py:165
  29.2 0.9 %shard_map.39.total_ref = f32[2,64,1024]{2,1,0:T(8,128)S(1)} custom-call(bf16[8,2,128,1024]{3,2,1,0:T(8,128)(2,1)S(1)} %get-tuple-element.20.green_ref, bf16[2,64,1024]{2,1,0:T(8,128)(2,1)S(1)} %get-tuple-element.28.refs_0_, bf16[2,128,1024]{2,1,0:T(8,128)(2,1)S(1)} %collective-permute-done.refs_1_, ...), custom_call_target="tpu_custom_call" | custom-call | flops 3145728 | bytes 6553600 | tf_op jit(solution)/shard_map/pallas_call | solution.py:60
  30.1 1.0 %shard_map.40 = (bf16[2,64,256]{2,1,0:T(8,128)(2,1)S(1)}, bf16[2,64,256]{2,1,0:T(8,128)(2,1)S(1)}, bf16[4,64,256]{2,1,0:T(8,128)(2,1)S(1)}) custom-call(bf16[8,2,128,1024]{3,2,1,0:T(8,128)(2,1)S(1)} %get-tuple-element.20.green_ref, f32[2,64,1024]{2,1,0:T(8,128)S(1)} %shard_map.39.total_ref, bf16[2,1024,1024]{2,1,0:T(8,128)(2,1)S(1)} %get-tuple-element.22.table_ref, ...), custom_call_target="tpu_custom_call" | custom-call | flops 536870912 | bytes 9699328 | tf_op jit(solution)/shard_map/pallas_call | solution.py:60
  31.1 3.2 %collective-permute-start.17 = (bf16[4,64,256]{2,1,0:T(8,128)(2,1)S(1)}, bf16[4,64,256]{2,1,0:T(8,128)(2,1)S(1)}, u32[]{:S(2)}, u32[]{:S(2)}) collective-permute-start(bf16[4,64,256]{2,1,0:T(8,128)(2,1)S(1)} %get-tuple-element.31), channel_id=1, source_target_pairs={{0,2},{1,3},{2,0},{3,1},{4,6},{5,7},{6,4},{7,5},{8,10},{9,11},{10,... | collective-permute-start | bytes 393224 | tf_op jit(solution)/shard_map/ppermute | solution.py:365
  34.3 1.6 %collective-permute-start.16 = (bf16[2,64,256]{2,1,0:T(8,128)(2,1)S(1)}, bf16[2,64,256]{2,1,0:T(8,128)(2,1)S(1)}, u32[]{:S(2)}, u32[]{:S(2)}) collective-permute-start(bf16[2,64,256]{2,1,0:T(8,128)(2,1)S(1)} %get-tuple-element.30), channel_id=1, source_target_pairs={{0,1},{1,0},{2,3},{3,2},{4,5},{5,4},{6,7},{7,6},{8,9},{9,8},{10,11... | collective-permute-start | bytes 196616 | tf_op jit(solution)/shard_map/ppermute | solution.py:365
  35.9 0.8 %shard_map.37.total_ref = f32[2,64,1024]{2,1,0:T(8,128)S(1)} custom-call(bf16[8,2,128,1024]{3,2,1,0:T(8,128)(2,1)S(1)} %get-tuple-element.20.green_ref, bf16[2,64,1024]{2,1,0:T(8,128)(2,1)S(1)} %get-tuple-element.21.refs_0_, bf16[2,128,1024]{2,1,0:T(8,128)(2,1)S(1)} %collective-permute-done.refs_1_, bf16[2,64,1024]{2,1,0:T(8,128)(2,1)S(1)} %collective-permute-done.1.refs_2_, ...), custom_call_target="tpu_custom_call" | custom-call | flops 3145728 | bytes 6553600 | tf_op jit(solution)/shard_map/pallas_call | solution.py:60
  36.7 4.5 %collective-permute-done.17.pair_ref.refs_2_ = bf16[4,64,256]{2,1,0:T(8,128)(2,1)S(1)} collective-permute-done((bf16[4,64,256]{2,1,0:T(8,128)(2,1)S(1)}, bf16[4,64,256]{2,1,0:T(8,128)(2,1)S(1)}, u32[]{:S(2)}, u32[]{:S(2)}) %collective-permute-start.17) | collective-permute-done | bytes 131104 | tf_op jit(solution)/shard_map/ppermute | solution.py:365
  41.2 0.7 %collective-permute-start.18 = (bf16[2,64,256]{2,1,0:T(8,128)(2,1)S(1)}, bf16[2,64,256]{2,1,0:T(8,128)(2,1)S(1)}, u32[]{:S(2)}, u32[]{:S(2)}) collective-permute-start(bf16[2,64,256]{2,1,0:T(8,128)(2,1)S(1)} %shard_map.41), channel_id=1, source_target_pairs={{0,1},{1,0},{2,3},{3,2},{4,5},{5,4},{6,7},{7,6},{8,9},{9,8},{10,11... | collective-permute-start | bytes 196616 | tf_op jit(solution)/shard_map/ppermute | solution.py:375
  42.0 1.0 %shard_map.38 = (bf16[2,64,256]{2,1,0:T(8,128)(2,1)S(1)}, bf16[2,64,256]{2,1,0:T(8,128)(2,1)S(1)}, bf16[2,64,256]{2,1,0:T(8,128)(2,1)S(1)}, bf16[2,64,256]{2,1,0:T(8,128)(2,1)S(1)}) custom-call(bf16[8,2,128,1024]{3,2,1,0:T(8,128)(2,1)S(1)} %get-tuple-element.20.green_ref, f32[2,64,1024]{2,1,0:T(8,128)S(1)} %shard_map.37.total_ref, ...), custom_call_target="tpu_custom_call" | custom-call | flops 536870912 | bytes 9699328 | tf_op jit(solution)/shard_map/pallas_call | solution.py:60
  43.0 1.3 %collective-permute-start.7 = (bf16[2,64,256]{2,1,0:T(8,128)(2,1)S(1)}, bf16[2,64,256]{2,1,0:T(8,128)(2,1)S(1)}, u32[]{:S(2)}, u32[]{:S(2)}) collective-permute-start(bf16[2,64,256]{2,1,0:T(8,128)(2,1)S(1)} %get-tuple-element.24), channel_id=1, source_target_pairs={{0,1},{1,0},{2,3},{3,2},{4,5},{5,4},{6,7},{7,6},{8,9},{9,8},{10,11... | collective-permute-start | bytes 196616 | tf_op jit(solution)/shard_map/ppermute | solution.py:365
  44.3 2.2 %collective-permute-start.8 = (bf16[2,64,256]{2,1,0:T(8,128)(2,1)S(1)}, bf16[2,64,256]{2,1,0:T(8,128)(2,1)S(1)}, u32[]{:S(2)}, u32[]{:S(2)}) collective-permute-start(bf16[2,64,256]{2,1,0:T(8,128)(2,1)S(1)} %get-tuple-element.25), channel_id=1, source_target_pairs={{0,2},{1,3},{2,0},{3,1},{4,6},{5,7},{6,4},{7,5},{8,10},{9,11},{10,... | collective-permute-start | bytes 196616 | tf_op jit(solution)/shard_map/ppermute | solution.py:365
  46.5 1.4 %collective-permute-start.9 = (bf16[2,64,256]{2,1,0:T(8,128)(2,1)S(1)}, bf16[2,64,256]{2,1,0:T(8,128)(2,1)S(1)}, u32[]{:S(2)}, u32[]{:S(2)}) collective-permute-start(bf16[2,64,256]{2,1,0:T(8,128)(2,1)S(1)} %get-tuple-element.26), channel_id=1, source_target_pairs={{0,3},{1,2},{2,1},{3,0},{4,7},{5,6},{6,5},{7,4},{8,11},{9,10},{10,... | collective-permute-start | bytes 196616 | tf_op jit(solution)/shard_map/ppermute | solution.py:365
  48.3 4.4 %collective-permute-done.8.refs_2_ = bf16[2,64,256]{2,1,0:T(8,128)(2,1)S(1)} collective-permute-done((bf16[2,64,256]{2,1,0:T(8,128)(2,1)S(1)}, bf16[2,64,256]{2,1,0:T(8,128)(2,1)S(1)}, u32[]{:S(2)}, u32[]{:S(2)}) %collective-permute-start.8) | collective-permute-done | bytes 65568 | tf_op jit(solution)/shard_map/ppermute | solution.py:365
  52.7 1.1 %transform_x_last.1 = bf16[2,512,256]{2,1,0:T(8,128)(2,1)} custom-call(bf16[2,512,256]{2,1,0:T(8,128)(2,1)S(1)} %get-tuple-element.19.table_ref, bf16[2,64,256]{2,1,0:T(8,128)(2,1)S(1)} %get-tuple-element.23.refs_0_, bf16[2,64,256]{2,1,0:T(8,128)(2,1)S(1)} %collective-permute-done.7.refs_1_, bf16[2,64,256]{2,1,0:T(8,128)(2,1)S(1)} %collective-permute-done.8.refs_2_, ...), custom_call_target="tpu_custom_call" | custom-call | flops 268435456 | bytes 4194304 | tf_op jit(solution)/shard_map/transform_x_last/pallas_call | solution.py:312
  (24 shorter events, 1.3 us)
Async XLA Ops:
  0.0 11.3 %collective-permute-start = (bf16[2,128,1024]{2,1,0:T(8,128)(2,1)}, bf16[2,128,1024]{2,1,0:T(8,128)(2,1)S(1)}, u32[]{:S(2)}, u32[]{:S(2)}) collective-permute-start(bf16[2,128,1024]{2,1,0:T(8,128)(2,1)} %bitcast.6), channel_id=1, source_target_pairs={{0,4},{4,0},{8,12},{12,8},{16,20},{20,16},{24,28},{28,24},{1,5},{5... | collective-permute-start | bytes 1572872 | tf_op jit(solution)/shard_map/ppermute | solution.py:333
  1.5 6.9 %collective-permute-start.10 = (bf16[2,64,1024]{2,1,0:T(8,128)(2,1)S(1)}, bf16[2,64,1024]{2,1,0:T(8,128)(2,1)S(1)}, u32[]{:S(2)}, u32[]{:S(2)}) collective-permute-start(bf16[2,64,1024]{2,1,0:T(8,128)(2,1)S(1)} %get-tuple-element.28.refs_0_), channel_id=1, source_target_pairs={{0,8},{4,20},{8,0},{12,28},{16,24},{20,4},{24,16},{28,12},{1,9},{5... | collective-permute-start | bytes 786440 | tf_op jit(solution)/shard_map/ppermute | solution.py:333
  4.1 7.2 %collective-permute-start.1 = (bf16[2,64,1024]{2,1,0:T(8,128)(2,1)S(1)}, bf16[2,64,1024]{2,1,0:T(8,128)(2,1)S(1)}, u32[]{:S(2)}, u32[]{:S(2)}) collective-permute-start(bf16[2,64,1024]{2,1,0:T(8,128)(2,1)S(1)} %get-tuple-element.21.refs_0_), channel_id=1, source_target_pairs={{0,8},{4,20},{8,0},{12,28},{16,24},{20,4},{24,16},{28,12},{1,9},{5... | collective-permute-start | bytes 786440 | tf_op jit(solution)/shard_map/ppermute | solution.py:333
  8.4 4.9 %collective-permute-start.11 = (bf16[2,64,1024]{2,1,0:T(8,128)(2,1)S(1)}, bf16[2,64,1024]{2,1,0:T(8,128)(2,1)S(1)}, u32[]{:S(2)}, u32[]{:S(2)}) collective-permute-start(bf16[2,64,1024]{2,1,0:T(8,128)(2,1)S(1)} %collective-permute-done.10.refs_2_), channel_id=1, source_target_pairs={{0,4},{4,0},{8,12},{12,8},{16,20},{20,16},{24,28},{28,24},{1,5},{5... | collective-permute-start | bytes 786440 | tf_op jit(solution)/shard_map/ppermute | solution.py:333
  11.3 4.2 %collective-permute-start.2 = (bf16[2,64,1024]{2,1,0:T(8,128)(2,1)S(1)}, bf16[2,64,1024]{2,1,0:T(8,128)(2,1)S(1)}, u32[]{:S(2)}, u32[]{:S(2)}) collective-permute-start(bf16[2,64,1024]{2,1,0:T(8,128)(2,1)S(1)} %collective-permute-done.1.refs_2_), channel_id=1, source_target_pairs={{0,4},{4,0},{8,12},{12,8},{16,20},{20,16},{24,28},{28,24},{1,5},{5... | collective-permute-start | bytes 786440 | tf_op jit(solution)/shard_map/ppermute | solution.py:333
  11.3 6.4 %collective-permute-start.12 = (bf16[2,64,1024]{2,1,0:T(8,128)(2,1)S(1)}, bf16[2,64,1024]{2,1,0:T(8,128)(2,1)S(1)}, u32[]{:S(2)}, u32[]{:S(2)}) collective-permute-start(bf16[2,64,1024]{2,1,0:T(8,128)(2,1)S(1)} %get-tuple-element.33), channel_id=1, source_target_pairs={{0,8},{4,20},{8,0},{12,28},{16,24},{20,4},{24,16},{28,12},{1,9},{5... | collective-permute-start | bytes 786440 | tf_op jit(solution)/shard_map/ppermute | solution.py:333
  13.4 7.2 %collective-permute-start.14 = (bf16[2,64,1024]{2,1,0:T(8,128)(2,1)S(1)}, bf16[2,64,1024]{2,1,0:T(8,128)(2,1)S(1)}, u32[]{:S(2)}, u32[]{:S(2)}) collective-permute-start(bf16[2,64,1024]{2,1,0:T(8,128)(2,1)S(1)} %collective-permute-done.11.refs_3_), channel_id=1, source_target_pairs={{0,8},{4,20},{8,0},{12,28},{16,24},{20,4},{24,16},{28,12},{1,9},{5... | collective-permute-start | bytes 786440 | tf_op jit(solution)/shard_map/ppermute | solution.py:333
  13.5 9.9 %collective-permute-start.3 = (bf16[2,64,1024]{2,1,0:T(8,128)(2,1)S(1)}, bf16[2,64,1024]{2,1,0:T(8,128)(2,1)S(1)}, u32[]{:S(2)}, u32[]{:S(2)}) collective-permute-start(bf16[2,64,1024]{2,1,0:T(8,128)(2,1)S(1)} %get-tuple-element.34), channel_id=1, source_target_pairs={{0,8},{4,20},{8,0},{12,28},{16,24},{20,4},{24,16},{28,12},{1,9},{5... | collective-permute-start | bytes 786440 | tf_op jit(solution)/shard_map/ppermute | solution.py:333
  15.4 10.7 %collective-permute-start.5 = (bf16[2,64,1024]{2,1,0:T(8,128)(2,1)S(1)}, bf16[2,64,1024]{2,1,0:T(8,128)(2,1)S(1)}, u32[]{:S(2)}, u32[]{:S(2)}) collective-permute-start(bf16[2,64,1024]{2,1,0:T(8,128)(2,1)S(1)} %collective-permute-done.2.refs_3_), channel_id=1, source_target_pairs={{0,8},{4,20},{8,0},{12,28},{16,24},{20,4},{24,16},{28,12},{1,9},{5... | collective-permute-start | bytes 786440 | tf_op jit(solution)/shard_map/ppermute | solution.py:333
  17.7 11.5 %collective-permute-start.13 = (bf16[2,64,1024]{2,1,0:T(8,128)(2,1)S(1)}, bf16[2,64,1024]{2,1,0:T(8,128)(2,1)S(1)}, u32[]{:S(2)}, u32[]{:S(2)}) collective-permute-start(bf16[2,64,1024]{2,1,0:T(8,128)(2,1)S(1)} %collective-permute-done.12.refs_4_), channel_id=1, source_target_pairs={{0,4},{4,0},{8,12},{12,8},{16,20},{20,16},{24,28},{28,24},{1,5},{5... | collective-permute-start | bytes 786440 | tf_op jit(solution)/shard_map/ppermute | solution.py:333
  20.5 9.5 %collective-permute-start.15 = (bf16[2,64,1024]{2,1,0:T(8,128)(2,1)S(1)}, bf16[2,64,1024]{2,1,0:T(8,128)(2,1)S(1)}, u32[]{:S(2)}, u32[]{:S(2)}) collective-permute-start(bf16[2,64,1024]{2,1,0:T(8,128)(2,1)S(1)} %collective-permute-done.14.refs_0_), channel_id=1, source_target_pairs={{0,4},{4,0},{8,12},{12,8},{16,20},{20,16},{24,28},{28,24},{1,5},{5... | collective-permute-start | bytes 786440 | tf_op jit(solution)/shard_map/ppermute | solution.py:333
  23.4 12.5 %collective-permute-start.4 = (bf16[2,64,1024]{2,1,0:T(8,128)(2,1)S(1)}, bf16[2,64,1024]{2,1,0:T(8,128)(2,1)S(1)}, u32[]{:S(2)}, u32[]{:S(2)}) collective-permute-start(bf16[2,64,1024]{2,1,0:T(8,128)(2,1)S(1)} %collective-permute-done.3.refs_4_), channel_id=1, source_target_pairs={{0,4},{4,0},{8,12},{12,8},{16,20},{20,16},{24,28},{28,24},{1,5},{5... | collective-permute-start | bytes 786440 | tf_op jit(solution)/shard_map/ppermute | solution.py:333
  26.2 15.8 %collective-permute-start.6 = (bf16[2,64,1024]{2,1,0:T(8,128)(2,1)S(1)}, bf16[2,64,1024]{2,1,0:T(8,128)(2,1)S(1)}, u32[]{:S(2)}, u32[]{:S(2)}) collective-permute-start(bf16[2,64,1024]{2,1,0:T(8,128)(2,1)S(1)} %collective-permute-done.5.refs_0_), channel_id=1, source_target_pairs={{0,4},{4,0},{8,12},{12,8},{16,20},{20,16},{24,28},{28,24},{1,5},{5... | collective-permute-start | bytes 786440 | tf_op jit(solution)/shard_map/ppermute | solution.py:333
  31.1 10.2 %collective-permute-start.17 = (bf16[4,64,256]{2,1,0:T(8,128)(2,1)S(1)}, bf16[4,64,256]{2,1,0:T(8,128)(2,1)S(1)}, u32[]{:S(2)}, u32[]{:S(2)}) collective-permute-start(bf16[4,64,256]{2,1,0:T(8,128)(2,1)S(1)} %get-tuple-element.31), channel_id=1, source_target_pairs={{0,2},{1,3},{2,0},{3,1},{4,6},{5,7},{6,4},{7,5},{8,10},{9,11},{10,... | collective-permute-start | bytes 393224 | tf_op jit(solution)/shard_map/ppermute | solution.py:365
  34.3 13.6 %collective-permute-start.16 = (bf16[2,64,256]{2,1,0:T(8,128)(2,1)S(1)}, bf16[2,64,256]{2,1,0:T(8,128)(2,1)S(1)}, u32[]{:S(2)}, u32[]{:S(2)}) collective-permute-start(bf16[2,64,256]{2,1,0:T(8,128)(2,1)S(1)} %get-tuple-element.30), channel_id=1, source_target_pairs={{0,1},{1,0},{2,3},{3,2},{4,5},{5,4},{6,7},{7,6},{8,9},{9,8},{10,11... | collective-permute-start | bytes 196616 | tf_op jit(solution)/shard_map/ppermute | solution.py:365
  41.2 6.6 %collective-permute-start.18 = (bf16[2,64,256]{2,1,0:T(8,128)(2,1)S(1)}, bf16[2,64,256]{2,1,0:T(8,128)(2,1)S(1)}, u32[]{:S(2)}, u32[]{:S(2)}) collective-permute-start(bf16[2,64,256]{2,1,0:T(8,128)(2,1)S(1)} %shard_map.41), channel_id=1, source_target_pairs={{0,1},{1,0},{2,3},{3,2},{4,5},{5,4},{6,7},{7,6},{8,9},{9,8},{10,11... | collective-permute-start | bytes 196616 | tf_op jit(solution)/shard_map/ppermute | solution.py:375
  43.0 5.3 %collective-permute-start.7 = (bf16[2,64,256]{2,1,0:T(8,128)(2,1)S(1)}, bf16[2,64,256]{2,1,0:T(8,128)(2,1)S(1)}, u32[]{:S(2)}, u32[]{:S(2)}) collective-permute-start(bf16[2,64,256]{2,1,0:T(8,128)(2,1)S(1)} %get-tuple-element.24), channel_id=1, source_target_pairs={{0,1},{1,0},{2,3},{3,2},{4,5},{5,4},{6,7},{7,6},{8,9},{9,8},{10,11... | collective-permute-start | bytes 196616 | tf_op jit(solution)/shard_map/ppermute | solution.py:365
  44.3 8.4 %collective-permute-start.8 = (bf16[2,64,256]{2,1,0:T(8,128)(2,1)S(1)}, bf16[2,64,256]{2,1,0:T(8,128)(2,1)S(1)}, u32[]{:S(2)}, u32[]{:S(2)}) collective-permute-start(bf16[2,64,256]{2,1,0:T(8,128)(2,1)S(1)} %get-tuple-element.25), channel_id=1, source_target_pairs={{0,2},{1,3},{2,0},{3,1},{4,6},{5,7},{6,4},{7,5},{8,10},{9,11},{10,... | collective-permute-start | bytes 196616 | tf_op jit(solution)/shard_map/ppermute | solution.py:365
  46.5 6.2 %collective-permute-start.9 = (bf16[2,64,256]{2,1,0:T(8,128)(2,1)S(1)}, bf16[2,64,256]{2,1,0:T(8,128)(2,1)S(1)}, u32[]{:S(2)}, u32[]{:S(2)}) collective-permute-start(bf16[2,64,256]{2,1,0:T(8,128)(2,1)S(1)} %get-tuple-element.26), channel_id=1, source_target_pairs={{0,3},{1,2},{2,1},{3,0},{4,7},{5,6},{6,5},{7,4},{8,11},{9,10},{10,... | collective-permute-start | bytes 196616 | tf_op jit(solution)/shard_map/ppermute | solution.py:365
where the time goes:
time: 54 us; the launch traced here: 53.8 us
  waiting for transfers between devices  26.7 us (49%)
  starting transfers between devices  17.7 us (33%)
  Pallas kernels  9.31 us (17%)
    ppermute x13, waiting for transfers between devices, send(): return lax.ppermute(v, 'depth', route)  17.7 us
    ppermute x5, starting transfers between devices, hop(): return lax.ppermute(v, 'kslab', [(k, k ^ m) for k in range(slabs)])  9.65 us
    ppermute x5, waiting for transfers between devices, hop(): return lax.ppermute(v, 'kslab', [(k, k ^ m) for k in range(slabs)])  8.92 us
    ppermute x13, starting transfers between devices, send(): return lax.ppermute(v, 'depth', route)  7.33 us
    pallas_call x6, Pallas kernels, call(): pl.pallas_call(body, out_shape=[pltpu.VMEM(o.shape, o.dtype) for o in out...  4.1 us
    pallas_call x1, Pallas kernels, prepare(): pl.pallas_call(body, out_shape=[pltpu.VMEM(o.shape, o.dtype) for o in out...  3.03 us
    pallas_call x1, Pallas kernels, transform_x(): pl.pallas_call(last_body, out_shape=struct((2, nx, wide), BF16), in_specs...  1.14 us
  transfers between devices with their start and end apart: 19, of which 8 were waited for; matrix products, arithmetic and copies ran while one was open for 0% of the time, Pallas kernels for 15%

commit v1 on v0

--- a/solution.py
+++ b/solution.py
@@ -78,21 +78,22 @@
 
 def fill_table(length, columns, coarse_ref, put):
     width = columns.shape[1]
-    step = 2.0 * math.pi / length
+    unit = 2.0 * math.pi / length
     factor = 1.0 / math.sqrt(length)
     rows = lax.broadcasted_iota(jnp.int32, (length // FINE, width), 0) * FINE
-    angle = modulo(rows * columns, length).astype(F32) * step
+    angle = modulo(rows * columns, length).astype(F32) * unit
     coarse_ref[0, pl.ds(0, length // FINE)] = jnp.cos(angle) * factor
     coarse_ref[1, pl.ds(0, length // FINE)] = jnp.sin(angle) * factor
     rows = lax.broadcasted_iota(jnp.int32, (FINE, width), 0)
-    angle = modulo(rows * columns, length).astype(F32) * step
+    angle = modulo(rows * columns, length).astype(F32) * unit
     coarse_ref[2, pl.ds(0, FINE)] = jnp.cos(angle)
     coarse_ref[3, pl.ds(0, FINE)] = jnp.sin(angle)
 
     @pl.loop(0, length // FINE)
     def _(block):
-        for left in range(0, width, 256):
-            cols = pl.ds(left, min(256, width - left))
+        step = 256 if width % 256 == 0 else width
+        for left in range(0, width, step):
+            cols = pl.ds(left, step)
             cos_c, sin_c = coarse_ref[0, pl.ds(block, 1), cols], coarse_ref[1, pl.ds(block, 1), cols]
             cos_f, sin_f = coarse_ref[2, pl.ds(0, FINE), cols], coarse_ref[3, pl.ds(0, FINE), cols]
             row = pl.ds(pl.multiple_of(block * FINE, FINE), FINE)
@@ -125,42 +126,47 @@
     )(pltpu.with_memory_space_constraint(own, pltpu.HBM))
 
 
-def prepare(green, contrast, kx_dev, parts, slabs):
+def prepare(green, contrast, kx_dev, columns_of, slabs):
     ny, nx = green.shape[3], contrast.shape[0]
     args = [green, contrast]
 
     def body(*refs):
-        given, (ty_ref, *tx_refs) = refs[:2], refs[2 : 3 + len(parts)]
-        kept, (coarse_y, coarse_x, sems) = refs[3 + len(parts) : -3], refs[-3:]
+        given, (ty_ref, *tx_refs) = refs[:2], refs[2 : 3 + len(columns_of)]
+        count = len(columns_of)
+        kept, (coarse_y, *coarse_x, sems) = refs[3 + count : -2 - count], refs[-2 - count :]
         copies = [pltpu.make_async_copy(a, b, sems.at[i]) for i, (a, b) in enumerate(zip(given, kept))]
         for copy in copies:
             copy.start()
         z = lax.axis_index("kslab")
         wide = ny // slabs
         lane = lax.broadcasted_iota(jnp.int32, (1, ny), 1)
-        columns = jnp.bitwise_xor(lane // wide, z) * wide + lane % wide
+        columns = lax.rem(lane // wide + z, slabs) * wide + lane % wide
 
         def put_y(row, left, cols, cos, sin):
             ty_ref[0, row, cols] = cos.astype(BF16)
             ty_ref[1, row, cols] = sin.astype(BF16)
 
         fill_table(ny, columns, coarse_y, put_y)
-        for (start, size), tx_ref in zip(parts, tx_refs):
-            lane = lax.broadcasted_iota(jnp.int32, (1, slabs * size), 1)
-            columns = jnp.bitwise_xor(lane // size, z) * kx_dev + start + lane % size
+        for blocks, tx_ref, coarse_ref in zip(columns_of, tx_refs, coarse_x):
+            total = tx_ref.shape[2]
+            lane = lax.broadcasted_iota(jnp.int32, (1, total), 1)
+            columns, at = lane, 0
+            for m, start, size in blocks:
+                here = lax.rem(z + slabs - m, slabs) * kx_dev + start - at + lane
+                columns, at = jnp.where(lane >= at, here, columns), at + size
 
             def put_x(row, left, cols, cos, sin):
                 tx_ref[0, row, cols] = cos.astype(BF16)
                 tx_ref[1, row, cols] = sin.astype(BF16)
 
-            fill_table(nx, columns, coarse_x.at[:, :, pl.ds(0, slabs * size)], put_x)
+            fill_table(nx, columns, coarse_ref, put_x)
         for copy in copies:
             copy.wait()
 
     outs = [struct((2, ny, ny), BF16)]
-    outs += [struct((2, nx, slabs * size), BF16) for _, size in parts]
+    widths = [-(-sum(size for _, _, size in blocks) // 128) * 128 for blocks in columns_of]
+    outs += [struct((2, nx, width), BF16) for width in widths]
     outs += [struct(v.shape, v.dtype) for v in args]
-    most = max(size for _, size in parts)
     anywhere, vmem = pl.BlockSpec(memory_space=pl.ANY), pl.BlockSpec(memory_space=pltpu.VMEM)
     made = pl.pallas_call(
         body,
@@ -169,23 +175,23 @@
         out_specs=[vmem] * len(outs),
         scratch_shapes=[
             pltpu.VMEM((4, max(ny // FINE, FINE), ny), F32),
-            pltpu.VMEM((4, max(nx // FINE, FINE), slabs * most), F32),
+            *[pltpu.VMEM((4, max(nx // FINE, FINE), width), F32) for width in widths],
             pltpu.SemaphoreType.DMA((2,)),
         ],
         compiler_params=pltpu.CompilerParams(vmem_limit_bytes=24 * MIB),
         cost_estimate=pl.CostEstimate(flops=8 * ny * ny, bytes_accessed=8 * MIB, transcendentals=0),
         name="prepare",
     )(*[pltpu.with_memory_space_constraint(v, pltpu.HBM) for v in args])
-    return made[0], made[1 : 1 + len(parts)], made[1 + len(parts) :]
+    return made[0], made[1 : 1 + len(widths)], made[1 + len(widths) :]
 
 
 def add_sources(total, green_ref, sources, step, start, cols):
     real, imag = total
     whole = pl.ds(pl.multiple_of(start + step * ROWS, ROWS), ROWS)
-    for ref, at, layer in sources:
+    for ref, plane, at, layer in sources:
         row = pl.ds(pl.multiple_of(at + step * ROWS, ROWS), ROWS)
         g_real, g_imag = green_ref[layer, 0, whole, cols].astype(F32), green_ref[layer, 1, whole, cols].astype(F32)
-        s_real, s_imag = ref[0, row, cols].astype(F32), ref[1, row, cols].astype(F32)
+        s_real, s_imag = ref[plane, row, cols].astype(F32), ref[plane + 1, row, cols].astype(F32)
         p_real = g_real * s_real - g_imag * s_imag
         p_imag = g_real * s_imag + g_imag * s_real
         real = p_real if real is None else real + p_real
@@ -193,12 +199,21 @@
     return real, imag
 
 
-def early_sum(green, arrays, offsets, layers, start, size):
+def unique(arrays):
+    kept = []
+    for array in arrays:
+        if not any(array is other for other in kept):
+            kept.append(array)
+    return kept, [next(i for i, other in enumerate(kept) if other is array) for array in arrays]
+
+
+def early_sum(green, sources, layers, start, size):
+    arrays, at = unique([array for array, _, _ in sources])
     ny = arrays[0].shape[2]
 
     def body(green_ref, *refs):
         total_ref = refs[-1]
-        sources = list(zip(refs[:-1], offsets, layers()))
+        given = [(refs[i], plane, row, layer) for i, (_, plane, row), layer in zip(at, sources, layers())]
 
         @pl.loop(0, size // ROWS)
         def _(step):
@@ -206,19 +221,21 @@
             for left in range(0, ny, 256):
                 cols = pl.ds(left, 256)
                 total_ref[0, row, cols], total_ref[1, row, cols] = add_sources(
-                    (None, None), green_ref, sources, step, start, cols
+                    (None, None), green_ref, given, step, start, cols
                 )
 
-    return call(body, [struct((2, size, ny), F32)], [green, *arrays], flops=8 * len(arrays) * size * ny)[0]
-
-
-def finish_rows(green, total, arrays, layers, table_y, start, slabs, groups):
-    _, size, ny = arrays[0].shape
+    flops = 8 * len(sources) * size * ny
+    return call(body, [struct((2, size, ny), F32)], [green, *arrays], flops=flops)[0]
+
+
+def finish_rows(green, total, sources, layers, table_y, start, size, slabs):
+    arrays, at = unique([array for array, _, _ in sources])
+    ny = arrays[0].shape[2]
     wide = ny // slabs
 
     def body(green_ref, total_ref, table_ref, *refs):
         ins, outs, left_ref = refs[: len(arrays)], refs[len(arrays) : -1], refs[-1]
-        sources = [(ref, 0, layer) for ref, layer in zip(ins, layers())]
+        given = [(ins[i], plane, row, layer) for i, (_, plane, row), layer in zip(at, sources, layers())]
 
         @pl.loop(0, size // ROWS)
         def _(step):
@@ -227,53 +244,43 @@
             for left in range(0, ny, 256):
                 cols = pl.ds(left, 256)
                 begun = total_ref[0, row, cols], total_ref[1, row, cols]
-                real, imag = add_sources(begun, green_ref, sources, step, start, cols)
+                real, imag = add_sources(begun, green_ref, given, step, start, cols)
                 left_ref[row, pl.ds(left, 256)] = real.astype(BF16)
                 left_ref[row, pl.ds(ny + left, 256)] = (-imag).astype(BF16)
                 left_ref[low, pl.ds(left, 256)] = imag.astype(BF16)
                 left_ref[low, pl.ds(ny + left, 256)] = real.astype(BF16)
 
-        for group, out_ref in zip(groups, outs):
-            for i, m in enumerate(group):
-                cols = pl.ds(m * wide, wide)
-                both = jnp.dot(left_ref[:, pl.ds(0, ny)], table_ref[0, :, cols], preferred_element_type=F32)
-                both += jnp.dot(left_ref[:, pl.ds(ny, ny)], table_ref[1, :, cols], preferred_element_type=F32)
-                out_ref[2 * i] = both[:size].astype(BF16)
-                out_ref[2 * i + 1] = both[size:].astype(BF16)
-
-    outs = [struct((2 * len(group), size, wide), BF16) for group in groups]
+        for m, out_ref in enumerate(outs):
+            cols = pl.ds(m * wide, wide)
+            both = jnp.dot(left_ref[:, pl.ds(0, ny)], table_ref[0, :, cols], preferred_element_type=F32)
+            both += jnp.dot(left_ref[:, pl.ds(ny, ny)], table_ref[1, :, cols], preferred_element_type=F32)
+            out_ref[0] = both[:size].astype(BF16)
+            out_ref[1] = both[size:].astype(BF16)
+
+    outs = [struct((2, size, wide), BF16)] * slabs
     flops = 8 * size * ny * ny
     return call(body, outs, [green, total, table_y, *arrays], [pltpu.VMEM((2 * size, 2 * ny), BF16)], flops)
 
 
-def second_half(pair):
-    count = pair.shape[0] // 2
-
-    def body(pair_ref, out_ref):
-        out_ref[...] = pair_ref[count:]
-
-    return call(body, [struct((count, *pair.shape[1:]), pair.dtype)], [pair])[0]
-
-
-def transform_x(table_x, blocks, size, total=None, contrast=None):
-    arrays = []
-    for array, _ in blocks:
-        if not any(array is other for other in arrays):
-            arrays.append(array)
-    at = [next(i for i, other in enumerate(arrays) if other is array) for array, _ in blocks]
-    wide = arrays[0].shape[2]
-    nx = table_x.shape[1]
-    half = len(blocks) * size
+def transform_x(table_x, blocks, total=None, contrast=None):
+    wide = blocks[0].shape[2]
+    _, nx, half = table_x.shape
     tall = min(nx, 128)
 
     def fill(ins, right_ref):
-        for m, (_, place) in enumerate(blocks):
-            real, imag = ins[at[m]][place], ins[at[m]][place + 1]
-            top, low = pl.ds(m * size, size), pl.ds(half + m * size, size)
+        start = 0
+        for ref in ins[: len(blocks)]:
+            real, imag, size = ref[0], ref[1], ref.shape[1]
+            top, low = pl.ds(start, size), pl.ds(half + start, size)
             right_ref[top, pl.ds(0, wide)] = real
             right_ref[top, pl.ds(wide, wide)] = imag
             right_ref[low, pl.ds(0, wide)] = -imag
             right_ref[low, pl.ds(wide, wide)] = real
+            start += size
+        if start < half:
+            none = jnp.zeros((half - start, 2 * wide), BF16)
+            right_ref[pl.ds(start, half - start), :] = none
+            right_ref[pl.ds(half + start, half - start), :] = none
 
     def product(table_ref, right_ref, row):
         part = jnp.dot(table_ref[0, row, :], right_ref[pl.ds(0, half), :], preferred_element_type=F32)
@@ -306,9 +313,9 @@
     scratch = [pltpu.VMEM((2 * half, 2 * wide), BF16)]
     flops = 8 * nx * half * wide
     if contrast is None:
-        ins = [table_x, *arrays] + ([] if total is None else [total])
+        ins = [table_x, *blocks] + ([] if total is None else [total])
         return call(body, [struct((nx, 2 * wide), F32)], ins, scratch, flops)[0]
-    ins = [table_x, *arrays, total, contrast]
+    ins = [table_x, *blocks, total, contrast]
     return pl.pallas_call(
         last_body,
         out_shape=struct((2, nx, wide), BF16),
@@ -343,38 +350,26 @@
     owns = split_rows(own, parts)
     near = [send(v, out) for v in owns]
     own_swap = send(own, swap)
-    table_y, table_x, (green, contrast) = prepare(green, contrast, kx_dev, parts, slabs)
+    columns_of = [[(m, start, size) for m in range(slabs)] for start, size in parts]
+    table_y, table_x, (green, contrast) = prepare(green, contrast, kx_dev, columns_of, slabs)
     near_swap = [send(v, swap) for v in near]
     far = [send(own_swap[:, s : s + n], out) for s, n in parts]
     across = [send(v, out) for v in near_swap]
-    field = None
-    results = []
+
+    def hop(m, v):
+        return lax.ppermute(v, "kslab", [(k, (k + m) % slabs) for k in range(slabs)])
+
+    halves = []
     for i, (start, size) in enumerate(parts):
         far_swap, across_swap = send(far[i], swap), send(across[i], swap)
-        total = early_sum(
-            green, [owns[i], own_swap, near[i], near_swap[i], far[i], far_swap], [0, start, 0, 0, 0, 0],
-            layers([(0, 0), (1, 1), (2, 4), (5, 3), (3, 5), (4, 2)]), start, size,
-        )
-        relay = slabs == 4 and i < len(parts) - 1
-        groups = [[0], [1], [2, 3]] if relay else [[m] for m in range(slabs)]
-        halves = finish_rows(
-            green, total, [across[i], across_swap], layers([(7, 7), (6, 6)]), table_y, start, slabs, groups
-        )
-
-        def hop(m, v):
-            return lax.ppermute(v, "kslab", [(k, k ^ m) for k in range(slabs)])
-
-        if relay:
-            two, one = hop(2, halves[2]), hop(1, halves[1])
-            results.append([(halves[0], 0), (one, 0), (two, 0), (two, 2)])
-        else:
-            results.append([(halves[0], 0)] + [(hop(m, halves[m]), 0) for m in range(1, slabs)])
-    for result in results[:-1]:
-        if slabs == 4:
-            passed = second_half(result[3][0])
-            result[3] = (lax.ppermute(passed, "kslab", [(k, k ^ 1) for k in range(slabs)]), 0)
-    for i, (start, size) in enumerate(parts):
-        field = transform_x(table_x[i], results[i], size, field, contrast if i == len(parts) - 1 else None)
+        sources = [(owns[i], 0, 0), (own_swap, 0, start), (near[i], 0, 0), (near_swap[i], 0, 0), (far[i], 0, 0)]
+        total = early_sum(green, sources, layers([(0, 0), (1, 1), (2, 4), (5, 3), (3, 5)]), start, size)
+        sources = [(far_swap, 0, 0), (across[i], 0, 0), (across_swap, 0, 0)]
+        halves.append(finish_rows(green, total, sources, layers([(4, 2), (7, 7), (6, 6)]), table_y, start, size, slabs))
+    field = None
+    for i, slab in enumerate(halves):
+        blocks = [slab[0]] + [hop(m, slab[m]) for m in range(1, slabs)]
+        field = transform_x(table_x[i], blocks, field, contrast if i == len(parts) - 1 else None)
     return field[None]
 
 
@@ -388,8 +383,8 @@
     depth, slabs = mesh.shape["depth"], mesh.shape["kslab"]
 
     def on_device(spectra, green, contrast):
-        cube = depth == 8 and spectra.shape[0] == 1 and slabs & (slabs - 1) == 0
-        if cube and spectra.shape[2] % 64 == 0 and (spectra.shape[3] // slabs) % 128 == 0:
+        cube = depth == 8 and spectra.shape[0] == 1 and slabs == 4
+        if cube and spectra.shape[2] % 128 == 0 and (spectra.shape[3] // slabs) % 128 == 0:
             return on_cube_device(slabs, spectra, green, contrast)
         return on_any_device(spectra, green, contrast)
 

time: 54 us -> 48.8 us (0.904)
  waiting for transfers between devices: 26.7 us -> 21.8 us
    ppermute x6, waiting for transfers between devices: 8.93 us -> 4.09 us  [hop(): lax.ppermute(v, 'kslab', [(k, (k + m) % slabs) for k in range(slabs)])]
    pallas_call x6 -> x5, Pallas kernels: 4.1 us -> 4.1 us  [call(): pl.pallas_call(body, out_shape=[pltpu.VMEM(o.shape, o.dtype) for o in out...]
  transfers between devices with their start and end apart: 19 -> 19, of which waited for: 8 -> 8; matrix products, arithmetic and copies ran while one was open for 0% -> 0% of each run, Pallas kernels for 15% -> 17%
where the time goes in v1:
time: 48.8 us; the launch traced here: 48.6 us
  waiting for transfers between devices  21.8 us (45%)
  starting transfers between devices  17.4 us (36%)
  Pallas kernels  9.31 us (19%)
    ppermute x13, waiting for transfers between devices, send(): return lax.ppermute(v, 'depth', route)  17.7 us
    ppermute x6, starting transfers between devices, hop(): lax.ppermute(v, 'kslab', [(k, (k + m) % slabs) for k in range(slabs)])  10 us
    ppermute x13, starting transfers between devices, send(): return lax.ppermute(v, 'depth', route)  7.33 us
    pallas_call x5, Pallas kernels, call(): pl.pallas_call(body, out_shape=[pltpu.VMEM(o.shape, o.dtype) for o in out...  4.1 us
    ppermute x6, waiting for transfers between devices, hop(): lax.ppermute(v, 'kslab', [(k, (k + m) % slabs) for k in range(slabs)])  4.09 us
    pallas_call x1, Pallas kernels, prepare(): pl.pallas_call(body, out_shape=[pltpu.VMEM(o.shape, o.dtype) for o in out...  3.03 us
    pallas_call x1, Pallas kernels, transform_x(): pl.pallas_call(last_body, out_shape=struct((2, nx, wide), BF16), in_specs...  1.14 us
    pallas_call x1, Pallas kernels, split_rows(): pl.pallas_call(body, out_shape=[pltpu.VMEM((planes, size, ny), own.dtype)...  1.04 us
  transfers between devices with their start and end apart: 19, of which 8 were waited for; matrix products, arithmetic and copies ran while one was open for 0% of the time, Pallas kernels for 17%

profile of v1, /device:TPU:0, one launch (start us, length us, event | category | flops | bytes accessed | tf_op | source)
XLA Modules:
  0.0 48.6 jit_solution(12080918915950510197)
XLA Ops:
  0.0 0.5 %collective-permute-start = (bf16[2,128,1024]{2,1,0:T(8,128)(2,1)}, bf16[2,128,1024]{2,1,0:T(8,128)(2,1)S(1)}, u32[]{:S(2)}, u32[]{:S(2)}) collective-permute-start(bf16[2,128,1024]{2,1,0:T(8,128)(2,1)} %bitcast.6), channel_id=1, source_target_pairs={{0,4},{4,0},{8,12},{12,8},{16,20},{20,16},{24,28},{28,24},{1,5},{5... | collective-permute-start | bytes 1572872 | tf_op jit(solution)/shard_map/ppermute | solution.py:340
  0.5 1.0 %split_rows.1 = (bf16[2,64,1024]{2,1,0:T(8,128)(2,1)S(1)}, bf16[2,64,1024]{2,1,0:T(8,128)(2,1)S(1)}) custom-call(bf16[2,128,1024]{2,1,0:T(8,128)(2,1)} %bitcast.7), custom_call_target="tpu_custom_call" | custom-call | bytes 1048576 | tf_op jit(solution)/shard_map/split_rows/pallas_call | solution.py:117
  1.5 2.5 %collective-permute-start.10 = (bf16[2,64,1024]{2,1,0:T(8,128)(2,1)S(1)}, bf16[2,64,1024]{2,1,0:T(8,128)(2,1)S(1)}, u32[]{:S(2)}, u32[]{:S(2)}) collective-permute-start(bf16[2,64,1024]{2,1,0:T(8,128)(2,1)S(1)} %get-tuple-element.29.refs_0_), channel_id=1, source_target_pairs={{0,8},{4,20},{8,0},{12,28},{16,24},{20,4},{24,16},{28,12},{1,9},{5... | collective-permute-start | bytes 786440 | tf_op jit(solution)/shard_map/ppermute | solution.py:340
  4.2 4.3 %collective-permute-done.10.refs_2_ = bf16[2,64,1024]{2,1,0:T(8,128)(2,1)S(1)} collective-permute-done((bf16[2,64,1024]{2,1,0:T(8,128)(2,1)S(1)}, bf16[2,64,1024]{2,1,0:T(8,128)(2,1)S(1)}, u32[]{:S(2)}, u32[]{:S(2)}) %collective-permute-start.10) | collective-permute-done | bytes 262176 | tf_op jit(solution)/shard_map/ppermute | solution.py:340
  8.4 2.8 %collective-permute-done.1.refs_2_ = bf16[2,64,1024]{2,1,0:T(8,128)(2,1)S(1)} collective-permute-done((bf16[2,64,1024]{2,1,0:T(8,128)(2,1)S(1)}, bf16[2,64,1024]{2,1,0:T(8,128)(2,1)S(1)}, u32[]{:S(2)}, u32[]{:S(2)}) %collective-permute-start.1) | collective-permute-done | bytes 262176 | tf_op jit(solution)/shard_map/ppermute | solution.py:340
  11.3 2.1 %collective-permute-start.12 = (bf16[2,64,1024]{2,1,0:T(8,128)(2,1)S(1)}, bf16[2,64,1024]{2,1,0:T(8,128)(2,1)S(1)}, u32[]{:S(2)}, u32[]{:S(2)}) collective-permute-start(bf16[2,64,1024]{2,1,0:T(8,128)(2,1)S(1)} %get-tuple-element.35), channel_id=1, source_target_pairs={{0,8},{4,20},{8,0},{12,28},{16,24},{20,4},{24,16},{28,12},{1,9},{5... | collective-permute-start | bytes 786440 | tf_op jit(solution)/shard_map/ppermute | solution.py:340
  13.5 1.9 %collective-permute-start.3 = (bf16[2,64,1024]{2,1,0:T(8,128)(2,1)S(1)}, bf16[2,64,1024]{2,1,0:T(8,128)(2,1)S(1)}, u32[]{:S(2)}, u32[]{:S(2)}) collective-permute-start(bf16[2,64,1024]{2,1,0:T(8,128)(2,1)S(1)} %get-tuple-element.36), channel_id=1, source_target_pairs={{0,8},{4,20},{8,0},{12,28},{16,24},{20,4},{24,16},{28,12},{1,9},{5... | collective-permute-start | bytes 786440 | tf_op jit(solution)/shard_map/ppermute | solution.py:340
  15.5 2.2 %collective-permute-done.12.refs_4_ = bf16[2,64,1024]{2,1,0:T(8,128)(2,1)S(1)} collective-permute-done((bf16[2,64,1024]{2,1,0:T(8,128)(2,1)S(1)}, bf16[2,64,1024]{2,1,0:T(8,128)(2,1)S(1)}, u32[]{:S(2)}, u32[]{:S(2)}) %collective-permute-start.12) | collective-permute-done | bytes 262176 | tf_op jit(solution)/shard_map/ppermute | solution.py:340
  17.7 2.8 %collective-permute-done.14.refs_1_ = bf16[2,64,1024]{2,1,0:T(8,128)(2,1)S(1)} collective-permute-done((bf16[2,64,1024]{2,1,0:T(8,128)(2,1)S(1)}, bf16[2,64,1024]{2,1,0:T(8,128)(2,1)S(1)}, u32[]{:S(2)}, u32[]{:S(2)}) %collective-permute-start.14) | collective-permute-done | bytes 262176 | tf_op jit(solution)/shard_map/ppermute | solution.py:340
  20.5 2.8 %collective-permute-done.3.refs_4_ = bf16[2,64,1024]{2,1,0:T(8,128)(2,1)S(1)} collective-permute-done((bf16[2,64,1024]{2,1,0:T(8,128)(2,1)S(1)}, bf16[2,64,1024]{2,1,0:T(8,128)(2,1)S(1)}, u32[]{:S(2)}, u32[]{:S(2)}) %collective-permute-start.3) | collective-permute-done | bytes 262176 | tf_op jit(solution)/shard_map/ppermute | solution.py:340
  23.4 2.8 %collective-permute-done.5.refs_1_ = bf16[2,64,1024]{2,1,0:T(8,128)(2,1)S(1)} collective-permute-done((bf16[2,64,1024]{2,1,0:T(8,128)(2,1)S(1)}, bf16[2,64,1024]{2,1,0:T(8,128)(2,1)S(1)}, u32[]{:S(2)}, u32[]{:S(2)}) %collective-permute-start.5) | collective-permute-done | bytes 262176 | tf_op jit(solution)/shard_map/ppermute | solution.py:340
  26.2 3.0 %prepare.1 = (bf16[2,1024,1024]{2,1,0:T(8,128)(2,1)S(1)}, bf16[2,512,256]{2,1,0:T(8,128)(2,1)S(1)}, bf16[2,512,256]{2,1,0:T(8,128)(2,1)S(1)}, bf16[8,2,128,1024]{3,2,1,0:T(8,128)(2,1)S(1)}, f32[512,256]{1,0:T(8,128)S(1)}) custom-call(bf16[8,2,128,1024]{3,2,1,0:T(8,128)(2,1)} %bitcast.4, f32[512,256]{1,0:T(8,128)} %bitcast.5), custom_call_target="tpu_custom_call" | custom-call | flops 8388608 | bytes 8388608 | tf_op jit(solution)/shard_map/prepare/pallas_call | solution.py:171
  29.2 0.7 %shard_map.39.total_ref = f32[2,64,1024]{2,1,0:T(8,128)S(1)} custom-call(bf16[8,2,128,1024]{3,2,1,0:T(8,128)(2,1)S(1)} %get-tuple-element.21.green_ref, bf16[2,64,1024]{2,1,0:T(8,128)(2,1)S(1)} %get-tuple-element.29.refs_0_, bf16[2,128,1024]{2,1,0:T(8,128)(2,1)S(1)} %collective-permute-done.refs_1_, ...), custom_call_target="tpu_custom_call" | custom-call | flops 2621440 | bytes 6291456 | tf_op jit(solution)/shard_map/pallas_call | solution.py:60
  30.0 1.1 %shard_map.40 = (bf16[2,64,256]{2,1,0:T(8,128)(2,1)S(1)}, bf16[2,64,256]{2,1,0:T(8,128)(2,1)S(1)}, bf16[2,64,256]{2,1,0:T(8,128)(2,1)S(1)}, bf16[2,64,256]{2,1,0:T(8,128)(2,1)S(1)}) custom-call(bf16[8,2,128,1024]{3,2,1,0:T(8,128)(2,1)S(1)} %get-tuple-element.21.green_ref, f32[2,64,1024]{2,1,0:T(8,128)S(1)} %shard_map.39.total_ref, ...), custom_call_target="tpu_custom_call" | custom-call | flops 536870912 | bytes 9961472 | tf_op jit(solution)/shard_map/pallas_call | solution.py:60
  31.1 2.2 %collective-permute-start.16 = (bf16[2,64,256]{2,1,0:T(8,128)(2,1)S(1)}, bf16[2,64,256]{2,1,0:T(8,128)(2,1)S(1)}, u32[]{:S(2)}, u32[]{:S(2)}) collective-permute-start(bf16[2,64,256]{2,1,0:T(8,128)(2,1)S(1)} %get-tuple-element.31), channel_id=1, source_target_pairs={{0,1},{1,2},{2,3},{3,0},{4,5},{5,6},{6,7},{7,4},{8,9},{9,10},{10,1... | collective-permute-start | bytes 196616 | tf_op jit(solution)/shard_map/ppermute | solution.py:360
  33.2 0.7 %shard_map.37.total_ref = f32[2,64,1024]{2,1,0:T(8,128)S(1)} custom-call(bf16[8,2,128,1024]{3,2,1,0:T(8,128)(2,1)S(1)} %get-tuple-element.21.green_ref, bf16[2,64,1024]{2,1,0:T(8,128)(2,1)S(1)} %get-tuple-element.22.refs_0_, bf16[2,128,1024]{2,1,0:T(8,128)(2,1)S(1)} %collective-permute-done.refs_1_, bf16[2,64,1024]{2,1,0:T(8,128)(2,1)S(1)} %collective-permute-done.1.refs_2_, ...), custom_call_target="tpu_custom_call" | custom-call | flops 2621440 | bytes 6291456 | tf_op jit(solution)/shard_map/pallas_call | solution.py:60
  33.9 2.7 %collective-permute-start.17 = (bf16[2,64,256]{2,1,0:T(8,128)(2,1)S(1)}, bf16[2,64,256]{2,1,0:T(8,128)(2,1)S(1)}, u32[]{:S(2)}, u32[]{:S(2)}) collective-permute-start(bf16[2,64,256]{2,1,0:T(8,128)(2,1)S(1)} %get-tuple-element.32), channel_id=1, source_target_pairs={{0,2},{1,3},{2,0},{3,1},{4,6},{5,7},{6,4},{7,5},{8,10},{9,11},{10,... | collective-permute-start | bytes 196616 | tf_op jit(solution)/shard_map/ppermute | solution.py:360
  36.6 1.3 %collective-permute-start.18 = (bf16[2,64,256]{2,1,0:T(8,128)(2,1)S(1)}, bf16[2,64,256]{2,1,0:T(8,128)(2,1)S(1)}, u32[]{:S(2)}, u32[]{:S(2)}) collective-permute-start(bf16[2,64,256]{2,1,0:T(8,128)(2,1)S(1)} %get-tuple-element.33), channel_id=1, source_target_pairs={{0,3},{1,0},{2,1},{3,2},{4,7},{5,4},{6,5},{7,6},{8,11},{9,8},{10,9... | collective-permute-start | bytes 196616 | tf_op jit(solution)/shard_map/ppermute | solution.py:360
  38.0 1.1 %shard_map.38 = (bf16[2,64,256]{2,1,0:T(8,128)(2,1)S(1)}, bf16[2,64,256]{2,1,0:T(8,128)(2,1)S(1)}, bf16[2,64,256]{2,1,0:T(8,128)(2,1)S(1)}, bf16[2,64,256]{2,1,0:T(8,128)(2,1)S(1)}) custom-call(bf16[8,2,128,1024]{3,2,1,0:T(8,128)(2,1)S(1)} %get-tuple-element.21.green_ref, f32[2,64,1024]{2,1,0:T(8,128)S(1)} %shard_map.37.total_ref, ...), custom_call_target="tpu_custom_call" | custom-call | flops 536870912 | bytes 9961472 | tf_op jit(solution)/shard_map/pallas_call | solution.py:60
  39.1 0.7 %collective-permute-start.7 = (bf16[2,64,256]{2,1,0:T(8,128)(2,1)S(1)}, bf16[2,64,256]{2,1,0:T(8,128)(2,1)S(1)}, u32[]{:S(2)}, u32[]{:S(2)}) collective-permute-start(bf16[2,64,256]{2,1,0:T(8,128)(2,1)S(1)} %get-tuple-element.25), channel_id=1, source_target_pairs={{0,1},{1,2},{2,3},{3,0},{4,5},{5,6},{6,7},{7,4},{8,9},{9,10},{10,1... | collective-permute-start | bytes 196616 | tf_op jit(solution)/shard_map/ppermute | solution.py:360
  40.1 2.8 %collective-permute-start.9 = (bf16[2,64,256]{2,1,0:T(8,128)(2,1)S(1)}, bf16[2,64,256]{2,1,0:T(8,128)(2,1)S(1)}, u32[]{:S(2)}, u32[]{:S(2)}) collective-permute-start(bf16[2,64,256]{2,1,0:T(8,128)(2,1)S(1)} %get-tuple-element.27), channel_id=1, source_target_pairs={{0,3},{1,0},{2,1},{3,2},{4,7},{5,4},{6,5},{7,6},{8,11},{9,8},{10,9... | collective-permute-start | bytes 196616 | tf_op jit(solution)/shard_map/ppermute | solution.py:360
  43.4 2.5 %collective-permute-done.7.refs_1_ = bf16[2,64,256]{2,1,0:T(8,128)(2,1)S(1)} collective-permute-done((bf16[2,64,256]{2,1,0:T(8,128)(2,1)S(1)}, bf16[2,64,256]{2,1,0:T(8,128)(2,1)S(1)}, u32[]{:S(2)}, u32[]{:S(2)}) %collective-permute-start.7) | collective-permute-done | bytes 65568 | tf_op jit(solution)/shard_map/ppermute | solution.py:360
  45.9 1.6 %collective-permute-done.8.refs_2_ = bf16[2,64,256]{2,1,0:T(8,128)(2,1)S(1)} collective-permute-done((bf16[2,64,256]{2,1,0:T(8,128)(2,1)S(1)}, bf16[2,64,256]{2,1,0:T(8,128)(2,1)S(1)}, u32[]{:S(2)}, u32[]{:S(2)}) %collective-permute-start.8) | collective-permute-done | bytes 65568 | tf_op jit(solution)/shard_map/ppermute | solution.py:360
  47.5 1.1 %transform_x_last.1 = bf16[2,512,256]{2,1,0:T(8,128)(2,1)} custom-call(bf16[2,512,256]{2,1,0:T(8,128)(2,1)S(1)} %get-tuple-element.20.table_ref, bf16[2,64,256]{2,1,0:T(8,128)(2,1)S(1)} %get-tuple-element.24.refs_0_, bf16[2,64,256]{2,1,0:T(8,128)(2,1)S(1)} %collective-permute-done.7.refs_1_, bf16[2,64,256]{2,1,0:T(8,128)(2,1)S(1)} %collective-permute-done.8.refs_2_, ...), custom_call_target="tpu_custom_call" | custom-call | flops 268435456 | bytes 4194304 | tf_op jit(solution)/shard_map/transform_x_last/pallas_call | solution.py:319
  (23 shorter events, 1.1 us)
Async XLA Ops:
  0.0 11.3 %collective-permute-start = (bf16[2,128,1024]{2,1,0:T(8,128)(2,1)}, bf16[2,128,1024]{2,1,0:T(8,128)(2,1)S(1)}, u32[]{:S(2)}, u32[]{:S(2)}) collective-permute-start(bf16[2,128,1024]{2,1,0:T(8,128)(2,1)} %bitcast.6), channel_id=1, source_target_pairs={{0,4},{4,0},{8,12},{12,8},{16,20},{20,16},{24,28},{28,24},{1,5},{5... | collective-permute-start | bytes 1572872 | tf_op jit(solution)/shard_map/ppermute | solution.py:340
  1.5 6.9 %collective-permute-start.10 = (bf16[2,64,1024]{2,1,0:T(8,128)(2,1)S(1)}, bf16[2,64,1024]{2,1,0:T(8,128)(2,1)S(1)}, u32[]{:S(2)}, u32[]{:S(2)}) collective-permute-start(bf16[2,64,1024]{2,1,0:T(8,128)(2,1)S(1)} %get-tuple-element.29.refs_0_), channel_id=1, source_target_pairs={{0,8},{4,20},{8,0},{12,28},{16,24},{20,4},{24,16},{28,12},{1,9},{5... | collective-permute-start | bytes 786440 | tf_op jit(solution)/shard_map/ppermute | solution.py:340
  4.1 7.2 %collective-permute-start.1 = (bf16[2,64,1024]{2,1,0:T(8,128)(2,1)S(1)}, bf16[2,64,1024]{2,1,0:T(8,128)(2,1)S(1)}, u32[]{:S(2)}, u32[]{:S(2)}) collective-permute-start(bf16[2,64,1024]{2,1,0:T(8,128)(2,1)S(1)} %get-tuple-element.22.refs_0_), channel_id=1, source_target_pairs={{0,8},{4,20},{8,0},{12,28},{16,24},{20,4},{24,16},{28,12},{1,9},{5... | collective-permute-start | bytes 786440 | tf_op jit(solution)/shard_map/ppermute | solution.py:340
  8.4 4.9 %collective-permute-start.11 = (bf16[2,64,1024]{2,1,0:T(8,128)(2,1)S(1)}, bf16[2,64,1024]{2,1,0:T(8,128)(2,1)S(1)}, u32[]{:S(2)}, u32[]{:S(2)}) collective-permute-start(bf16[2,64,1024]{2,1,0:T(8,128)(2,1)S(1)} %collective-permute-done.10.refs_2_), channel_id=1, source_target_pairs={{0,4},{4,0},{8,12},{12,8},{16,20},{20,16},{24,28},{28,24},{1,5},{5... | collective-permute-start | bytes 786440 | tf_op jit(solution)/shard_map/ppermute | solution.py:340
  11.3 4.2 %collective-permute-start.2 = (bf16[2,64,1024]{2,1,0:T(8,128)(2,1)S(1)}, bf16[2,64,1024]{2,1,0:T(8,128)(2,1)S(1)}, u32[]{:S(2)}, u32[]{:S(2)}) collective-permute-start(bf16[2,64,1024]{2,1,0:T(8,128)(2,1)S(1)} %collective-permute-done.1.refs_2_), channel_id=1, source_target_pairs={{0,4},{4,0},{8,12},{12,8},{16,20},{20,16},{24,28},{28,24},{1,5},{5... | collective-permute-start | bytes 786440 | tf_op jit(solution)/shard_map/ppermute | solution.py:340
  11.3 6.4 %collective-permute-start.12 = (bf16[2,64,1024]{2,1,0:T(8,128)(2,1)S(1)}, bf16[2,64,1024]{2,1,0:T(8,128)(2,1)S(1)}, u32[]{:S(2)}, u32[]{:S(2)}) collective-permute-start(bf16[2,64,1024]{2,1,0:T(8,128)(2,1)S(1)} %get-tuple-element.35), channel_id=1, source_target_pairs={{0,8},{4,20},{8,0},{12,28},{16,24},{20,4},{24,16},{28,12},{1,9},{5... | collective-permute-start | bytes 786440 | tf_op jit(solution)/shard_map/ppermute | solution.py:340
  13.4 7.2 %collective-permute-start.14 = (bf16[2,64,1024]{2,1,0:T(8,128)(2,1)S(1)}, bf16[2,64,1024]{2,1,0:T(8,128)(2,1)S(1)}, u32[]{:S(2)}, u32[]{:S(2)}) collective-permute-start(bf16[2,64,1024]{2,1,0:T(8,128)(2,1)S(1)} %collective-permute-done.11.refs_3_), channel_id=1, source_target_pairs={{0,8},{4,20},{8,0},{12,28},{16,24},{20,4},{24,16},{28,12},{1,9},{5... | collective-permute-start | bytes 786440 | tf_op jit(solution)/shard_map/ppermute | solution.py:340
  13.5 9.9 %collective-permute-start.3 = (bf16[2,64,1024]{2,1,0:T(8,128)(2,1)S(1)}, bf16[2,64,1024]{2,1,0:T(8,128)(2,1)S(1)}, u32[]{:S(2)}, u32[]{:S(2)}) collective-permute-start(bf16[2,64,1024]{2,1,0:T(8,128)(2,1)S(1)} %get-tuple-element.36), channel_id=1, source_target_pairs={{0,8},{4,20},{8,0},{12,28},{16,24},{20,4},{24,16},{28,12},{1,9},{5... | collective-permute-start | bytes 786440 | tf_op jit(solution)/shard_map/ppermute | solution.py:340
  15.4 10.7 %collective-permute-start.5 = (bf16[2,64,1024]{2,1,0:T(8,128)(2,1)S(1)}, bf16[2,64,1024]{2,1,0:T(8,128)(2,1)S(1)}, u32[]{:S(2)}, u32[]{:S(2)}) collective-permute-start(bf16[2,64,1024]{2,1,0:T(8,128)(2,1)S(1)} %collective-permute-done.2.refs_3_), channel_id=1, source_target_pairs={{0,8},{4,20},{8,0},{12,28},{16,24},{20,4},{24,16},{28,12},{1,9},{5... | collective-permute-start | bytes 786440 | tf_op jit(solution)/shard_map/ppermute | solution.py:340
  17.7 12.2 %collective-permute-start.13 = (bf16[2,64,1024]{2,1,0:T(8,128)(2,1)S(1)}, bf16[2,64,1024]{2,1,0:T(8,128)(2,1)S(1)}, u32[]{:S(2)}, u32[]{:S(2)}) collective-permute-start(bf16[2,64,1024]{2,1,0:T(8,128)(2,1)S(1)} %collective-permute-done.12.refs_4_), channel_id=1, source_target_pairs={{0,4},{4,0},{8,12},{12,8},{16,20},{20,16},{24,28},{28,24},{1,5},{5... | collective-permute-start | bytes 786440 | tf_op jit(solution)/shard_map/ppermute | solution.py:340
  20.5 9.4 %collective-permute-start.15 = (bf16[2,64,1024]{2,1,0:T(8,128)(2,1)S(1)}, bf16[2,64,1024]{2,1,0:T(8,128)(2,1)S(1)}, u32[]{:S(2)}, u32[]{:S(2)}) collective-permute-start(bf16[2,64,1024]{2,1,0:T(8,128)(2,1)S(1)} %collective-permute-done.14.refs_1_), channel_id=1, source_target_pairs={{0,4},{4,0},{8,12},{12,8},{16,20},{20,16},{24,28},{28,24},{1,5},{5... | collective-permute-start | bytes 786440 | tf_op jit(solution)/shard_map/ppermute | solution.py:340
  23.4 14.6 %collective-permute-start.4 = (bf16[2,64,1024]{2,1,0:T(8,128)(2,1)S(1)}, bf16[2,64,1024]{2,1,0:T(8,128)(2,1)S(1)}, u32[]{:S(2)}, u32[]{:S(2)}) collective-permute-start(bf16[2,64,1024]{2,1,0:T(8,128)(2,1)S(1)} %collective-permute-done.3.refs_4_), channel_id=1, source_target_pairs={{0,4},{4,0},{8,12},{12,8},{16,20},{20,16},{24,28},{28,24},{1,5},{5... | collective-permute-start | bytes 786440 | tf_op jit(solution)/shard_map/ppermute | solution.py:340
  26.2 11.8 %collective-permute-start.6 = (bf16[2,64,1024]{2,1,0:T(8,128)(2,1)S(1)}, bf16[2,64,1024]{2,1,0:T(8,128)(2,1)S(1)}, u32[]{:S(2)}, u32[]{:S(2)}) collective-permute-start(bf16[2,64,1024]{2,1,0:T(8,128)(2,1)S(1)} %collective-permute-done.5.refs_1_), channel_id=1, source_target_pairs={{0,4},{4,0},{8,12},{12,8},{16,20},{20,16},{24,28},{28,24},{1,5},{5... | collective-permute-start | bytes 786440 | tf_op jit(solution)/shard_map/ppermute | solution.py:340
  31.1 9.1 %collective-permute-start.16 = (bf16[2,64,256]{2,1,0:T(8,128)(2,1)S(1)}, bf16[2,64,256]{2,1,0:T(8,128)(2,1)S(1)}, u32[]{:S(2)}, u32[]{:S(2)}) collective-permute-start(bf16[2,64,256]{2,1,0:T(8,128)(2,1)S(1)} %get-tuple-element.31), channel_id=1, source_target_pairs={{0,1},{1,2},{2,3},{3,0},{4,5},{5,6},{6,7},{7,4},{8,9},{9,10},{10,1... | collective-permute-start | bytes 196616 | tf_op jit(solution)/shard_map/ppermute | solution.py:360
  33.9 9.0 %collective-permute-start.17 = (bf16[2,64,256]{2,1,0:T(8,128)(2,1)S(1)}, bf16[2,64,256]{2,1,0:T(8,128)(2,1)S(1)}, u32[]{:S(2)}, u32[]{:S(2)}) collective-permute-start(bf16[2,64,256]{2,1,0:T(8,128)(2,1)S(1)} %get-tuple-element.32), channel_id=1, source_target_pairs={{0,2},{1,3},{2,0},{3,1},{4,6},{5,7},{6,4},{7,5},{8,10},{9,11},{10,... | collective-permute-start | bytes 196616 | tf_op jit(solution)/shard_map/ppermute | solution.py:360
  36.6 6.4 %collective-permute-start.18 = (bf16[2,64,256]{2,1,0:T(8,128)(2,1)S(1)}, bf16[2,64,256]{2,1,0:T(8,128)(2,1)S(1)}, u32[]{:S(2)}, u32[]{:S(2)}) collective-permute-start(bf16[2,64,256]{2,1,0:T(8,128)(2,1)S(1)} %get-tuple-element.33), channel_id=1, source_target_pairs={{0,3},{1,0},{2,1},{3,2},{4,7},{5,4},{6,5},{7,6},{8,11},{9,8},{10,9... | collective-permute-start | bytes 196616 | tf_op jit(solution)/shard_map/ppermute | solution.py:360
  39.1 6.8 %collective-permute-start.7 = (bf16[2,64,256]{2,1,0:T(8,128)(2,1)S(1)}, bf16[2,64,256]{2,1,0:T(8,128)(2,1)S(1)}, u32[]{:S(2)}, u32[]{:S(2)}) collective-permute-start(bf16[2,64,256]{2,1,0:T(8,128)(2,1)S(1)} %get-tuple-element.25), channel_id=1, source_target_pairs={{0,1},{1,2},{2,3},{3,0},{4,5},{5,6},{6,7},{7,4},{8,9},{9,10},{10,1... | collective-permute-start | bytes 196616 | tf_op jit(solution)/shard_map/ppermute | solution.py:360
  39.8 7.7 %collective-permute-start.8 = (bf16[2,64,256]{2,1,0:T(8,128)(2,1)S(1)}, bf16[2,64,256]{2,1,0:T(8,128)(2,1)S(1)}, u32[]{:S(2)}, u32[]{:S(2)}) collective-permute-start(bf16[2,64,256]{2,1,0:T(8,128)(2,1)S(1)} %get-tuple-element.26), channel_id=1, source_target_pairs={{0,2},{1,3},{2,0},{3,1},{4,6},{5,7},{6,4},{7,5},{8,10},{9,11},{10,... | collective-permute-start | bytes 196616 | tf_op jit(solution)/shard_map/ppermute | solution.py:360
  40.1 7.4 %collective-permute-start.9 = (bf16[2,64,256]{2,1,0:T(8,128)(2,1)S(1)}, bf16[2,64,256]{2,1,0:T(8,128)(2,1)S(1)}, u32[]{:S(2)}, u32[]{:S(2)}) collective-permute-start(bf16[2,64,256]{2,1,0:T(8,128)(2,1)S(1)} %get-tuple-element.27), channel_id=1, source_target_pairs={{0,3},{1,0},{2,1},{3,2},{4,7},{5,4},{6,5},{7,6},{8,11},{9,8},{10,9... | collective-permute-start | bytes 196616 | tf_op jit(solution)/shard_map/ppermute | solution.py:360

commit v2 on v1

--- a/solution.py
+++ b/solution.py
@@ -13,6 +13,7 @@
 ROWS = 16
 FINE = 32
 MIB = 1 << 20
+TALL = 128
 
 
 def fourier_tables(length):
@@ -207,25 +208,27 @@
     return kept, [next(i for i, other in enumerate(kept) if other is array) for array in arrays]
 
 
-def early_sum(green, sources, layers, start, size):
+def early_sum(green, sources, layers, start, size, total=None):
     arrays, at = unique([array for array, _, _ in sources])
     ny = arrays[0].shape[2]
 
     def body(green_ref, *refs):
-        total_ref = refs[-1]
-        given = [(refs[i], plane, row, layer) for i, (_, plane, row), layer in zip(at, sources, layers())]
+        ins, total_ref = refs[:-1], refs[-1]
+        given = [(ins[i], plane, row, layer) for i, (_, plane, row), layer in zip(at, sources, layers())]
 
         @pl.loop(0, size // ROWS)
         def _(step):
             row = pl.ds(pl.multiple_of(step * ROWS, ROWS), ROWS)
             for left in range(0, ny, 256):
                 cols = pl.ds(left, 256)
+                begun = (None, None) if total is None else (ins[-1][0, row, cols], ins[-1][1, row, cols])
                 total_ref[0, row, cols], total_ref[1, row, cols] = add_sources(
-                    (None, None), green_ref, given, step, start, cols
+                    begun, green_ref, given, step, start, cols
                 )
 
     flops = 8 * len(sources) * size * ny
-    return call(body, [struct((2, size, ny), F32)], [green, *arrays], flops=flops)[0]
+    ins = [green, *arrays] + ([] if total is None else [total])
+    return call(body, [struct((2, size, ny), F32)], ins, flops=flops)[0]
 
 
 def finish_rows(green, total, sources, layers, table_y, start, size, slabs):
@@ -265,7 +268,7 @@
 def transform_x(table_x, blocks, total=None, contrast=None):
     wide = blocks[0].shape[2]
     _, nx, half = table_x.shape
-    tall = min(nx, 128)
+    tall = min(nx, TALL)
 
     def fill(ins, right_ref):
         start = 0
@@ -364,8 +367,9 @@
         far_swap, across_swap = send(far[i], swap), send(across[i], swap)
         sources = [(owns[i], 0, 0), (own_swap, 0, start), (near[i], 0, 0), (near_swap[i], 0, 0), (far[i], 0, 0)]
         total = early_sum(green, sources, layers([(0, 0), (1, 1), (2, 4), (5, 3), (3, 5)]), start, size)
-        sources = [(far_swap, 0, 0), (across[i], 0, 0), (across_swap, 0, 0)]
-        halves.append(finish_rows(green, total, sources, layers([(4, 2), (7, 7), (6, 6)]), table_y, start, size, slabs))
+        sources = [(far_swap, 0, 0), (across[i], 0, 0)]
+        total = early_sum(green, sources, layers([(4, 2), (7, 7)]), start, size, total)
+        halves.append(finish_rows(green, total, [(across_swap, 0, 0)], layers([(6, 6)]), table_y, start, size, slabs))
     field = None
     for i, slab in enumerate(halves):
         blocks = [slab[0]] + [hop(m, slab[m]) for m in range(1, slabs)]

time: 48.8 us -> 48.8 us (level)
    pallas_call x5 -> x7, Pallas kernels: 4.1 us -> 4.06 us  [call(): pl.pallas_call(body, out_shape=[pltpu.VMEM(o.shape, o.dtype) for o in out...]
where the time goes in v2:
time: 48.8 us; the launch traced here: 48.6 us
  waiting for transfers between devices  21.8 us (45%)
  starting transfers between devices  17.4 us (36%)
  Pallas kernels  9.27 us (19%)
    ppermute x13, waiting for transfers between devices, send(): return lax.ppermute(v, 'depth', route)  17.7 us
    ppermute x6, starting transfers between devices, hop(): lax.ppermute(v, 'kslab', [(k, (k + m) % slabs) for k in range(slabs)])  10 us
    ppermute x13, starting transfers between devices, send(): return lax.ppermute(v, 'depth', route)  7.33 us
    ppermute x6, waiting for transfers between devices, hop(): lax.ppermute(v, 'kslab', [(k, (k + m) % slabs) for k in range(slabs)])  4.09 us
    pallas_call x7, Pallas kernels, call(): pl.pallas_call(body, out_shape=[pltpu.VMEM(o.shape, o.dtype) for o in out...  4.06 us
    pallas_call x1, Pallas kernels, prepare(): pl.pallas_call(body, out_shape=[pltpu.VMEM(o.shape, o.dtype) for o in out...  3.03 us
    pallas_call x1, Pallas kernels, transform_x(): pl.pallas_call(last_body, out_shape=struct((2, nx, wide), BF16), in_specs...  1.14 us
    pallas_call x1, Pallas kernels, split_rows(): pl.pallas_call(body, out_shape=[pltpu.VMEM((planes, size, ny), own.dtype)...  1.04 us
  transfers between devices with their start and end apart: 19, of which 8 were waited for; matrix products, arithmetic and copies ran while one was open for 0% of the time, Pallas kernels for 17%

profile of v2, /device:TPU:0, one launch (start us, length us, event | category | flops | bytes accessed | tf_op | source)
XLA Modules:
  0.0 48.6 jit_solution(6205766302444799717)
XLA Ops:
  0.0 0.5 %collective-permute-start = (bf16[2,128,1024]{2,1,0:T(8,128)(2,1)}, bf16[2,128,1024]{2,1,0:T(8,128)(2,1)S(1)}, u32[]{:S(2)}, u32[]{:S(2)}) collective-permute-start(bf16[2,128,1024]{2,1,0:T(8,128)(2,1)} %bitcast.6), channel_id=1, source_target_pairs={{0,4},{4,0},{8,12},{12,8},{16,20},{20,16},{24,28},{28,24},{1,5},{5... | collective-permute-start | bytes 1572872 | tf_op jit(solution)/shard_map/ppermute | solution.py:343
  0.5 1.0 %split_rows.1 = (bf16[2,64,1024]{2,1,0:T(8,128)(2,1)S(1)}, bf16[2,64,1024]{2,1,0:T(8,128)(2,1)S(1)}) custom-call(bf16[2,128,1024]{2,1,0:T(8,128)(2,1)} %bitcast.7), custom_call_target="tpu_custom_call" | custom-call | bytes 1048576 | tf_op jit(solution)/shard_map/split_rows/pallas_call | solution.py:118
  1.5 2.5 %collective-permute-start.12 = (bf16[2,64,1024]{2,1,0:T(8,128)(2,1)S(1)}, bf16[2,64,1024]{2,1,0:T(8,128)(2,1)S(1)}, u32[]{:S(2)}, u32[]{:S(2)}) collective-permute-start(bf16[2,64,1024]{2,1,0:T(8,128)(2,1)S(1)} %get-tuple-element.29.refs_0_), channel_id=1, source_target_pairs={{0,8},{4,20},{8,0},{12,28},{16,24},{20,4},{24,16},{28,12},{1,9},{5... | collective-permute-start | bytes 786440 | tf_op jit(solution)/shard_map/ppermute | solution.py:343
  4.2 4.3 %collective-permute-done.12.refs_2_ = bf16[2,64,1024]{2,1,0:T(8,128)(2,1)S(1)} collective-permute-done((bf16[2,64,1024]{2,1,0:T(8,128)(2,1)S(1)}, bf16[2,64,1024]{2,1,0:T(8,128)(2,1)S(1)}, u32[]{:S(2)}, u32[]{:S(2)}) %collective-permute-start.12) | collective-permute-done | bytes 262176 | tf_op jit(solution)/shard_map/ppermute | solution.py:343
  8.4 2.8 %collective-permute-done.3.refs_2_ = bf16[2,64,1024]{2,1,0:T(8,128)(2,1)S(1)} collective-permute-done((bf16[2,64,1024]{2,1,0:T(8,128)(2,1)S(1)}, bf16[2,64,1024]{2,1,0:T(8,128)(2,1)S(1)}, u32[]{:S(2)}, u32[]{:S(2)}) %collective-permute-start.3) | collective-permute-done | bytes 262176 | tf_op jit(solution)/shard_map/ppermute | solution.py:343
  11.3 2.1 %collective-permute-start.10 = (bf16[2,64,1024]{2,1,0:T(8,128)(2,1)S(1)}, bf16[2,64,1024]{2,1,0:T(8,128)(2,1)S(1)}, u32[]{:S(2)}, u32[]{:S(2)}) collective-permute-start(bf16[2,64,1024]{2,1,0:T(8,128)(2,1)S(1)} %get-tuple-element.35), channel_id=1, source_target_pairs={{0,8},{4,20},{8,0},{12,28},{16,24},{20,4},{24,16},{28,12},{1,9},{5... | collective-permute-start | bytes 786440 | tf_op jit(solution)/shard_map/ppermute | solution.py:343
  13.5 1.9 %collective-permute-start.1 = (bf16[2,64,1024]{2,1,0:T(8,128)(2,1)S(1)}, bf16[2,64,1024]{2,1,0:T(8,128)(2,1)S(1)}, u32[]{:S(2)}, u32[]{:S(2)}) collective-permute-start(bf16[2,64,1024]{2,1,0:T(8,128)(2,1)S(1)} %get-tuple-element.36), channel_id=1, source_target_pairs={{0,8},{4,20},{8,0},{12,28},{16,24},{20,4},{24,16},{28,12},{1,9},{5... | collective-permute-start | bytes 786440 | tf_op jit(solution)/shard_map/ppermute | solution.py:343
  15.5 2.2 %collective-permute-done.10.refs_4_ = bf16[2,64,1024]{2,1,0:T(8,128)(2,1)S(1)} collective-permute-done((bf16[2,64,1024]{2,1,0:T(8,128)(2,1)S(1)}, bf16[2,64,1024]{2,1,0:T(8,128)(2,1)S(1)}, u32[]{:S(2)}, u32[]{:S(2)}) %collective-permute-start.10) | collective-permute-done | bytes 262176 | tf_op jit(solution)/shard_map/ppermute | solution.py:343
  17.7 2.8 %collective-permute-done.14.refs_1_ = bf16[2,64,1024]{2,1,0:T(8,128)(2,1)S(1)} collective-permute-done((bf16[2,64,1024]{2,1,0:T(8,128)(2,1)S(1)}, bf16[2,64,1024]{2,1,0:T(8,128)(2,1)S(1)}, u32[]{:S(2)}, u32[]{:S(2)}) %collective-permute-start.14) | collective-permute-done | bytes 262176 | tf_op jit(solution)/shard_map/ppermute | solution.py:343
  20.5 2.8 %collective-permute-done.1.refs_4_ = bf16[2,64,1024]{2,1,0:T(8,128)(2,1)S(1)} collective-permute-done((bf16[2,64,1024]{2,1,0:T(8,128)(2,1)S(1)}, bf16[2,64,1024]{2,1,0:T(8,128)(2,1)S(1)}, u32[]{:S(2)}, u32[]{:S(2)}) %collective-permute-start.1) | collective-permute-done | bytes 262176 | tf_op jit(solution)/shard_map/ppermute | solution.py:343
  23.4 2.8 %collective-permute-done.5.refs_1_ = bf16[2,64,1024]{2,1,0:T(8,128)(2,1)S(1)} collective-permute-done((bf16[2,64,1024]{2,1,0:T(8,128)(2,1)S(1)}, bf16[2,64,1024]{2,1,0:T(8,128)(2,1)S(1)}, u32[]{:S(2)}, u32[]{:S(2)}) %collective-permute-start.5) | collective-permute-done | bytes 262176 | tf_op jit(solution)/shard_map/ppermute | solution.py:343
  26.2 3.0 %prepare.1 = (bf16[2,1024,1024]{2,1,0:T(8,128)(2,1)S(1)}, bf16[2,512,256]{2,1,0:T(8,128)(2,1)S(1)}, bf16[2,512,256]{2,1,0:T(8,128)(2,1)S(1)}, bf16[8,2,128,1024]{3,2,1,0:T(8,128)(2,1)S(1)}, f32[512,256]{1,0:T(8,128)S(1)}) custom-call(bf16[8,2,128,1024]{3,2,1,0:T(8,128)(2,1)} %bitcast.4, f32[512,256]{1,0:T(8,128)} %bitcast.5), custom_call_target="tpu_custom_call" | custom-call | flops 8388608 | bytes 8388608 | tf_op jit(solution)/shard_map/prepare/pallas_call | solution.py:172
  29.2 0.7 %shard_map.40.refs_2_ = f32[2,64,1024]{2,1,0:T(8,128)S(1)} custom-call(bf16[8,2,128,1024]{3,2,1,0:T(8,128)(2,1)S(1)} %get-tuple-element.21.green_ref, bf16[2,64,1024]{2,1,0:T(8,128)(2,1)S(1)} %get-tuple-element.29.refs_0_, bf16[2,128,1024]{2,1,0:T(8,128)(2,1)S(1)} %collective-permute-done.refs_1_, bf16[2,64,1024]{2,1,0:T(8,128)(2,1)S(1)} %collective-permute-done.12.refs_2_, ...), custom_call_target="tpu_custom_call" | custom-call | flops 2621440 | bytes 6291456 | tf_op jit(solution)/shard_map/pallas_call | solution.py:61
  30.2 0.9 %shard_map.42 = (bf16[2,64,256]{2,1,0:T(8,128)(2,1)S(1)}, bf16[2,64,256]{2,1,0:T(8,128)(2,1)S(1)}, bf16[2,64,256]{2,1,0:T(8,128)(2,1)S(1)}, bf16[2,64,256]{2,1,0:T(8,128)(2,1)S(1)}) custom-call(bf16[8,2,128,1024]{3,2,1,0:T(8,128)(2,1)S(1)} %get-tuple-element.21.green_ref, f32[2,64,1024]{2,1,0:T(8,128)S(1)} %shard_map.41.total_ref, ...), custom_call_target="tpu_custom_call" | custom-call | flops 536870912 | bytes 9437184 | tf_op jit(solution)/shard_map/pallas_call | solution.py:61
  31.1 2.2 %collective-permute-start.16 = (bf16[2,64,256]{2,1,0:T(8,128)(2,1)S(1)}, bf16[2,64,256]{2,1,0:T(8,128)(2,1)S(1)}, u32[]{:S(2)}, u32[]{:S(2)}) collective-permute-start(bf16[2,64,256]{2,1,0:T(8,128)(2,1)S(1)} %get-tuple-element.31), channel_id=1, source_target_pairs={{0,1},{1,2},{2,3},{3,0},{4,5},{5,6},{6,7},{7,4},{8,9},{9,10},{10,1... | collective-permute-start | bytes 196616 | tf_op jit(solution)/shard_map/ppermute | solution.py:363
  33.2 0.7 %shard_map.37.refs_2_ = f32[2,64,1024]{2,1,0:T(8,128)S(1)} custom-call(bf16[8,2,128,1024]{3,2,1,0:T(8,128)(2,1)S(1)} %get-tuple-element.21.green_ref, bf16[2,64,1024]{2,1,0:T(8,128)(2,1)S(1)} %get-tuple-element.22.refs_0_, bf16[2,128,1024]{2,1,0:T(8,128)(2,1)S(1)} %collective-permute-done.refs_1_, bf16[2,64,1024]{2,1,0:T(8,128)(2,1)S(1)} %collective-permute-done.3.refs_2_, ...), custom_call_target="tpu_custom_call" | custom-call | flops 2621440 | bytes 6291456 | tf_op jit(solution)/shard_map/pallas_call | solution.py:61
  33.9 2.7 %collective-permute-start.17 = (bf16[2,64,256]{2,1,0:T(8,128)(2,1)S(1)}, bf16[2,64,256]{2,1,0:T(8,128)(2,1)S(1)}, u32[]{:S(2)}, u32[]{:S(2)}) collective-permute-start(bf16[2,64,256]{2,1,0:T(8,128)(2,1)S(1)} %get-tuple-element.32), channel_id=1, source_target_pairs={{0,2},{1,3},{2,0},{3,1},{4,6},{5,7},{6,4},{7,5},{8,10},{9,11},{10,... | collective-permute-start | bytes 196616 | tf_op jit(solution)/shard_map/ppermute | solution.py:363
  36.6 1.3 %collective-permute-start.18 = (bf16[2,64,256]{2,1,0:T(8,128)(2,1)S(1)}, bf16[2,64,256]{2,1,0:T(8,128)(2,1)S(1)}, u32[]{:S(2)}, u32[]{:S(2)}) collective-permute-start(bf16[2,64,256]{2,1,0:T(8,128)(2,1)S(1)} %get-tuple-element.33), channel_id=1, source_target_pairs={{0,3},{1,0},{2,1},{3,2},{4,7},{5,4},{6,5},{7,6},{8,11},{9,8},{10,9... | collective-permute-start | bytes 196616 | tf_op jit(solution)/shard_map/ppermute | solution.py:363
  38.2 0.9 %shard_map.39 = (bf16[2,64,256]{2,1,0:T(8,128)(2,1)S(1)}, bf16[2,64,256]{2,1,0:T(8,128)(2,1)S(1)}, bf16[2,64,256]{2,1,0:T(8,128)(2,1)S(1)}, bf16[2,64,256]{2,1,0:T(8,128)(2,1)S(1)}) custom-call(bf16[8,2,128,1024]{3,2,1,0:T(8,128)(2,1)S(1)} %get-tuple-element.21.green_ref, f32[2,64,1024]{2,1,0:T(8,128)S(1)} %shard_map.38.total_ref, ...), custom_call_target="tpu_custom_call" | custom-call | flops 536870912 | bytes 9437184 | tf_op jit(solution)/shard_map/pallas_call | solution.py:61
  39.1 0.7 %collective-permute-start.7 = (bf16[2,64,256]{2,1,0:T(8,128)(2,1)S(1)}, bf16[2,64,256]{2,1,0:T(8,128)(2,1)S(1)}, u32[]{:S(2)}, u32[]{:S(2)}) collective-permute-start(bf16[2,64,256]{2,1,0:T(8,128)(2,1)S(1)} %get-tuple-element.25), channel_id=1, source_target_pairs={{0,1},{1,2},{2,3},{3,0},{4,5},{5,6},{6,7},{7,4},{8,9},{9,10},{10,1... | collective-permute-start | bytes 196616 | tf_op jit(solution)/shard_map/ppermute | solution.py:363
  40.2 2.8 %collective-permute-start.9 = (bf16[2,64,256]{2,1,0:T(8,128)(2,1)S(1)}, bf16[2,64,256]{2,1,0:T(8,128)(2,1)S(1)}, u32[]{:S(2)}, u32[]{:S(2)}) collective-permute-start(bf16[2,64,256]{2,1,0:T(8,128)(2,1)S(1)} %get-tuple-element.27), channel_id=1, source_target_pairs={{0,3},{1,0},{2,1},{3,2},{4,7},{5,4},{6,5},{7,6},{8,11},{9,8},{10,9... | collective-permute-start | bytes 196616 | tf_op jit(solution)/shard_map/ppermute | solution.py:363
  43.4 2.5 %collective-permute-done.7.refs_1_ = bf16[2,64,256]{2,1,0:T(8,128)(2,1)S(1)} collective-permute-done((bf16[2,64,256]{2,1,0:T(8,128)(2,1)S(1)}, bf16[2,64,256]{2,1,0:T(8,128)(2,1)S(1)}, u32[]{:S(2)}, u32[]{:S(2)}) %collective-permute-start.7) | collective-permute-done | bytes 65568 | tf_op jit(solution)/shard_map/ppermute | solution.py:363
  45.9 1.6 %collective-permute-done.8.refs_2_ = bf16[2,64,256]{2,1,0:T(8,128)(2,1)S(1)} collective-permute-done((bf16[2,64,256]{2,1,0:T(8,128)(2,1)S(1)}, bf16[2,64,256]{2,1,0:T(8,128)(2,1)S(1)}, u32[]{:S(2)}, u32[]{:S(2)}) %collective-permute-start.8) | collective-permute-done | bytes 65568 | tf_op jit(solution)/shard_map/ppermute | solution.py:363
  47.5 1.1 %transform_x_last.1 = bf16[2,512,256]{2,1,0:T(8,128)(2,1)} custom-call(bf16[2,512,256]{2,1,0:T(8,128)(2,1)S(1)} %get-tuple-element.20.table_ref, bf16[2,64,256]{2,1,0:T(8,128)(2,1)S(1)} %get-tuple-element.24.refs_0_, bf16[2,64,256]{2,1,0:T(8,128)(2,1)S(1)} %collective-permute-done.7.refs_1_, bf16[2,64,256]{2,1,0:T(8,128)(2,1)S(1)} %collective-permute-done.8.refs_2_, ...), custom_call_target="tpu_custom_call" | custom-call | flops 268435456 | bytes 4194304 | tf_op jit(solution)/shard_map/transform_x_last/pallas_call | solution.py:322
  (25 shorter events, 1.6 us)
Async XLA Ops:
  0.0 11.3 %collective-permute-start = (bf16[2,128,1024]{2,1,0:T(8,128)(2,1)}, bf16[2,128,1024]{2,1,0:T(8,128)(2,1)S(1)}, u32[]{:S(2)}, u32[]{:S(2)}) collective-permute-start(bf16[2,128,1024]{2,1,0:T(8,128)(2,1)} %bitcast.6), channel_id=1, source_target_pairs={{0,4},{4,0},{8,12},{12,8},{16,20},{20,16},{24,28},{28,24},{1,5},{5... | collective-permute-start | bytes 1572872 | tf_op jit(solution)/shard_map/ppermute | solution.py:343
  1.5 6.9 %collective-permute-start.12 = (bf16[2,64,1024]{2,1,0:T(8,128)(2,1)S(1)}, bf16[2,64,1024]{2,1,0:T(8,128)(2,1)S(1)}, u32[]{:S(2)}, u32[]{:S(2)}) collective-permute-start(bf16[2,64,1024]{2,1,0:T(8,128)(2,1)S(1)} %get-tuple-element.29.refs_0_), channel_id=1, source_target_pairs={{0,8},{4,20},{8,0},{12,28},{16,24},{20,4},{24,16},{28,12},{1,9},{5... | collective-permute-start | bytes 786440 | tf_op jit(solution)/shard_map/ppermute | solution.py:343
  4.1 7.2 %collective-permute-start.3 = (bf16[2,64,1024]{2,1,0:T(8,128)(2,1)S(1)}, bf16[2,64,1024]{2,1,0:T(8,128)(2,1)S(1)}, u32[]{:S(2)}, u32[]{:S(2)}) collective-permute-start(bf16[2,64,1024]{2,1,0:T(8,128)(2,1)S(1)} %get-tuple-element.22.refs_0_), channel_id=1, source_target_pairs={{0,8},{4,20},{8,0},{12,28},{16,24},{20,4},{24,16},{28,12},{1,9},{5... | collective-permute-start | bytes 786440 | tf_op jit(solution)/shard_map/ppermute | solution.py:343
  8.4 4.9 %collective-permute-start.13 = (bf16[2,64,1024]{2,1,0:T(8,128)(2,1)S(1)}, bf16[2,64,1024]{2,1,0:T(8,128)(2,1)S(1)}, u32[]{:S(2)}, u32[]{:S(2)}) collective-permute-start(bf16[2,64,1024]{2,1,0:T(8,128)(2,1)S(1)} %collective-permute-done.12.refs_2_), channel_id=1, source_target_pairs={{0,4},{4,0},{8,12},{12,8},{16,20},{20,16},{24,28},{28,24},{1,5},{5... | collective-permute-start | bytes 786440 | tf_op jit(solution)/shard_map/ppermute | solution.py:343
  11.3 4.2 %collective-permute-start.4 = (bf16[2,64,1024]{2,1,0:T(8,128)(2,1)S(1)}, bf16[2,64,1024]{2,1,0:T(8,128)(2,1)S(1)}, u32[]{:S(2)}, u32[]{:S(2)}) collective-permute-start(bf16[2,64,1024]{2,1,0:T(8,128)(2,1)S(1)} %collective-permute-done.3.refs_2_), channel_id=1, source_target_pairs={{0,4},{4,0},{8,12},{12,8},{16,20},{20,16},{24,28},{28,24},{1,5},{5... | collective-permute-start | bytes 786440 | tf_op jit(solution)/shard_map/ppermute | solution.py:343
  11.3 6.4 %collective-permute-start.10 = (bf16[2,64,1024]{2,1,0:T(8,128)(2,1)S(1)}, bf16[2,64,1024]{2,1,0:T(8,128)(2,1)S(1)}, u32[]{:S(2)}, u32[]{:S(2)}) collective-permute-start(bf16[2,64,1024]{2,1,0:T(8,128)(2,1)S(1)} %get-tuple-element.35), channel_id=1, source_target_pairs={{0,8},{4,20},{8,0},{12,28},{16,24},{20,4},{24,16},{28,12},{1,9},{5... | collective-permute-start | bytes 786440 | tf_op jit(solution)/shard_map/ppermute | solution.py:343
  13.4 7.2 %collective-permute-start.14 = (bf16[2,64,1024]{2,1,0:T(8,128)(2,1)S(1)}, bf16[2,64,1024]{2,1,0:T(8,128)(2,1)S(1)}, u32[]{:S(2)}, u32[]{:S(2)}) collective-permute-start(bf16[2,64,1024]{2,1,0:T(8,128)(2,1)S(1)} %collective-permute-done.13.refs_3_), channel_id=1, source_target_pairs={{0,8},{4,20},{8,0},{12,28},{16,24},{20,4},{24,16},{28,12},{1,9},{5... | collective-permute-start | bytes 786440 | tf_op jit(solution)/shard_map/ppermute | solution.py:343
  13.5 9.9 %collective-permute-start.1 = (bf16[2,64,1024]{2,1,0:T(8,128)(2,1)S(1)}, bf16[2,64,1024]{2,1,0:T(8,128)(2,1)S(1)}, u32[]{:S(2)}, u32[]{:S(2)}) collective-permute-start(bf16[2,64,1024]{2,1,0:T(8,128)(2,1)S(1)} %get-tuple-element.36), channel_id=1, source_target_pairs={{0,8},{4,20},{8,0},{12,28},{16,24},{20,4},{24,16},{28,12},{1,9},{5... | collective-permute-start | bytes 786440 | tf_op jit(solution)/shard_map/ppermute | solution.py:343
  15.4 10.7 %collective-permute-start.5 = (bf16[2,64,1024]{2,1,0:T(8,128)(2,1)S(1)}, bf16[2,64,1024]{2,1,0:T(8,128)(2,1)S(1)}, u32[]{:S(2)}, u32[]{:S(2)}) collective-permute-start(bf16[2,64,1024]{2,1,0:T(8,128)(2,1)S(1)} %collective-permute-done.4.refs_3_), channel_id=1, source_target_pairs={{0,8},{4,20},{8,0},{12,28},{16,24},{20,4},{24,16},{28,12},{1,9},{5... | collective-permute-start | bytes 786440 | tf_op jit(solution)/shard_map/ppermute | solution.py:343
  17.7 12.2 %collective-permute-start.11 = (bf16[2,64,1024]{2,1,0:T(8,128)(2,1)S(1)}, bf16[2,64,1024]{2,1,0:T(8,128)(2,1)S(1)}, u32[]{:S(2)}, u32[]{:S(2)}) collective-permute-start(bf16[2,64,1024]{2,1,0:T(8,128)(2,1)S(1)} %collective-permute-done.10.refs_4_), channel_id=1, source_target_pairs={{0,4},{4,0},{8,12},{12,8},{16,20},{20,16},{24,28},{28,24},{1,5},{5... | collective-permute-start | bytes 786440 | tf_op jit(solution)/shard_map/ppermute | solution.py:343
  20.5 9.7 %collective-permute-start.15 = (bf16[2,64,1024]{2,1,0:T(8,128)(2,1)S(1)}, bf16[2,64,1024]{2,1,0:T(8,128)(2,1)S(1)}, u32[]{:S(2)}, u32[]{:S(2)}) collective-permute-start(bf16[2,64,1024]{2,1,0:T(8,128)(2,1)S(1)} %collective-permute-done.14.refs_1_), channel_id=1, source_target_pairs={{0,4},{4,0},{8,12},{12,8},{16,20},{20,16},{24,28},{28,24},{1,5},{5... | collective-permute-start | bytes 786440 | tf_op jit(solution)/shard_map/ppermute | solution.py:343
  23.4 14.6 %collective-permute-start.2 = (bf16[2,64,1024]{2,1,0:T(8,128)(2,1)S(1)}, bf16[2,64,1024]{2,1,0:T(8,128)(2,1)S(1)}, u32[]{:S(2)}, u32[]{:S(2)}) collective-permute-start(bf16[2,64,1024]{2,1,0:T(8,128)(2,1)S(1)} %collective-permute-done.1.refs_4_), channel_id=1, source_target_pairs={{0,4},{4,0},{8,12},{12,8},{16,20},{20,16},{24,28},{28,24},{1,5},{5... | collective-permute-start | bytes 786440 | tf_op jit(solution)/shard_map/ppermute | solution.py:343
  26.2 12.0 %collective-permute-start.6 = (bf16[2,64,1024]{2,1,0:T(8,128)(2,1)S(1)}, bf16[2,64,1024]{2,1,0:T(8,128)(2,1)S(1)}, u32[]{:S(2)}, u32[]{:S(2)}) collective-permute-start(bf16[2,64,1024]{2,1,0:T(8,128)(2,1)S(1)} %collective-permute-done.5.refs_1_), channel_id=1, source_target_pairs={{0,4},{4,0},{8,12},{12,8},{16,20},{20,16},{24,28},{28,24},{1,5},{5... | collective-permute-start | bytes 786440 | tf_op jit(solution)/shard_map/ppermute | solution.py:343
  31.1 9.1 %collective-permute-start.16 = (bf16[2,64,256]{2,1,0:T(8,128)(2,1)S(1)}, bf16[2,64,256]{2,1,0:T(8,128)(2,1)S(1)}, u32[]{:S(2)}, u32[]{:S(2)}) collective-permute-start(bf16[2,64,256]{2,1,0:T(8,128)(2,1)S(1)} %get-tuple-element.31), channel_id=1, source_target_pairs={{0,1},{1,2},{2,3},{3,0},{4,5},{5,6},{6,7},{7,4},{8,9},{9,10},{10,1... | collective-permute-start | bytes 196616 | tf_op jit(solution)/shard_map/ppermute | solution.py:363
  33.9 9.0 %collective-permute-start.17 = (bf16[2,64,256]{2,1,0:T(8,128)(2,1)S(1)}, bf16[2,64,256]{2,1,0:T(8,128)(2,1)S(1)}, u32[]{:S(2)}, u32[]{:S(2)}) collective-permute-start(bf16[2,64,256]{2,1,0:T(8,128)(2,1)S(1)} %get-tuple-element.32), channel_id=1, source_target_pairs={{0,2},{1,3},{2,0},{3,1},{4,6},{5,7},{6,4},{7,5},{8,10},{9,11},{10,... | collective-permute-start | bytes 196616 | tf_op jit(solution)/shard_map/ppermute | solution.py:363
  36.6 6.4 %collective-permute-start.18 = (bf16[2,64,256]{2,1,0:T(8,128)(2,1)S(1)}, bf16[2,64,256]{2,1,0:T(8,128)(2,1)S(1)}, u32[]{:S(2)}, u32[]{:S(2)}) collective-permute-start(bf16[2,64,256]{2,1,0:T(8,128)(2,1)S(1)} %get-tuple-element.33), channel_id=1, source_target_pairs={{0,3},{1,0},{2,1},{3,2},{4,7},{5,4},{6,5},{7,6},{8,11},{9,8},{10,9... | collective-permute-start | bytes 196616 | tf_op jit(solution)/shard_map/ppermute | solution.py:363
  39.1 6.8 %collective-permute-start.7 = (bf16[2,64,256]{2,1,0:T(8,128)(2,1)S(1)}, bf16[2,64,256]{2,1,0:T(8,128)(2,1)S(1)}, u32[]{:S(2)}, u32[]{:S(2)}) collective-permute-start(bf16[2,64,256]{2,1,0:T(8,128)(2,1)S(1)} %get-tuple-element.25), channel_id=1, source_target_pairs={{0,1},{1,2},{2,3},{3,0},{4,5},{5,6},{6,7},{7,4},{8,9},{9,10},{10,1... | collective-permute-start | bytes 196616 | tf_op jit(solution)/shard_map/ppermute | solution.py:363
  39.8 7.7 %collective-permute-start.8 = (bf16[2,64,256]{2,1,0:T(8,128)(2,1)S(1)}, bf16[2,64,256]{2,1,0:T(8,128)(2,1)S(1)}, u32[]{:S(2)}, u32[]{:S(2)}) collective-permute-start(bf16[2,64,256]{2,1,0:T(8,128)(2,1)S(1)} %get-tuple-element.26), channel_id=1, source_target_pairs={{0,2},{1,3},{2,0},{3,1},{4,6},{5,7},{6,4},{7,5},{8,10},{9,11},{10,... | collective-permute-start | bytes 196616 | tf_op jit(solution)/shard_map/ppermute | solution.py:363
  40.2 7.3 %collective-permute-start.9 = (bf16[2,64,256]{2,1,0:T(8,128)(2,1)S(1)}, bf16[2,64,256]{2,1,0:T(8,128)(2,1)S(1)}, u32[]{:S(2)}, u32[]{:S(2)}) collective-permute-start(bf16[2,64,256]{2,1,0:T(8,128)(2,1)S(1)} %get-tuple-element.27), channel_id=1, source_target_pairs={{0,3},{1,0},{2,1},{3,2},{4,7},{5,4},{6,5},{7,6},{8,11},{9,8},{10,9... | collective-permute-start | bytes 196616 | tf_op jit(solution)/shard_map/ppermute | solution.py:363

commit v3 on v2

--- a/solution.py
+++ b/solution.py
@@ -14,6 +14,10 @@
 FINE = 32
 MIB = 1 << 20
 TALL = 128
+ROUTES = (
+    ((0, 1, 2, 3), (1, 2, 3, 0), (2, 3, 0, 1), (3, 0, 1, 2)),
+    ((0, 1, 2, 3), (1, 2, 3, 0), (3, 0, 1, 2), (2, 3, 0, 1)),
+)
 
 
 def fourier_tables(length):
@@ -77,6 +81,13 @@
     return v & (length - 1) if length & (length - 1) == 0 else lax.rem(v, length)
 
 
+def at_rank(rank, values):
+    picked = values[0]
+    for k, value in enumerate(values[1:], 1):
+        picked = jnp.where(rank == k, value, picked)
+    return picked
+
+
 def fill_table(length, columns, coarse_ref, put):
     width = columns.shape[1]
     unit = 2.0 * math.pi / length
@@ -141,7 +152,15 @@
         z = lax.axis_index("kslab")
         wide = ny // slabs
         lane = lax.broadcasted_iota(jnp.int32, (1, ny), 1)
-        columns = lax.rem(lane // wide + z, slabs) * wide + lane % wide
+        columns = lane
+        core = lax.rem(lax.axis_index("depth"), 2)
+
+        def by_core(*values):
+            return jnp.where(core == 0, *[at_rank(z, v) for v in values])
+
+        for m, routes in enumerate(zip(*ROUTES)):
+            here = by_core(*routes) * wide - m * wide + lane
+            columns = jnp.where(lane >= m * wide, here, columns)
 
         def put_y(row, left, cols, cos, sin):
             ty_ref[0, row, cols] = cos.astype(BF16)
@@ -153,7 +172,8 @@
             lane = lax.broadcasted_iota(jnp.int32, (1, total), 1)
             columns, at = lane, 0
             for m, start, size in blocks:
-                here = lax.rem(z + slabs - m, slabs) * kx_dev + start - at + lane
+                origins = [[routes[m].index(k) for k in range(slabs)] for routes in ROUTES]
+                here = by_core(*origins) * kx_dev + start - at + lane
                 columns, at = jnp.where(lane >= at, here, columns), at + size
 
             def put_x(row, left, cols, cos, sin):
@@ -360,7 +380,8 @@
     across = [send(v, out) for v in near_swap]
 
     def hop(m, v):
-        return lax.ppermute(v, "kslab", [(k, (k + m) % slabs) for k in range(slabs)])
+        pairs = [(d * slabs + k, d * slabs + ROUTES[d % 2][m][k]) for d in range(8) for k in range(slabs)]
+        return lax.ppermute(v, ("depth", "kslab"), pairs)
 
     halves = []
     for i, (start, size) in enumerate(parts):

time: 48.8 us -> 48.6 us (level)
  no operation moved by 1% of the time
where the time goes in v3:
time: 48.6 us; the launch traced here: 48.5 us
  waiting for transfers between devices  21.7 us (45%)
  starting transfers between devices  17.4 us (36%)
  Pallas kernels  9.27 us (19%)
    ppermute x13, waiting for transfers between devices, send(): return lax.ppermute(v, 'depth', route)  17.7 us
    ppermute x6, starting transfers between devices, hop(): return lax.ppermute(v, ('depth', 'kslab'), pairs)  10 us
    ppermute x13, starting transfers between devices, send(): return lax.ppermute(v, 'depth', route)  7.33 us
    pallas_call x7, Pallas kernels, call(): pl.pallas_call(body, out_shape=[pltpu.VMEM(o.shape, o.dtype) for o in out...  4.07 us
    ppermute x6, waiting for transfers between devices, hop(): return lax.ppermute(v, ('depth', 'kslab'), pairs)  3.94 us
    pallas_call x1, Pallas kernels, prepare(): pl.pallas_call(body, out_shape=[pltpu.VMEM(o.shape, o.dtype) for o in out...  3.02 us
    pallas_call x1, Pallas kernels, transform_x(): pl.pallas_call(last_body, out_shape=struct((2, nx, wide), BF16), in_specs...  1.14 us
    pallas_call x1, Pallas kernels, split_rows(): pl.pallas_call(body, out_shape=[pltpu.VMEM((planes, size, ny), own.dtype)...  1.04 us
  transfers between devices with their start and end apart: 19, of which 8 were waited for; matrix products, arithmetic and copies ran while one was open for 0% of the time, Pallas kernels for 17%

profile of v3, /device:TPU:0, one launch (start us, length us, event | category | flops | bytes accessed | tf_op | source)
XLA Modules:
  0.0 48.5 jit_solution(8010759550765296305)
XLA Ops:
  0.0 0.5 %collective-permute-start = (bf16[2,128,1024]{2,1,0:T(8,128)(2,1)}, bf16[2,128,1024]{2,1,0:T(8,128)(2,1)S(1)}, u32[]{:S(2)}, u32[]{:S(2)}) collective-permute-start(bf16[2,128,1024]{2,1,0:T(8,128)(2,1)} %bitcast.6), channel_id=1, source_target_pairs={{0,4},{4,0},{8,12},{12,8},{16,20},{20,16},{24,28},{28,24},{1,5},{5... | collective-permute-start | bytes 1572872 | tf_op jit(solution)/shard_map/ppermute | solution.py:363
  0.5 1.0 %split_rows.1 = (bf16[2,64,1024]{2,1,0:T(8,128)(2,1)S(1)}, bf16[2,64,1024]{2,1,0:T(8,128)(2,1)S(1)}) custom-call(bf16[2,128,1024]{2,1,0:T(8,128)(2,1)} %bitcast.7), custom_call_target="tpu_custom_call" | custom-call | bytes 1048576 | tf_op jit(solution)/shard_map/split_rows/pallas_call | solution.py:129
  1.5 2.5 %collective-permute-start.12 = (bf16[2,64,1024]{2,1,0:T(8,128)(2,1)S(1)}, bf16[2,64,1024]{2,1,0:T(8,128)(2,1)S(1)}, u32[]{:S(2)}, u32[]{:S(2)}) collective-permute-start(bf16[2,64,1024]{2,1,0:T(8,128)(2,1)S(1)} %get-tuple-element.29.refs_0_), channel_id=1, source_target_pairs={{0,8},{4,20},{8,0},{12,28},{16,24},{20,4},{24,16},{28,12},{1,9},{5... | collective-permute-start | bytes 786440 | tf_op jit(solution)/shard_map/ppermute | solution.py:363
  4.2 4.3 %collective-permute-done.12.refs_2_ = bf16[2,64,1024]{2,1,0:T(8,128)(2,1)S(1)} collective-permute-done((bf16[2,64,1024]{2,1,0:T(8,128)(2,1)S(1)}, bf16[2,64,1024]{2,1,0:T(8,128)(2,1)S(1)}, u32[]{:S(2)}, u32[]{:S(2)}) %collective-permute-start.12) | collective-permute-done | bytes 262176 | tf_op jit(solution)/shard_map/ppermute | solution.py:363
  8.4 2.8 %collective-permute-done.3.refs_2_ = bf16[2,64,1024]{2,1,0:T(8,128)(2,1)S(1)} collective-permute-done((bf16[2,64,1024]{2,1,0:T(8,128)(2,1)S(1)}, bf16[2,64,1024]{2,1,0:T(8,128)(2,1)S(1)}, u32[]{:S(2)}, u32[]{:S(2)}) %collective-permute-start.3) | collective-permute-done | bytes 262176 | tf_op jit(solution)/shard_map/ppermute | solution.py:363
  11.3 2.1 %collective-permute-start.10 = (bf16[2,64,1024]{2,1,0:T(8,128)(2,1)S(1)}, bf16[2,64,1024]{2,1,0:T(8,128)(2,1)S(1)}, u32[]{:S(2)}, u32[]{:S(2)}) collective-permute-start(bf16[2,64,1024]{2,1,0:T(8,128)(2,1)S(1)} %get-tuple-element.35), channel_id=1, source_target_pairs={{0,8},{4,20},{8,0},{12,28},{16,24},{20,4},{24,16},{28,12},{1,9},{5... | collective-permute-start | bytes 786440 | tf_op jit(solution)/shard_map/ppermute | solution.py:363
  13.5 1.9 %collective-permute-start.1 = (bf16[2,64,1024]{2,1,0:T(8,128)(2,1)S(1)}, bf16[2,64,1024]{2,1,0:T(8,128)(2,1)S(1)}, u32[]{:S(2)}, u32[]{:S(2)}) collective-permute-start(bf16[2,64,1024]{2,1,0:T(8,128)(2,1)S(1)} %get-tuple-element.36), channel_id=1, source_target_pairs={{0,8},{4,20},{8,0},{12,28},{16,24},{20,4},{24,16},{28,12},{1,9},{5... | collective-permute-start | bytes 786440 | tf_op jit(solution)/shard_map/ppermute | solution.py:363
  15.5 2.2 %collective-permute-done.10.refs_4_ = bf16[2,64,1024]{2,1,0:T(8,128)(2,1)S(1)} collective-permute-done((bf16[2,64,1024]{2,1,0:T(8,128)(2,1)S(1)}, bf16[2,64,1024]{2,1,0:T(8,128)(2,1)S(1)}, u32[]{:S(2)}, u32[]{:S(2)}) %collective-permute-start.10) | collective-permute-done | bytes 262176 | tf_op jit(solution)/shard_map/ppermute | solution.py:363
  17.7 2.8 %collective-permute-done.14.refs_1_ = bf16[2,64,1024]{2,1,0:T(8,128)(2,1)S(1)} collective-permute-done((bf16[2,64,1024]{2,1,0:T(8,128)(2,1)S(1)}, bf16[2,64,1024]{2,1,0:T(8,128)(2,1)S(1)}, u32[]{:S(2)}, u32[]{:S(2)}) %collective-permute-start.14) | collective-permute-done | bytes 262176 | tf_op jit(solution)/shard_map/ppermute | solution.py:363
  20.5 2.8 %collective-permute-done.1.refs_4_ = bf16[2,64,1024]{2,1,0:T(8,128)(2,1)S(1)} collective-permute-done((bf16[2,64,1024]{2,1,0:T(8,128)(2,1)S(1)}, bf16[2,64,1024]{2,1,0:T(8,128)(2,1)S(1)}, u32[]{:S(2)}, u32[]{:S(2)}) %collective-permute-start.1) | collective-permute-done | bytes 262176 | tf_op jit(solution)/shard_map/ppermute | solution.py:363
  23.4 2.8 %collective-permute-done.5.refs_1_ = bf16[2,64,1024]{2,1,0:T(8,128)(2,1)S(1)} collective-permute-done((bf16[2,64,1024]{2,1,0:T(8,128)(2,1)S(1)}, bf16[2,64,1024]{2,1,0:T(8,128)(2,1)S(1)}, u32[]{:S(2)}, u32[]{:S(2)}) %collective-permute-start.5) | collective-permute-done | bytes 262176 | tf_op jit(solution)/shard_map/ppermute | solution.py:363
  26.2 3.0 %prepare.1 = (bf16[2,1024,1024]{2,1,0:T(8,128)(2,1)S(1)}, bf16[2,512,256]{2,1,0:T(8,128)(2,1)S(1)}, bf16[2,512,256]{2,1,0:T(8,128)(2,1)S(1)}, bf16[8,2,128,1024]{3,2,1,0:T(8,128)(2,1)S(1)}, f32[512,256]{1,0:T(8,128)S(1)}) custom-call(bf16[8,2,128,1024]{3,2,1,0:T(8,128)(2,1)} %bitcast.4, f32[512,256]{1,0:T(8,128)} %bitcast.5), custom_call_target="tpu_custom_call" | custom-call | flops 8388608 | bytes 8388608 | tf_op jit(solution)/shard_map/prepare/pallas_call | solution.py:192
  29.2 0.7 %shard_map.40.refs_2_ = f32[2,64,1024]{2,1,0:T(8,128)S(1)} custom-call(bf16[8,2,128,1024]{3,2,1,0:T(8,128)(2,1)S(1)} %get-tuple-element.21.green_ref, bf16[2,64,1024]{2,1,0:T(8,128)(2,1)S(1)} %get-tuple-element.29.refs_0_, bf16[2,128,1024]{2,1,0:T(8,128)(2,1)S(1)} %collective-permute-done.refs_1_, bf16[2,64,1024]{2,1,0:T(8,128)(2,1)S(1)} %collective-permute-done.12.refs_2_, ...), custom_call_target="tpu_custom_call" | custom-call | flops 2621440 | bytes 6291456 | tf_op jit(solution)/shard_map/pallas_call | solution.py:65
  30.2 0.9 %shard_map.42 = (bf16[2,64,256]{2,1,0:T(8,128)(2,1)S(1)}, bf16[2,64,256]{2,1,0:T(8,128)(2,1)S(1)}, bf16[2,64,256]{2,1,0:T(8,128)(2,1)S(1)}, bf16[2,64,256]{2,1,0:T(8,128)(2,1)S(1)}) custom-call(bf16[8,2,128,1024]{3,2,1,0:T(8,128)(2,1)S(1)} %get-tuple-element.21.green_ref, f32[2,64,1024]{2,1,0:T(8,128)S(1)} %shard_map.41.total_ref, ...), custom_call_target="tpu_custom_call" | custom-call | flops 536870912 | bytes 9437184 | tf_op jit(solution)/shard_map/pallas_call | solution.py:65
  31.1 2.2 %collective-permute-start.16 = (bf16[2,64,256]{2,1,0:T(8,128)(2,1)S(1)}, bf16[2,64,256]{2,1,0:T(8,128)(2,1)S(1)}, u32[]{:S(2)}, u32[]{:S(2)}) collective-permute-start(bf16[2,64,256]{2,1,0:T(8,128)(2,1)S(1)} %get-tuple-element.31), channel_id=1, source_target_pairs={{0,1},{1,2},{2,3},{3,0},{4,5},{5,6},{6,7},{7,4},{8,9},{9,10},{10,1... | collective-permute-start | bytes 196616 | tf_op jit(solution)/shard_map/ppermute | solution.py:384
  33.2 0.7 %shard_map.37.refs_2_ = f32[2,64,1024]{2,1,0:T(8,128)S(1)} custom-call(bf16[8,2,128,1024]{3,2,1,0:T(8,128)(2,1)S(1)} %get-tuple-element.21.green_ref, bf16[2,64,1024]{2,1,0:T(8,128)(2,1)S(1)} %get-tuple-element.22.refs_0_, bf16[2,128,1024]{2,1,0:T(8,128)(2,1)S(1)} %collective-permute-done.refs_1_, bf16[2,64,1024]{2,1,0:T(8,128)(2,1)S(1)} %collective-permute-done.3.refs_2_, ...), custom_call_target="tpu_custom_call" | custom-call | flops 2621440 | bytes 6291456 | tf_op jit(solution)/shard_map/pallas_call | solution.py:65
  33.9 2.6 %collective-permute-start.17 = (bf16[2,64,256]{2,1,0:T(8,128)(2,1)S(1)}, bf16[2,64,256]{2,1,0:T(8,128)(2,1)S(1)}, u32[]{:S(2)}, u32[]{:S(2)}) collective-permute-start(bf16[2,64,256]{2,1,0:T(8,128)(2,1)S(1)} %get-tuple-element.32), channel_id=1, source_target_pairs={{0,2},{1,3},{2,0},{3,1},{4,7},{5,4},{6,5},{7,6},{8,10},{9,11},{10,... | collective-permute-start | bytes 196616 | tf_op jit(solution)/shard_map/ppermute | solution.py:384
  36.6 1.3 %collective-permute-start.18 = (bf16[2,64,256]{2,1,0:T(8,128)(2,1)S(1)}, bf16[2,64,256]{2,1,0:T(8,128)(2,1)S(1)}, u32[]{:S(2)}, u32[]{:S(2)}) collective-permute-start(bf16[2,64,256]{2,1,0:T(8,128)(2,1)S(1)} %get-tuple-element.33), channel_id=1, source_target_pairs={{0,3},{1,0},{2,1},{3,2},{4,6},{5,7},{6,4},{7,5},{8,11},{9,8},{10,9... | collective-permute-start | bytes 196616 | tf_op jit(solution)/shard_map/ppermute | solution.py:384
  38.2 0.9 %shard_map.39 = (bf16[2,64,256]{2,1,0:T(8,128)(2,1)S(1)}, bf16[2,64,256]{2,1,0:T(8,128)(2,1)S(1)}, bf16[2,64,256]{2,1,0:T(8,128)(2,1)S(1)}, bf16[2,64,256]{2,1,0:T(8,128)(2,1)S(1)}) custom-call(bf16[8,2,128,1024]{3,2,1,0:T(8,128)(2,1)S(1)} %get-tuple-element.21.green_ref, f32[2,64,1024]{2,1,0:T(8,128)S(1)} %shard_map.38.total_ref, ...), custom_call_target="tpu_custom_call" | custom-call | flops 536870912 | bytes 9437184 | tf_op jit(solution)/shard_map/pallas_call | solution.py:65
  39.1 0.7 %collective-permute-start.7 = (bf16[2,64,256]{2,1,0:T(8,128)(2,1)S(1)}, bf16[2,64,256]{2,1,0:T(8,128)(2,1)S(1)}, u32[]{:S(2)}, u32[]{:S(2)}) collective-permute-start(bf16[2,64,256]{2,1,0:T(8,128)(2,1)S(1)} %get-tuple-element.25), channel_id=1, source_target_pairs={{0,1},{1,2},{2,3},{3,0},{4,5},{5,6},{6,7},{7,4},{8,9},{9,10},{10,1... | collective-permute-start | bytes 196616 | tf_op jit(solution)/shard_map/ppermute | solution.py:384
  40.1 2.8 %collective-permute-start.9 = (bf16[2,64,256]{2,1,0:T(8,128)(2,1)S(1)}, bf16[2,64,256]{2,1,0:T(8,128)(2,1)S(1)}, u32[]{:S(2)}, u32[]{:S(2)}) collective-permute-start(bf16[2,64,256]{2,1,0:T(8,128)(2,1)S(1)} %get-tuple-element.27), channel_id=1, source_target_pairs={{0,3},{1,0},{2,1},{3,2},{4,6},{5,7},{6,4},{7,5},{8,11},{9,8},{10,9... | collective-permute-start | bytes 196616 | tf_op jit(solution)/shard_map/ppermute | solution.py:384
  43.4 2.0 %collective-permute-done.7.refs_1_ = bf16[2,64,256]{2,1,0:T(8,128)(2,1)S(1)} collective-permute-done((bf16[2,64,256]{2,1,0:T(8,128)(2,1)S(1)}, bf16[2,64,256]{2,1,0:T(8,128)(2,1)S(1)}, u32[]{:S(2)}, u32[]{:S(2)}) %collective-permute-start.7) | collective-permute-done | bytes 65568 | tf_op jit(solution)/shard_map/ppermute | solution.py:384
  45.4 1.9 %collective-permute-done.8.refs_2_ = bf16[2,64,256]{2,1,0:T(8,128)(2,1)S(1)} collective-permute-done((bf16[2,64,256]{2,1,0:T(8,128)(2,1)S(1)}, bf16[2,64,256]{2,1,0:T(8,128)(2,1)S(1)}, u32[]{:S(2)}, u32[]{:S(2)}) %collective-permute-start.8) | collective-permute-done | bytes 65568 | tf_op jit(solution)/shard_map/ppermute | solution.py:384
  47.3 1.1 %transform_x_last.1 = bf16[2,512,256]{2,1,0:T(8,128)(2,1)} custom-call(bf16[2,512,256]{2,1,0:T(8,128)(2,1)S(1)} %get-tuple-element.20.table_ref, bf16[2,64,256]{2,1,0:T(8,128)(2,1)S(1)} %get-tuple-element.24.refs_0_, bf16[2,64,256]{2,1,0:T(8,128)(2,1)S(1)} %collective-permute-done.7.refs_1_, bf16[2,64,256]{2,1,0:T(8,128)(2,1)S(1)} %collective-permute-done.8.refs_2_, ...), custom_call_target="tpu_custom_call" | custom-call | flops 268435456 | bytes 4194304 | tf_op jit(solution)/shard_map/transform_x_last/pallas_call | solution.py:342
  (25 shorter events, 1.6 us)
Async XLA Ops:
  0.0 11.3 %collective-permute-start = (bf16[2,128,1024]{2,1,0:T(8,128)(2,1)}, bf16[2,128,1024]{2,1,0:T(8,128)(2,1)S(1)}, u32[]{:S(2)}, u32[]{:S(2)}) collective-permute-start(bf16[2,128,1024]{2,1,0:T(8,128)(2,1)} %bitcast.6), channel_id=1, source_target_pairs={{0,4},{4,0},{8,12},{12,8},{16,20},{20,16},{24,28},{28,24},{1,5},{5... | collective-permute-start | bytes 1572872 | tf_op jit(solution)/shard_map/ppermute | solution.py:363
  1.5 6.9 %collective-permute-start.12 = (bf16[2,64,1024]{2,1,0:T(8,128)(2,1)S(1)}, bf16[2,64,1024]{2,1,0:T(8,128)(2,1)S(1)}, u32[]{:S(2)}, u32[]{:S(2)}) collective-permute-start(bf16[2,64,1024]{2,1,0:T(8,128)(2,1)S(1)} %get-tuple-element.29.refs_0_), channel_id=1, source_target_pairs={{0,8},{4,20},{8,0},{12,28},{16,24},{20,4},{24,16},{28,12},{1,9},{5... | collective-permute-start | bytes 786440 | tf_op jit(solution)/shard_map/ppermute | solution.py:363
  4.1 7.2 %collective-permute-start.3 = (bf16[2,64,1024]{2,1,0:T(8,128)(2,1)S(1)}, bf16[2,64,1024]{2,1,0:T(8,128)(2,1)S(1)}, u32[]{:S(2)}, u32[]{:S(2)}) collective-permute-start(bf16[2,64,1024]{2,1,0:T(8,128)(2,1)S(1)} %get-tuple-element.22.refs_0_), channel_id=1, source_target_pairs={{0,8},{4,20},{8,0},{12,28},{16,24},{20,4},{24,16},{28,12},{1,9},{5... | collective-permute-start | bytes 786440 | tf_op jit(solution)/shard_map/ppermute | solution.py:363
  8.4 4.9 %collective-permute-start.13 = (bf16[2,64,1024]{2,1,0:T(8,128)(2,1)S(1)}, bf16[2,64,1024]{2,1,0:T(8,128)(2,1)S(1)}, u32[]{:S(2)}, u32[]{:S(2)}) collective-permute-start(bf16[2,64,1024]{2,1,0:T(8,128)(2,1)S(1)} %collective-permute-done.12.refs_2_), channel_id=1, source_target_pairs={{0,4},{4,0},{8,12},{12,8},{16,20},{20,16},{24,28},{28,24},{1,5},{5... | collective-permute-start | bytes 786440 | tf_op jit(solution)/shard_map/ppermute | solution.py:363
  11.3 4.2 %collective-permute-start.4 = (bf16[2,64,1024]{2,1,0:T(8,128)(2,1)S(1)}, bf16[2,64,1024]{2,1,0:T(8,128)(2,1)S(1)}, u32[]{:S(2)}, u32[]{:S(2)}) collective-permute-start(bf16[2,64,1024]{2,1,0:T(8,128)(2,1)S(1)} %collective-permute-done.3.refs_2_), channel_id=1, source_target_pairs={{0,4},{4,0},{8,12},{12,8},{16,20},{20,16},{24,28},{28,24},{1,5},{5... | collective-permute-start | bytes 786440 | tf_op jit(solution)/shard_map/ppermute | solution.py:363
  11.3 6.4 %collective-permute-start.10 = (bf16[2,64,1024]{2,1,0:T(8,128)(2,1)S(1)}, bf16[2,64,1024]{2,1,0:T(8,128)(2,1)S(1)}, u32[]{:S(2)}, u32[]{:S(2)}) collective-permute-start(bf16[2,64,1024]{2,1,0:T(8,128)(2,1)S(1)} %get-tuple-element.35), channel_id=1, source_target_pairs={{0,8},{4,20},{8,0},{12,28},{16,24},{20,4},{24,16},{28,12},{1,9},{5... | collective-permute-start | bytes 786440 | tf_op jit(solution)/shard_map/ppermute | solution.py:363
  13.4 7.2 %collective-permute-start.14 = (bf16[2,64,1024]{2,1,0:T(8,128)(2,1)S(1)}, bf16[2,64,1024]{2,1,0:T(8,128)(2,1)S(1)}, u32[]{:S(2)}, u32[]{:S(2)}) collective-permute-start(bf16[2,64,1024]{2,1,0:T(8,128)(2,1)S(1)} %collective-permute-done.13.refs_3_), channel_id=1, source_target_pairs={{0,8},{4,20},{8,0},{12,28},{16,24},{20,4},{24,16},{28,12},{1,9},{5... | collective-permute-start | bytes 786440 | tf_op jit(solution)/shard_map/ppermute | solution.py:363
  13.5 9.9 %collective-permute-start.1 = (bf16[2,64,1024]{2,1,0:T(8,128)(2,1)S(1)}, bf16[2,64,1024]{2,1,0:T(8,128)(2,1)S(1)}, u32[]{:S(2)}, u32[]{:S(2)}) collective-permute-start(bf16[2,64,1024]{2,1,0:T(8,128)(2,1)S(1)} %get-tuple-element.36), channel_id=1, source_target_pairs={{0,8},{4,20},{8,0},{12,28},{16,24},{20,4},{24,16},{28,12},{1,9},{5... | collective-permute-start | bytes 786440 | tf_op jit(solution)/shard_map/ppermute | solution.py:363
  15.4 10.7 %collective-permute-start.5 = (bf16[2,64,1024]{2,1,0:T(8,128)(2,1)S(1)}, bf16[2,64,1024]{2,1,0:T(8,128)(2,1)S(1)}, u32[]{:S(2)}, u32[]{:S(2)}) collective-permute-start(bf16[2,64,1024]{2,1,0:T(8,128)(2,1)S(1)} %collective-permute-done.4.refs_3_), channel_id=1, source_target_pairs={{0,8},{4,20},{8,0},{12,28},{16,24},{20,4},{24,16},{28,12},{1,9},{5... | collective-permute-start | bytes 786440 | tf_op jit(solution)/shard_map/ppermute | solution.py:363
  17.7 12.2 %collective-permute-start.11 = (bf16[2,64,1024]{2,1,0:T(8,128)(2,1)S(1)}, bf16[2,64,1024]{2,1,0:T(8,128)(2,1)S(1)}, u32[]{:S(2)}, u32[]{:S(2)}) collective-permute-start(bf16[2,64,1024]{2,1,0:T(8,128)(2,1)S(1)} %collective-permute-done.10.refs_4_), channel_id=1, source_target_pairs={{0,4},{4,0},{8,12},{12,8},{16,20},{20,16},{24,28},{28,24},{1,5},{5... | collective-permute-start | bytes 786440 | tf_op jit(solution)/shard_map/ppermute | solution.py:363
  20.5 9.6 %collective-permute-start.15 = (bf16[2,64,1024]{2,1,0:T(8,128)(2,1)S(1)}, bf16[2,64,1024]{2,1,0:T(8,128)(2,1)S(1)}, u32[]{:S(2)}, u32[]{:S(2)}) collective-permute-start(bf16[2,64,1024]{2,1,0:T(8,128)(2,1)S(1)} %collective-permute-done.14.refs_1_), channel_id=1, source_target_pairs={{0,4},{4,0},{8,12},{12,8},{16,20},{20,16},{24,28},{28,24},{1,5},{5... | collective-permute-start | bytes 786440 | tf_op jit(solution)/shard_map/ppermute | solution.py:363
  23.4 14.6 %collective-permute-start.2 = (bf16[2,64,1024]{2,1,0:T(8,128)(2,1)S(1)}, bf16[2,64,1024]{2,1,0:T(8,128)(2,1)S(1)}, u32[]{:S(2)}, u32[]{:S(2)}) collective-permute-start(bf16[2,64,1024]{2,1,0:T(8,128)(2,1)S(1)} %collective-permute-done.1.refs_4_), channel_id=1, source_target_pairs={{0,4},{4,0},{8,12},{12,8},{16,20},{20,16},{24,28},{28,24},{1,5},{5... | collective-permute-start | bytes 786440 | tf_op jit(solution)/shard_map/ppermute | solution.py:363
  26.2 12.0 %collective-permute-start.6 = (bf16[2,64,1024]{2,1,0:T(8,128)(2,1)S(1)}, bf16[2,64,1024]{2,1,0:T(8,128)(2,1)S(1)}, u32[]{:S(2)}, u32[]{:S(2)}) collective-permute-start(bf16[2,64,1024]{2,1,0:T(8,128)(2,1)S(1)} %collective-permute-done.5.refs_1_), channel_id=1, source_target_pairs={{0,4},{4,0},{8,12},{12,8},{16,20},{20,16},{24,28},{28,24},{1,5},{5... | collective-permute-start | bytes 786440 | tf_op jit(solution)/shard_map/ppermute | solution.py:363
  31.1 9.1 %collective-permute-start.16 = (bf16[2,64,256]{2,1,0:T(8,128)(2,1)S(1)}, bf16[2,64,256]{2,1,0:T(8,128)(2,1)S(1)}, u32[]{:S(2)}, u32[]{:S(2)}) collective-permute-start(bf16[2,64,256]{2,1,0:T(8,128)(2,1)S(1)} %get-tuple-element.31), channel_id=1, source_target_pairs={{0,1},{1,2},{2,3},{3,0},{4,5},{5,6},{6,7},{7,4},{8,9},{9,10},{10,1... | collective-permute-start | bytes 196616 | tf_op jit(solution)/shard_map/ppermute | solution.py:384
  33.9 9.0 %collective-permute-start.17 = (bf16[2,64,256]{2,1,0:T(8,128)(2,1)S(1)}, bf16[2,64,256]{2,1,0:T(8,128)(2,1)S(1)}, u32[]{:S(2)}, u32[]{:S(2)}) collective-permute-start(bf16[2,64,256]{2,1,0:T(8,128)(2,1)S(1)} %get-tuple-element.32), channel_id=1, source_target_pairs={{0,2},{1,3},{2,0},{3,1},{4,7},{5,4},{6,5},{7,6},{8,10},{9,11},{10,... | collective-permute-start | bytes 196616 | tf_op jit(solution)/shard_map/ppermute | solution.py:384
  36.6 6.4 %collective-permute-start.18 = (bf16[2,64,256]{2,1,0:T(8,128)(2,1)S(1)}, bf16[2,64,256]{2,1,0:T(8,128)(2,1)S(1)}, u32[]{:S(2)}, u32[]{:S(2)}) collective-permute-start(bf16[2,64,256]{2,1,0:T(8,128)(2,1)S(1)} %get-tuple-element.33), channel_id=1, source_target_pairs={{0,3},{1,0},{2,1},{3,2},{4,6},{5,7},{6,4},{7,5},{8,11},{9,8},{10,9... | collective-permute-start | bytes 196616 | tf_op jit(solution)/shard_map/ppermute | solution.py:384
  39.1 6.3 %collective-permute-start.7 = (bf16[2,64,256]{2,1,0:T(8,128)(2,1)S(1)}, bf16[2,64,256]{2,1,0:T(8,128)(2,1)S(1)}, u32[]{:S(2)}, u32[]{:S(2)}) collective-permute-start(bf16[2,64,256]{2,1,0:T(8,128)(2,1)S(1)} %get-tuple-element.25), channel_id=1, source_target_pairs={{0,1},{1,2},{2,3},{3,0},{4,5},{5,6},{6,7},{7,4},{8,9},{9,10},{10,1... | collective-permute-start | bytes 196616 | tf_op jit(solution)/shard_map/ppermute | solution.py:384
  39.8 7.5 %collective-permute-start.8 = (bf16[2,64,256]{2,1,0:T(8,128)(2,1)S(1)}, bf16[2,64,256]{2,1,0:T(8,128)(2,1)S(1)}, u32[]{:S(2)}, u32[]{:S(2)}) collective-permute-start(bf16[2,64,256]{2,1,0:T(8,128)(2,1)S(1)} %get-tuple-element.26), channel_id=1, source_target_pairs={{0,2},{1,3},{2,0},{3,1},{4,7},{5,4},{6,5},{7,6},{8,10},{9,11},{10,... | collective-permute-start | bytes 196616 | tf_op jit(solution)/shard_map/ppermute | solution.py:384
  40.1 7.2 %collective-permute-start.9 = (bf16[2,64,256]{2,1,0:T(8,128)(2,1)S(1)}, bf16[2,64,256]{2,1,0:T(8,128)(2,1)S(1)}, u32[]{:S(2)}, u32[]{:S(2)}) collective-permute-start(bf16[2,64,256]{2,1,0:T(8,128)(2,1)S(1)} %get-tuple-element.27), channel_id=1, source_target_pairs={{0,3},{1,0},{2,1},{3,2},{4,6},{5,7},{6,4},{7,5},{8,11},{9,8},{10,9... | collective-permute-start | bytes 196616 | tf_op jit(solution)/shard_map/ppermute | solution.py:384

commit v4 on v3

--- a/solution.py
+++ b/solution.py
@@ -239,8 +239,8 @@
         @pl.loop(0, size // ROWS)
         def _(step):
             row = pl.ds(pl.multiple_of(step * ROWS, ROWS), ROWS)
-            for left in range(0, ny, 256):
-                cols = pl.ds(left, 256)
+            for left in range(0, ny, 128):
+                cols = pl.ds(left, 128)
                 begun = (None, None) if total is None else (ins[-1][0, row, cols], ins[-1][1, row, cols])
                 total_ref[0, row, cols], total_ref[1, row, cols] = add_sources(
                     begun, green_ref, given, step, start, cols
@@ -264,14 +264,14 @@
         def _(step):
             row = pl.ds(pl.multiple_of(step * ROWS, ROWS), ROWS)
             low = pl.ds(pl.multiple_of(size + step * ROWS, ROWS), ROWS)
-            for left in range(0, ny, 256):
-                cols = pl.ds(left, 256)
+            for left in range(0, ny, 128):
+                cols = pl.ds(left, 128)
                 begun = total_ref[0, row, cols], total_ref[1, row, cols]
                 real, imag = add_sources(begun, green_ref, given, step, start, cols)
-                left_ref[row, pl.ds(left, 256)] = real.astype(BF16)
-                left_ref[row, pl.ds(ny + left, 256)] = (-imag).astype(BF16)
-                left_ref[low, pl.ds(left, 256)] = imag.astype(BF16)
-                left_ref[low, pl.ds(ny + left, 256)] = real.astype(BF16)
+                left_ref[row, pl.ds(left, 128)] = real.astype(BF16)
+                left_ref[row, pl.ds(ny + left, 128)] = (-imag).astype(BF16)
+                left_ref[low, pl.ds(left, 128)] = imag.astype(BF16)
+                left_ref[low, pl.ds(ny + left, 128)] = real.astype(BF16)
 
         for m, out_ref in enumerate(outs):
             cols = pl.ds(m * wide, wide)

time: 48.6 us -> 48.6 us (level)
  no operation moved by 1% of the time
where the time goes in v4:
time: 48.6 us; the launch traced here: 48.5 us
  waiting for transfers between devices  21.7 us (45%)
  starting transfers between devices  17.3 us (36%)
  Pallas kernels  9.26 us (19%)
    ppermute x13, waiting for transfers between devices, send(): return lax.ppermute(v, 'depth', route)  17.7 us
    ppermute x6, starting transfers between devices, hop(): return lax.ppermute(v, ('depth', 'kslab'), pairs)  10 us
    ppermute x13, starting transfers between devices, send(): return lax.ppermute(v, 'depth', route)  7.33 us
    pallas_call x7, Pallas kernels, call(): pl.pallas_call(body, out_shape=[pltpu.VMEM(o.shape, o.dtype) for o in out...  4.06 us
    ppermute x6, waiting for transfers between devices, hop(): return lax.ppermute(v, ('depth', 'kslab'), pairs)  3.95 us
    pallas_call x1, Pallas kernels, prepare(): pl.pallas_call(body, out_shape=[pltpu.VMEM(o.shape, o.dtype) for o in out...  3.02 us
    pallas_call x1, Pallas kernels, transform_x(): pl.pallas_call(last_body, out_shape=struct((2, nx, wide), BF16), in_specs...  1.14 us
    pallas_call x1, Pallas kernels, split_rows(): pl.pallas_call(body, out_shape=[pltpu.VMEM((planes, size, ny), own.dtype)...  1.04 us
  transfers between devices with their start and end apart: 19, of which 8 were waited for; matrix products, arithmetic and copies ran while one was open for 0% of the time, Pallas kernels for 17%

profile of v4, /device:TPU:0, one launch (start us, length us, event | category | flops | bytes accessed | tf_op | source)
XLA Modules:
  0.0 48.5 jit_solution(14094238570177480489)
XLA Ops:
  0.0 0.5 %collective-permute-start = (bf16[2,128,1024]{2,1,0:T(8,128)(2,1)}, bf16[2,128,1024]{2,1,0:T(8,128)(2,1)S(1)}, u32[]{:S(2)}, u32[]{:S(2)}) collective-permute-start(bf16[2,128,1024]{2,1,0:T(8,128)(2,1)} %bitcast.6), channel_id=1, source_target_pairs={{0,4},{4,0},{8,12},{12,8},{16,20},{20,16},{24,28},{28,24},{1,5},{5... | collective-permute-start | bytes 1572872 | tf_op jit(solution)/shard_map/ppermute | solution.py:363
  0.5 1.0 %split_rows.1 = (bf16[2,64,1024]{2,1,0:T(8,128)(2,1)S(1)}, bf16[2,64,1024]{2,1,0:T(8,128)(2,1)S(1)}) custom-call(bf16[2,128,1024]{2,1,0:T(8,128)(2,1)} %bitcast.7), custom_call_target="tpu_custom_call" | custom-call | bytes 1048576 | tf_op jit(solution)/shard_map/split_rows/pallas_call | solution.py:129
  1.5 2.5 %collective-permute-start.12 = (bf16[2,64,1024]{2,1,0:T(8,128)(2,1)S(1)}, bf16[2,64,1024]{2,1,0:T(8,128)(2,1)S(1)}, u32[]{:S(2)}, u32[]{:S(2)}) collective-permute-start(bf16[2,64,1024]{2,1,0:T(8,128)(2,1)S(1)} %get-tuple-element.29.refs_0_), channel_id=1, source_target_pairs={{0,8},{4,20},{8,0},{12,28},{16,24},{20,4},{24,16},{28,12},{1,9},{5... | collective-permute-start | bytes 786440 | tf_op jit(solution)/shard_map/ppermute | solution.py:363
  4.2 4.3 %collective-permute-done.12.refs_2_ = bf16[2,64,1024]{2,1,0:T(8,128)(2,1)S(1)} collective-permute-done((bf16[2,64,1024]{2,1,0:T(8,128)(2,1)S(1)}, bf16[2,64,1024]{2,1,0:T(8,128)(2,1)S(1)}, u32[]{:S(2)}, u32[]{:S(2)}) %collective-permute-start.12) | collective-permute-done | bytes 262176 | tf_op jit(solution)/shard_map/ppermute | solution.py:363
  8.4 2.8 %collective-permute-done.3.refs_2_ = bf16[2,64,1024]{2,1,0:T(8,128)(2,1)S(1)} collective-permute-done((bf16[2,64,1024]{2,1,0:T(8,128)(2,1)S(1)}, bf16[2,64,1024]{2,1,0:T(8,128)(2,1)S(1)}, u32[]{:S(2)}, u32[]{:S(2)}) %collective-permute-start.3) | collective-permute-done | bytes 262176 | tf_op jit(solution)/shard_map/ppermute | solution.py:363
  11.3 2.1 %collective-permute-start.10 = (bf16[2,64,1024]{2,1,0:T(8,128)(2,1)S(1)}, bf16[2,64,1024]{2,1,0:T(8,128)(2,1)S(1)}, u32[]{:S(2)}, u32[]{:S(2)}) collective-permute-start(bf16[2,64,1024]{2,1,0:T(8,128)(2,1)S(1)} %get-tuple-element.35), channel_id=1, source_target_pairs={{0,8},{4,20},{8,0},{12,28},{16,24},{20,4},{24,16},{28,12},{1,9},{5... | collective-permute-start | bytes 786440 | tf_op jit(solution)/shard_map/ppermute | solution.py:363
  13.5 1.9 %collective-permute-start.1 = (bf16[2,64,1024]{2,1,0:T(8,128)(2,1)S(1)}, bf16[2,64,1024]{2,1,0:T(8,128)(2,1)S(1)}, u32[]{:S(2)}, u32[]{:S(2)}) collective-permute-start(bf16[2,64,1024]{2,1,0:T(8,128)(2,1)S(1)} %get-tuple-element.36), channel_id=1, source_target_pairs={{0,8},{4,20},{8,0},{12,28},{16,24},{20,4},{24,16},{28,12},{1,9},{5... | collective-permute-start | bytes 786440 | tf_op jit(solution)/shard_map/ppermute | solution.py:363
  15.5 2.2 %collective-permute-done.10.refs_4_ = bf16[2,64,1024]{2,1,0:T(8,128)(2,1)S(1)} collective-permute-done((bf16[2,64,1024]{2,1,0:T(8,128)(2,1)S(1)}, bf16[2,64,1024]{2,1,0:T(8,128)(2,1)S(1)}, u32[]{:S(2)}, u32[]{:S(2)}) %collective-permute-start.10) | collective-permute-done | bytes 262176 | tf_op jit(solution)/shard_map/ppermute | solution.py:363
  17.7 2.8 %collective-permute-done.14.refs_1_ = bf16[2,64,1024]{2,1,0:T(8,128)(2,1)S(1)} collective-permute-done((bf16[2,64,1024]{2,1,0:T(8,128)(2,1)S(1)}, bf16[2,64,1024]{2,1,0:T(8,128)(2,1)S(1)}, u32[]{:S(2)}, u32[]{:S(2)}) %collective-permute-start.14) | collective-permute-done | bytes 262176 | tf_op jit(solution)/shard_map/ppermute | solution.py:363
  20.5 2.8 %collective-permute-done.1.refs_4_ = bf16[2,64,1024]{2,1,0:T(8,128)(2,1)S(1)} collective-permute-done((bf16[2,64,1024]{2,1,0:T(8,128)(2,1)S(1)}, bf16[2,64,1024]{2,1,0:T(8,128)(2,1)S(1)}, u32[]{:S(2)}, u32[]{:S(2)}) %collective-permute-start.1) | collective-permute-done | bytes 262176 | tf_op jit(solution)/shard_map/ppermute | solution.py:363
  23.4 2.8 %collective-permute-done.5.refs_1_ = bf16[2,64,1024]{2,1,0:T(8,128)(2,1)S(1)} collective-permute-done((bf16[2,64,1024]{2,1,0:T(8,128)(2,1)S(1)}, bf16[2,64,1024]{2,1,0:T(8,128)(2,1)S(1)}, u32[]{:S(2)}, u32[]{:S(2)}) %collective-permute-start.5) | collective-permute-done | bytes 262176 | tf_op jit(solution)/shard_map/ppermute | solution.py:363
  26.2 3.0 %prepare.1 = (bf16[2,1024,1024]{2,1,0:T(8,128)(2,1)S(1)}, bf16[2,512,256]{2,1,0:T(8,128)(2,1)S(1)}, bf16[2,512,256]{2,1,0:T(8,128)(2,1)S(1)}, bf16[8,2,128,1024]{3,2,1,0:T(8,128)(2,1)S(1)}, f32[512,256]{1,0:T(8,128)S(1)}) custom-call(bf16[8,2,128,1024]{3,2,1,0:T(8,128)(2,1)} %bitcast.4, f32[512,256]{1,0:T(8,128)} %bitcast.5), custom_call_target="tpu_custom_call" | custom-call | flops 8388608 | bytes 8388608 | tf_op jit(solution)/shard_map/prepare/pallas_call | solution.py:192
  29.2 0.7 %shard_map.40.refs_2_ = f32[2,64,1024]{2,1,0:T(8,128)S(1)} custom-call(bf16[8,2,128,1024]{3,2,1,0:T(8,128)(2,1)S(1)} %get-tuple-element.21.green_ref, bf16[2,64,1024]{2,1,0:T(8,128)(2,1)S(1)} %get-tuple-element.29.refs_0_, bf16[2,128,1024]{2,1,0:T(8,128)(2,1)S(1)} %collective-permute-done.refs_1_, bf16[2,64,1024]{2,1,0:T(8,128)(2,1)S(1)} %collective-permute-done.12.refs_2_, ...), custom_call_target="tpu_custom_call" | custom-call | flops 2621440 | bytes 6291456 | tf_op jit(solution)/shard_map/pallas_call | solution.py:65
  30.2 0.9 %shard_map.42 = (bf16[2,64,256]{2,1,0:T(8,128)(2,1)S(1)}, bf16[2,64,256]{2,1,0:T(8,128)(2,1)S(1)}, bf16[2,64,256]{2,1,0:T(8,128)(2,1)S(1)}, bf16[2,64,256]{2,1,0:T(8,128)(2,1)S(1)}) custom-call(bf16[8,2,128,1024]{3,2,1,0:T(8,128)(2,1)S(1)} %get-tuple-element.21.green_ref, f32[2,64,1024]{2,1,0:T(8,128)S(1)} %shard_map.41.total_ref, ...), custom_call_target="tpu_custom_call" | custom-call | flops 536870912 | bytes 9437184 | tf_op jit(solution)/shard_map/pallas_call | solution.py:65
  31.1 2.2 %collective-permute-start.16 = (bf16[2,64,256]{2,1,0:T(8,128)(2,1)S(1)}, bf16[2,64,256]{2,1,0:T(8,128)(2,1)S(1)}, u32[]{:S(2)}, u32[]{:S(2)}) collective-permute-start(bf16[2,64,256]{2,1,0:T(8,128)(2,1)S(1)} %get-tuple-element.31), channel_id=1, source_target_pairs={{0,1},{1,2},{2,3},{3,0},{4,5},{5,6},{6,7},{7,4},{8,9},{9,10},{10,1... | collective-permute-start | bytes 196616 | tf_op jit(solution)/shard_map/ppermute | solution.py:384
  33.2 0.7 %shard_map.37.refs_2_ = f32[2,64,1024]{2,1,0:T(8,128)S(1)} custom-call(bf16[8,2,128,1024]{3,2,1,0:T(8,128)(2,1)S(1)} %get-tuple-element.21.green_ref, bf16[2,64,1024]{2,1,0:T(8,128)(2,1)S(1)} %get-tuple-element.22.refs_0_, bf16[2,128,1024]{2,1,0:T(8,128)(2,1)S(1)} %collective-permute-done.refs_1_, bf16[2,64,1024]{2,1,0:T(8,128)(2,1)S(1)} %collective-permute-done.3.refs_2_, ...), custom_call_target="tpu_custom_call" | custom-call | flops 2621440 | bytes 6291456 | tf_op jit(solution)/shard_map/pallas_call | solution.py:65
  33.9 2.6 %collective-permute-start.17 = (bf16[2,64,256]{2,1,0:T(8,128)(2,1)S(1)}, bf16[2,64,256]{2,1,0:T(8,128)(2,1)S(1)}, u32[]{:S(2)}, u32[]{:S(2)}) collective-permute-start(bf16[2,64,256]{2,1,0:T(8,128)(2,1)S(1)} %get-tuple-element.32), channel_id=1, source_target_pairs={{0,2},{1,3},{2,0},{3,1},{4,7},{5,4},{6,5},{7,6},{8,10},{9,11},{10,... | collective-permute-start | bytes 196616 | tf_op jit(solution)/shard_map/ppermute | solution.py:384
  36.5 1.3 %collective-permute-start.18 = (bf16[2,64,256]{2,1,0:T(8,128)(2,1)S(1)}, bf16[2,64,256]{2,1,0:T(8,128)(2,1)S(1)}, u32[]{:S(2)}, u32[]{:S(2)}) collective-permute-start(bf16[2,64,256]{2,1,0:T(8,128)(2,1)S(1)} %get-tuple-element.33), channel_id=1, source_target_pairs={{0,3},{1,0},{2,1},{3,2},{4,6},{5,7},{6,4},{7,5},{8,11},{9,8},{10,9... | collective-permute-start | bytes 196616 | tf_op jit(solution)/shard_map/ppermute | solution.py:384
  38.1 0.9 %shard_map.39 = (bf16[2,64,256]{2,1,0:T(8,128)(2,1)S(1)}, bf16[2,64,256]{2,1,0:T(8,128)(2,1)S(1)}, bf16[2,64,256]{2,1,0:T(8,128)(2,1)S(1)}, bf16[2,64,256]{2,1,0:T(8,128)(2,1)S(1)}) custom-call(bf16[8,2,128,1024]{3,2,1,0:T(8,128)(2,1)S(1)} %get-tuple-element.21.green_ref, f32[2,64,1024]{2,1,0:T(8,128)S(1)} %shard_map.38.total_ref, ...), custom_call_target="tpu_custom_call" | custom-call | flops 536870912 | bytes 9437184 | tf_op jit(solution)/shard_map/pallas_call | solution.py:65
  39.0 0.7 %collective-permute-start.7 = (bf16[2,64,256]{2,1,0:T(8,128)(2,1)S(1)}, bf16[2,64,256]{2,1,0:T(8,128)(2,1)S(1)}, u32[]{:S(2)}, u32[]{:S(2)}) collective-permute-start(bf16[2,64,256]{2,1,0:T(8,128)(2,1)S(1)} %get-tuple-element.25), channel_id=1, source_target_pairs={{0,1},{1,2},{2,3},{3,0},{4,5},{5,6},{6,7},{7,4},{8,9},{9,10},{10,1... | collective-permute-start | bytes 196616 | tf_op jit(solution)/shard_map/ppermute | solution.py:384
  40.1 2.8 %collective-permute-start.9 = (bf16[2,64,256]{2,1,0:T(8,128)(2,1)S(1)}, bf16[2,64,256]{2,1,0:T(8,128)(2,1)S(1)}, u32[]{:S(2)}, u32[]{:S(2)}) collective-permute-start(bf16[2,64,256]{2,1,0:T(8,128)(2,1)S(1)} %get-tuple-element.27), channel_id=1, source_target_pairs={{0,3},{1,0},{2,1},{3,2},{4,6},{5,7},{6,4},{7,5},{8,11},{9,8},{10,9... | collective-permute-start | bytes 196616 | tf_op jit(solution)/shard_map/ppermute | solution.py:384
  43.4 2.0 %collective-permute-done.7.refs_1_ = bf16[2,64,256]{2,1,0:T(8,128)(2,1)S(1)} collective-permute-done((bf16[2,64,256]{2,1,0:T(8,128)(2,1)S(1)}, bf16[2,64,256]{2,1,0:T(8,128)(2,1)S(1)}, u32[]{:S(2)}, u32[]{:S(2)}) %collective-permute-start.7) | collective-permute-done | bytes 65568 | tf_op jit(solution)/shard_map/ppermute | solution.py:384
  45.4 1.9 %collective-permute-done.8.refs_2_ = bf16[2,64,256]{2,1,0:T(8,128)(2,1)S(1)} collective-permute-done((bf16[2,64,256]{2,1,0:T(8,128)(2,1)S(1)}, bf16[2,64,256]{2,1,0:T(8,128)(2,1)S(1)}, u32[]{:S(2)}, u32[]{:S(2)}) %collective-permute-start.8) | collective-permute-done | bytes 65568 | tf_op jit(solution)/shard_map/ppermute | solution.py:384
  47.3 1.1 %transform_x_last.1 = bf16[2,512,256]{2,1,0:T(8,128)(2,1)} custom-call(bf16[2,512,256]{2,1,0:T(8,128)(2,1)S(1)} %get-tuple-element.20.table_ref, bf16[2,64,256]{2,1,0:T(8,128)(2,1)S(1)} %get-tuple-element.24.refs_0_, bf16[2,64,256]{2,1,0:T(8,128)(2,1)S(1)} %collective-permute-done.7.refs_1_, bf16[2,64,256]{2,1,0:T(8,128)(2,1)S(1)} %collective-permute-done.8.refs_2_, ...), custom_call_target="tpu_custom_call" | custom-call | flops 268435456 | bytes 4194304 | tf_op jit(solution)/shard_map/transform_x_last/pallas_call | solution.py:342
  (25 shorter events, 1.6 us)
Async XLA Ops:
  0.0 11.3 %collective-permute-start = (bf16[2,128,1024]{2,1,0:T(8,128)(2,1)}, bf16[2,128,1024]{2,1,0:T(8,128)(2,1)S(1)}, u32[]{:S(2)}, u32[]{:S(2)}) collective-permute-start(bf16[2,128,1024]{2,1,0:T(8,128)(2,1)} %bitcast.6), channel_id=1, source_target_pairs={{0,4},{4,0},{8,12},{12,8},{16,20},{20,16},{24,28},{28,24},{1,5},{5... | collective-permute-start | bytes 1572872 | tf_op jit(solution)/shard_map/ppermute | solution.py:363
  1.5 6.9 %collective-permute-start.12 = (bf16[2,64,1024]{2,1,0:T(8,128)(2,1)S(1)}, bf16[2,64,1024]{2,1,0:T(8,128)(2,1)S(1)}, u32[]{:S(2)}, u32[]{:S(2)}) collective-permute-start(bf16[2,64,1024]{2,1,0:T(8,128)(2,1)S(1)} %get-tuple-element.29.refs_0_), channel_id=1, source_target_pairs={{0,8},{4,20},{8,0},{12,28},{16,24},{20,4},{24,16},{28,12},{1,9},{5... | collective-permute-start | bytes 786440 | tf_op jit(solution)/shard_map/ppermute | solution.py:363
  4.1 7.2 %collective-permute-start.3 = (bf16[2,64,1024]{2,1,0:T(8,128)(2,1)S(1)}, bf16[2,64,1024]{2,1,0:T(8,128)(2,1)S(1)}, u32[]{:S(2)}, u32[]{:S(2)}) collective-permute-start(bf16[2,64,1024]{2,1,0:T(8,128)(2,1)S(1)} %get-tuple-element.22.refs_0_), channel_id=1, source_target_pairs={{0,8},{4,20},{8,0},{12,28},{16,24},{20,4},{24,16},{28,12},{1,9},{5... | collective-permute-start | bytes 786440 | tf_op jit(solution)/shard_map/ppermute | solution.py:363
  8.4 4.9 %collective-permute-start.13 = (bf16[2,64,1024]{2,1,0:T(8,128)(2,1)S(1)}, bf16[2,64,1024]{2,1,0:T(8,128)(2,1)S(1)}, u32[]{:S(2)}, u32[]{:S(2)}) collective-permute-start(bf16[2,64,1024]{2,1,0:T(8,128)(2,1)S(1)} %collective-permute-done.12.refs_2_), channel_id=1, source_target_pairs={{0,4},{4,0},{8,12},{12,8},{16,20},{20,16},{24,28},{28,24},{1,5},{5... | collective-permute-start | bytes 786440 | tf_op jit(solution)/shard_map/ppermute | solution.py:363
  11.3 4.2 %collective-permute-start.4 = (bf16[2,64,1024]{2,1,0:T(8,128)(2,1)S(1)}, bf16[2,64,1024]{2,1,0:T(8,128)(2,1)S(1)}, u32[]{:S(2)}, u32[]{:S(2)}) collective-permute-start(bf16[2,64,1024]{2,1,0:T(8,128)(2,1)S(1)} %collective-permute-done.3.refs_2_), channel_id=1, source_target_pairs={{0,4},{4,0},{8,12},{12,8},{16,20},{20,16},{24,28},{28,24},{1,5},{5... | collective-permute-start | bytes 786440 | tf_op jit(solution)/shard_map/ppermute | solution.py:363
  11.3 6.4 %collective-permute-start.10 = (bf16[2,64,1024]{2,1,0:T(8,128)(2,1)S(1)}, bf16[2,64,1024]{2,1,0:T(8,128)(2,1)S(1)}, u32[]{:S(2)}, u32[]{:S(2)}) collective-permute-start(bf16[2,64,1024]{2,1,0:T(8,128)(2,1)S(1)} %get-tuple-element.35), channel_id=1, source_target_pairs={{0,8},{4,20},{8,0},{12,28},{16,24},{20,4},{24,16},{28,12},{1,9},{5... | collective-permute-start | bytes 786440 | tf_op jit(solution)/shard_map/ppermute | solution.py:363
  13.4 7.2 %collective-permute-start.14 = (bf16[2,64,1024]{2,1,0:T(8,128)(2,1)S(1)}, bf16[2,64,1024]{2,1,0:T(8,128)(2,1)S(1)}, u32[]{:S(2)}, u32[]{:S(2)}) collective-permute-start(bf16[2,64,1024]{2,1,0:T(8,128)(2,1)S(1)} %collective-permute-done.13.refs_3_), channel_id=1, source_target_pairs={{0,8},{4,20},{8,0},{12,28},{16,24},{20,4},{24,16},{28,12},{1,9},{5... | collective-permute-start | bytes 786440 | tf_op jit(solution)/shard_map/ppermute | solution.py:363
  13.5 9.9 %collective-permute-start.1 = (bf16[2,64,1024]{2,1,0:T(8,128)(2,1)S(1)}, bf16[2,64,1024]{2,1,0:T(8,128)(2,1)S(1)}, u32[]{:S(2)}, u32[]{:S(2)}) collective-permute-start(bf16[2,64,1024]{2,1,0:T(8,128)(2,1)S(1)} %get-tuple-element.36), channel_id=1, source_target_pairs={{0,8},{4,20},{8,0},{12,28},{16,24},{20,4},{24,16},{28,12},{1,9},{5... | collective-permute-start | bytes 786440 | tf_op jit(solution)/shard_map/ppermute | solution.py:363
  15.4 10.7 %collective-permute-start.5 = (bf16[2,64,1024]{2,1,0:T(8,128)(2,1)S(1)}, bf16[2,64,1024]{2,1,0:T(8,128)(2,1)S(1)}, u32[]{:S(2)}, u32[]{:S(2)}) collective-permute-start(bf16[2,64,1024]{2,1,0:T(8,128)(2,1)S(1)} %collective-permute-done.4.refs_3_), channel_id=1, source_target_pairs={{0,8},{4,20},{8,0},{12,28},{16,24},{20,4},{24,16},{28,12},{1,9},{5... | collective-permute-start | bytes 786440 | tf_op jit(solution)/shard_map/ppermute | solution.py:363
  17.7 12.2 %collective-permute-start.11 = (bf16[2,64,1024]{2,1,0:T(8,128)(2,1)S(1)}, bf16[2,64,1024]{2,1,0:T(8,128)(2,1)S(1)}, u32[]{:S(2)}, u32[]{:S(2)}) collective-permute-start(bf16[2,64,1024]{2,1,0:T(8,128)(2,1)S(1)} %collective-permute-done.10.refs_4_), channel_id=1, source_target_pairs={{0,4},{4,0},{8,12},{12,8},{16,20},{20,16},{24,28},{28,24},{1,5},{5... | collective-permute-start | bytes 786440 | tf_op jit(solution)/shard_map/ppermute | solution.py:363
  20.5 9.6 %collective-permute-start.15 = (bf16[2,64,1024]{2,1,0:T(8,128)(2,1)S(1)}, bf16[2,64,1024]{2,1,0:T(8,128)(2,1)S(1)}, u32[]{:S(2)}, u32[]{:S(2)}) collective-permute-start(bf16[2,64,1024]{2,1,0:T(8,128)(2,1)S(1)} %collective-permute-done.14.refs_1_), channel_id=1, source_target_pairs={{0,4},{4,0},{8,12},{12,8},{16,20},{20,16},{24,28},{28,24},{1,5},{5... | collective-permute-start | bytes 786440 | tf_op jit(solution)/shard_map/ppermute | solution.py:363
  23.4 14.5 %collective-permute-start.2 = (bf16[2,64,1024]{2,1,0:T(8,128)(2,1)S(1)}, bf16[2,64,1024]{2,1,0:T(8,128)(2,1)S(1)}, u32[]{:S(2)}, u32[]{:S(2)}) collective-permute-start(bf16[2,64,1024]{2,1,0:T(8,128)(2,1)S(1)} %collective-permute-done.1.refs_4_), channel_id=1, source_target_pairs={{0,4},{4,0},{8,12},{12,8},{16,20},{20,16},{24,28},{28,24},{1,5},{5... | collective-permute-start | bytes 786440 | tf_op jit(solution)/shard_map/ppermute | solution.py:363
  26.2 12.0 %collective-permute-start.6 = (bf16[2,64,1024]{2,1,0:T(8,128)(2,1)S(1)}, bf16[2,64,1024]{2,1,0:T(8,128)(2,1)S(1)}, u32[]{:S(2)}, u32[]{:S(2)}) collective-permute-start(bf16[2,64,1024]{2,1,0:T(8,128)(2,1)S(1)} %collective-permute-done.5.refs_1_), channel_id=1, source_target_pairs={{0,4},{4,0},{8,12},{12,8},{16,20},{20,16},{24,28},{28,24},{1,5},{5... | collective-permute-start | bytes 786440 | tf_op jit(solution)/shard_map/ppermute | solution.py:363
  31.1 9.0 %collective-permute-start.16 = (bf16[2,64,256]{2,1,0:T(8,128)(2,1)S(1)}, bf16[2,64,256]{2,1,0:T(8,128)(2,1)S(1)}, u32[]{:S(2)}, u32[]{:S(2)}) collective-permute-start(bf16[2,64,256]{2,1,0:T(8,128)(2,1)S(1)} %get-tuple-element.31), channel_id=1, source_target_pairs={{0,1},{1,2},{2,3},{3,0},{4,5},{5,6},{6,7},{7,4},{8,9},{9,10},{10,1... | collective-permute-start | bytes 196616 | tf_op jit(solution)/shard_map/ppermute | solution.py:384
  33.9 9.0 %collective-permute-start.17 = (bf16[2,64,256]{2,1,0:T(8,128)(2,1)S(1)}, bf16[2,64,256]{2,1,0:T(8,128)(2,1)S(1)}, u32[]{:S(2)}, u32[]{:S(2)}) collective-permute-start(bf16[2,64,256]{2,1,0:T(8,128)(2,1)S(1)} %get-tuple-element.32), channel_id=1, source_target_pairs={{0,2},{1,3},{2,0},{3,1},{4,7},{5,4},{6,5},{7,6},{8,10},{9,11},{10,... | collective-permute-start | bytes 196616 | tf_op jit(solution)/shard_map/ppermute | solution.py:384
  36.5 6.4 %collective-permute-start.18 = (bf16[2,64,256]{2,1,0:T(8,128)(2,1)S(1)}, bf16[2,64,256]{2,1,0:T(8,128)(2,1)S(1)}, u32[]{:S(2)}, u32[]{:S(2)}) collective-permute-start(bf16[2,64,256]{2,1,0:T(8,128)(2,1)S(1)} %get-tuple-element.33), channel_id=1, source_target_pairs={{0,3},{1,0},{2,1},{3,2},{4,6},{5,7},{6,4},{7,5},{8,11},{9,8},{10,9... | collective-permute-start | bytes 196616 | tf_op jit(solution)/shard_map/ppermute | solution.py:384
  39.0 6.3 %collective-permute-start.7 = (bf16[2,64,256]{2,1,0:T(8,128)(2,1)S(1)}, bf16[2,64,256]{2,1,0:T(8,128)(2,1)S(1)}, u32[]{:S(2)}, u32[]{:S(2)}) collective-permute-start(bf16[2,64,256]{2,1,0:T(8,128)(2,1)S(1)} %get-tuple-element.25), channel_id=1, source_target_pairs={{0,1},{1,2},{2,3},{3,0},{4,5},{5,6},{6,7},{7,4},{8,9},{9,10},{10,1... | collective-permute-start | bytes 196616 | tf_op jit(solution)/shard_map/ppermute | solution.py:384
  39.8 7.5 %collective-permute-start.8 = (bf16[2,64,256]{2,1,0:T(8,128)(2,1)S(1)}, bf16[2,64,256]{2,1,0:T(8,128)(2,1)S(1)}, u32[]{:S(2)}, u32[]{:S(2)}) collective-permute-start(bf16[2,64,256]{2,1,0:T(8,128)(2,1)S(1)} %get-tuple-element.26), channel_id=1, source_target_pairs={{0,2},{1,3},{2,0},{3,1},{4,7},{5,4},{6,5},{7,6},{8,10},{9,11},{10,... | collective-permute-start | bytes 196616 | tf_op jit(solution)/shard_map/ppermute | solution.py:384
  40.1 7.2 %collective-permute-start.9 = (bf16[2,64,256]{2,1,0:T(8,128)(2,1)S(1)}, bf16[2,64,256]{2,1,0:T(8,128)(2,1)S(1)}, u32[]{:S(2)}, u32[]{:S(2)}) collective-permute-start(bf16[2,64,256]{2,1,0:T(8,128)(2,1)S(1)} %get-tuple-element.27), channel_id=1, source_target_pairs={{0,3},{1,0},{2,1},{3,2},{4,6},{5,7},{6,4},{7,5},{8,11},{9,8},{10,9... | collective-permute-start | bytes 196616 | tf_op jit(solution)/shard_map/ppermute | solution.py:384

commit v5 on v3

--- a/solution.py
+++ b/solution.py
@@ -328,8 +328,9 @@
             scale = contrast_ref[row, :]
             kept_ref[0, row, :] = (part[:, :wide] * scale).astype(BF16)
             kept_ref[1, row, :] = (part[:, wide:] * scale).astype(BF16)
-            copies.append(pltpu.make_async_copy(kept_ref.at[:, row], out_ref.at[:, row], sems.at[i]))
-            copies[-1].start()
+            for c in range(2):
+                copies.append(pltpu.make_async_copy(kept_ref.at[c, row], out_ref.at[c, row], sems.at[2 * i + c]))
+                copies[-1].start(priority=c)
         for copy in copies:
             copy.wait()
 
@@ -344,7 +345,7 @@
         out_shape=struct((2, nx, wide), BF16),
         in_specs=[pl.BlockSpec(memory_space=pltpu.VMEM)] * len(ins),
         out_specs=pl.BlockSpec(memory_space=pl.ANY),
-        scratch_shapes=scratch + [pltpu.VMEM((2, nx, wide), BF16), pltpu.SemaphoreType.DMA((nx // tall,))],
+        scratch_shapes=scratch + [pltpu.VMEM((2, nx, wide), BF16), pltpu.SemaphoreType.DMA((2 * nx // tall,))],
         compiler_params=pltpu.CompilerParams(vmem_limit_bytes=24 * MIB),
         cost_estimate=pl.CostEstimate(flops=flops, bytes_accessed=4 * MIB, transcendentals=0),
         name="transform_x_last",

time: 48.6 us -> 48.6 us (level)
  no operation moved by 1% of the time
where the time goes in v5:
time: 48.6 us; the launch traced here: 48.5 us
  waiting for transfers between devices  21.7 us (45%)
  starting transfers between devices  17.4 us (36%)
  Pallas kernels  9.3 us (19%)
    ppermute x13, waiting for transfers between devices, send(): return lax.ppermute(v, 'depth', route)  17.7 us
    ppermute x6, starting transfers between devices, hop(): return lax.ppermute(v, ('depth', 'kslab'), pairs)  10 us
    ppermute x13, starting transfers between devices, send(): return lax.ppermute(v, 'depth', route)  7.33 us
    pallas_call x7, Pallas kernels, call(): pl.pallas_call(body, out_shape=[pltpu.VMEM(o.shape, o.dtype) for o in out...  4.07 us
    ppermute x6, waiting for transfers between devices, hop(): return lax.ppermute(v, ('depth', 'kslab'), pairs)  3.94 us
    pallas_call x1, Pallas kernels, prepare(): pl.pallas_call(body, out_shape=[pltpu.VMEM(o.shape, o.dtype) for o in out...  3.02 us
    pallas_call x1, Pallas kernels, transform_x(): pl.pallas_call(last_body, out_shape=struct((2, nx, wide), BF16), in_specs...  1.17 us
    pallas_call x1, Pallas kernels, split_rows(): pl.pallas_call(body, out_shape=[pltpu.VMEM((planes, size, ny), own.dtype)...  1.04 us
  transfers between devices with their start and end apart: 19, of which 8 were waited for; matrix products, arithmetic and copies ran while one was open for 0% of the time, Pallas kernels for 17%

profile of v5, /device:TPU:0, one launch (start us, length us, event | category | flops | bytes accessed | tf_op | source)
XLA Modules:
  0.0 48.5 jit_solution(637706062079039814)
XLA Ops:
  0.0 0.5 %collective-permute-start = (bf16[2,128,1024]{2,1,0:T(8,128)(2,1)}, bf16[2,128,1024]{2,1,0:T(8,128)(2,1)S(1)}, u32[]{:S(2)}, u32[]{:S(2)}) collective-permute-start(bf16[2,128,1024]{2,1,0:T(8,128)(2,1)} %bitcast.6), channel_id=1, source_target_pairs={{0,4},{4,0},{8,12},{12,8},{16,20},{20,16},{24,28},{28,24},{1,5},{5... | collective-permute-start | bytes 1572872 | tf_op jit(solution)/shard_map/ppermute | solution.py:364
  0.5 1.0 %split_rows.1 = (bf16[2,64,1024]{2,1,0:T(8,128)(2,1)S(1)}, bf16[2,64,1024]{2,1,0:T(8,128)(2,1)S(1)}) custom-call(bf16[2,128,1024]{2,1,0:T(8,128)(2,1)} %bitcast.7), custom_call_target="tpu_custom_call" | custom-call | bytes 1048576 | tf_op jit(solution)/shard_map/split_rows/pallas_call | solution.py:129
  1.5 2.5 %collective-permute-start.12 = (bf16[2,64,1024]{2,1,0:T(8,128)(2,1)S(1)}, bf16[2,64,1024]{2,1,0:T(8,128)(2,1)S(1)}, u32[]{:S(2)}, u32[]{:S(2)}) collective-permute-start(bf16[2,64,1024]{2,1,0:T(8,128)(2,1)S(1)} %get-tuple-element.29.refs_0_), channel_id=1, source_target_pairs={{0,8},{4,20},{8,0},{12,28},{16,24},{20,4},{24,16},{28,12},{1,9},{5... | collective-permute-start | bytes 786440 | tf_op jit(solution)/shard_map/ppermute | solution.py:364
  4.2 4.3 %collective-permute-done.12.refs_2_ = bf16[2,64,1024]{2,1,0:T(8,128)(2,1)S(1)} collective-permute-done((bf16[2,64,1024]{2,1,0:T(8,128)(2,1)S(1)}, bf16[2,64,1024]{2,1,0:T(8,128)(2,1)S(1)}, u32[]{:S(2)}, u32[]{:S(2)}) %collective-permute-start.12) | collective-permute-done | bytes 262176 | tf_op jit(solution)/shard_map/ppermute | solution.py:364
  8.4 2.8 %collective-permute-done.3.refs_2_ = bf16[2,64,1024]{2,1,0:T(8,128)(2,1)S(1)} collective-permute-done((bf16[2,64,1024]{2,1,0:T(8,128)(2,1)S(1)}, bf16[2,64,1024]{2,1,0:T(8,128)(2,1)S(1)}, u32[]{:S(2)}, u32[]{:S(2)}) %collective-permute-start.3) | collective-permute-done | bytes 262176 | tf_op jit(solution)/shard_map/ppermute | solution.py:364
  11.3 2.1 %collective-permute-start.10 = (bf16[2,64,1024]{2,1,0:T(8,128)(2,1)S(1)}, bf16[2,64,1024]{2,1,0:T(8,128)(2,1)S(1)}, u32[]{:S(2)}, u32[]{:S(2)}) collective-permute-start(bf16[2,64,1024]{2,1,0:T(8,128)(2,1)S(1)} %get-tuple-element.35), channel_id=1, source_target_pairs={{0,8},{4,20},{8,0},{12,28},{16,24},{20,4},{24,16},{28,12},{1,9},{5... | collective-permute-start | bytes 786440 | tf_op jit(solution)/shard_map/ppermute | solution.py:364
  13.5 1.9 %collective-permute-start.1 = (bf16[2,64,1024]{2,1,0:T(8,128)(2,1)S(1)}, bf16[2,64,1024]{2,1,0:T(8,128)(2,1)S(1)}, u32[]{:S(2)}, u32[]{:S(2)}) collective-permute-start(bf16[2,64,1024]{2,1,0:T(8,128)(2,1)S(1)} %get-tuple-element.36), channel_id=1, source_target_pairs={{0,8},{4,20},{8,0},{12,28},{16,24},{20,4},{24,16},{28,12},{1,9},{5... | collective-permute-start | bytes 786440 | tf_op jit(solution)/shard_map/ppermute | solution.py:364
  15.5 2.2 %collective-permute-done.10.refs_4_ = bf16[2,64,1024]{2,1,0:T(8,128)(2,1)S(1)} collective-permute-done((bf16[2,64,1024]{2,1,0:T(8,128)(2,1)S(1)}, bf16[2,64,1024]{2,1,0:T(8,128)(2,1)S(1)}, u32[]{:S(2)}, u32[]{:S(2)}) %collective-permute-start.10) | collective-permute-done | bytes 262176 | tf_op jit(solution)/shard_map/ppermute | solution.py:364
  17.7 2.8 %collective-permute-done.14.refs_1_ = bf16[2,64,1024]{2,1,0:T(8,128)(2,1)S(1)} collective-permute-done((bf16[2,64,1024]{2,1,0:T(8,128)(2,1)S(1)}, bf16[2,64,1024]{2,1,0:T(8,128)(2,1)S(1)}, u32[]{:S(2)}, u32[]{:S(2)}) %collective-permute-start.14) | collective-permute-done | bytes 262176 | tf_op jit(solution)/shard_map/ppermute | solution.py:364
  20.5 2.8 %collective-permute-done.1.refs_4_ = bf16[2,64,1024]{2,1,0:T(8,128)(2,1)S(1)} collective-permute-done((bf16[2,64,1024]{2,1,0:T(8,128)(2,1)S(1)}, bf16[2,64,1024]{2,1,0:T(8,128)(2,1)S(1)}, u32[]{:S(2)}, u32[]{:S(2)}) %collective-permute-start.1) | collective-permute-done | bytes 262176 | tf_op jit(solution)/shard_map/ppermute | solution.py:364
  23.4 2.8 %collective-permute-done.5.refs_1_ = bf16[2,64,1024]{2,1,0:T(8,128)(2,1)S(1)} collective-permute-done((bf16[2,64,1024]{2,1,0:T(8,128)(2,1)S(1)}, bf16[2,64,1024]{2,1,0:T(8,128)(2,1)S(1)}, u32[]{:S(2)}, u32[]{:S(2)}) %collective-permute-start.5) | collective-permute-done | bytes 262176 | tf_op jit(solution)/shard_map/ppermute | solution.py:364
  26.2 3.0 %prepare.1 = (bf16[2,1024,1024]{2,1,0:T(8,128)(2,1)S(1)}, bf16[2,512,256]{2,1,0:T(8,128)(2,1)S(1)}, bf16[2,512,256]{2,1,0:T(8,128)(2,1)S(1)}, bf16[8,2,128,1024]{3,2,1,0:T(8,128)(2,1)S(1)}, f32[512,256]{1,0:T(8,128)S(1)}) custom-call(bf16[8,2,128,1024]{3,2,1,0:T(8,128)(2,1)} %bitcast.4, f32[512,256]{1,0:T(8,128)} %bitcast.5), custom_call_target="tpu_custom_call" | custom-call | flops 8388608 | bytes 8388608 | tf_op jit(solution)/shard_map/prepare/pallas_call | solution.py:192
  29.2 0.7 %shard_map.40.refs_2_ = f32[2,64,1024]{2,1,0:T(8,128)S(1)} custom-call(bf16[8,2,128,1024]{3,2,1,0:T(8,128)(2,1)S(1)} %get-tuple-element.21.green_ref, bf16[2,64,1024]{2,1,0:T(8,128)(2,1)S(1)} %get-tuple-element.29.refs_0_, bf16[2,128,1024]{2,1,0:T(8,128)(2,1)S(1)} %collective-permute-done.refs_1_, bf16[2,64,1024]{2,1,0:T(8,128)(2,1)S(1)} %collective-permute-done.12.refs_2_, ...), custom_call_target="tpu_custom_call" | custom-call | flops 2621440 | bytes 6291456 | tf_op jit(solution)/shard_map/pallas_call | solution.py:65
  30.2 0.9 %shard_map.42 = (bf16[2,64,256]{2,1,0:T(8,128)(2,1)S(1)}, bf16[2,64,256]{2,1,0:T(8,128)(2,1)S(1)}, bf16[2,64,256]{2,1,0:T(8,128)(2,1)S(1)}, bf16[2,64,256]{2,1,0:T(8,128)(2,1)S(1)}) custom-call(bf16[8,2,128,1024]{3,2,1,0:T(8,128)(2,1)S(1)} %get-tuple-element.21.green_ref, f32[2,64,1024]{2,1,0:T(8,128)S(1)} %shard_map.41.total_ref, ...), custom_call_target="tpu_custom_call" | custom-call | flops 536870912 | bytes 9437184 | tf_op jit(solution)/shard_map/pallas_call | solution.py:65
  31.1 2.2 %collective-permute-start.16 = (bf16[2,64,256]{2,1,0:T(8,128)(2,1)S(1)}, bf16[2,64,256]{2,1,0:T(8,128)(2,1)S(1)}, u32[]{:S(2)}, u32[]{:S(2)}) collective-permute-start(bf16[2,64,256]{2,1,0:T(8,128)(2,1)S(1)} %get-tuple-element.31), channel_id=1, source_target_pairs={{0,1},{1,2},{2,3},{3,0},{4,5},{5,6},{6,7},{7,4},{8,9},{9,10},{10,1... | collective-permute-start | bytes 196616 | tf_op jit(solution)/shard_map/ppermute | solution.py:385
  33.2 0.7 %shard_map.37.refs_2_ = f32[2,64,1024]{2,1,0:T(8,128)S(1)} custom-call(bf16[8,2,128,1024]{3,2,1,0:T(8,128)(2,1)S(1)} %get-tuple-element.21.green_ref, bf16[2,64,1024]{2,1,0:T(8,128)(2,1)S(1)} %get-tuple-element.22.refs_0_, bf16[2,128,1024]{2,1,0:T(8,128)(2,1)S(1)} %collective-permute-done.refs_1_, bf16[2,64,1024]{2,1,0:T(8,128)(2,1)S(1)} %collective-permute-done.3.refs_2_, ...), custom_call_target="tpu_custom_call" | custom-call | flops 2621440 | bytes 6291456 | tf_op jit(solution)/shard_map/pallas_call | solution.py:65
  33.9 2.6 %collective-permute-start.17 = (bf16[2,64,256]{2,1,0:T(8,128)(2,1)S(1)}, bf16[2,64,256]{2,1,0:T(8,128)(2,1)S(1)}, u32[]{:S(2)}, u32[]{:S(2)}) collective-permute-start(bf16[2,64,256]{2,1,0:T(8,128)(2,1)S(1)} %get-tuple-element.32), channel_id=1, source_target_pairs={{0,2},{1,3},{2,0},{3,1},{4,7},{5,4},{6,5},{7,6},{8,10},{9,11},{10,... | collective-permute-start | bytes 196616 | tf_op jit(solution)/shard_map/ppermute | solution.py:385
  36.6 1.3 %collective-permute-start.18 = (bf16[2,64,256]{2,1,0:T(8,128)(2,1)S(1)}, bf16[2,64,256]{2,1,0:T(8,128)(2,1)S(1)}, u32[]{:S(2)}, u32[]{:S(2)}) collective-permute-start(bf16[2,64,256]{2,1,0:T(8,128)(2,1)S(1)} %get-tuple-element.33), channel_id=1, source_target_pairs={{0,3},{1,0},{2,1},{3,2},{4,6},{5,7},{6,4},{7,5},{8,11},{9,8},{10,9... | collective-permute-start | bytes 196616 | tf_op jit(solution)/shard_map/ppermute | solution.py:385
  38.2 0.9 %shard_map.39 = (bf16[2,64,256]{2,1,0:T(8,128)(2,1)S(1)}, bf16[2,64,256]{2,1,0:T(8,128)(2,1)S(1)}, bf16[2,64,256]{2,1,0:T(8,128)(2,1)S(1)}, bf16[2,64,256]{2,1,0:T(8,128)(2,1)S(1)}) custom-call(bf16[8,2,128,1024]{3,2,1,0:T(8,128)(2,1)S(1)} %get-tuple-element.21.green_ref, f32[2,64,1024]{2,1,0:T(8,128)S(1)} %shard_map.38.total_ref, ...), custom_call_target="tpu_custom_call" | custom-call | flops 536870912 | bytes 9437184 | tf_op jit(solution)/shard_map/pallas_call | solution.py:65
  39.1 0.7 %collective-permute-start.7 = (bf16[2,64,256]{2,1,0:T(8,128)(2,1)S(1)}, bf16[2,64,256]{2,1,0:T(8,128)(2,1)S(1)}, u32[]{:S(2)}, u32[]{:S(2)}) collective-permute-start(bf16[2,64,256]{2,1,0:T(8,128)(2,1)S(1)} %get-tuple-element.25), channel_id=1, source_target_pairs={{0,1},{1,2},{2,3},{3,0},{4,5},{5,6},{6,7},{7,4},{8,9},{9,10},{10,1... | collective-permute-start | bytes 196616 | tf_op jit(solution)/shard_map/ppermute | solution.py:385
  40.1 2.8 %collective-permute-start.9 = (bf16[2,64,256]{2,1,0:T(8,128)(2,1)S(1)}, bf16[2,64,256]{2,1,0:T(8,128)(2,1)S(1)}, u32[]{:S(2)}, u32[]{:S(2)}) collective-permute-start(bf16[2,64,256]{2,1,0:T(8,128)(2,1)S(1)} %get-tuple-element.27), channel_id=1, source_target_pairs={{0,3},{1,0},{2,1},{3,2},{4,6},{5,7},{6,4},{7,5},{8,11},{9,8},{10,9... | collective-permute-start | bytes 196616 | tf_op jit(solution)/shard_map/ppermute | solution.py:385
  43.4 2.0 %collective-permute-done.7.refs_1_ = bf16[2,64,256]{2,1,0:T(8,128)(2,1)S(1)} collective-permute-done((bf16[2,64,256]{2,1,0:T(8,128)(2,1)S(1)}, bf16[2,64,256]{2,1,0:T(8,128)(2,1)S(1)}, u32[]{:S(2)}, u32[]{:S(2)}) %collective-permute-start.7) | collective-permute-done | bytes 65568 | tf_op jit(solution)/shard_map/ppermute | solution.py:385
  45.4 1.9 %collective-permute-done.8.refs_2_ = bf16[2,64,256]{2,1,0:T(8,128)(2,1)S(1)} collective-permute-done((bf16[2,64,256]{2,1,0:T(8,128)(2,1)S(1)}, bf16[2,64,256]{2,1,0:T(8,128)(2,1)S(1)}, u32[]{:S(2)}, u32[]{:S(2)}) %collective-permute-start.8) | collective-permute-done | bytes 65568 | tf_op jit(solution)/shard_map/ppermute | solution.py:385
  47.3 1.2 %transform_x_last.1 = bf16[2,512,256]{2,1,0:T(8,128)(2,1)} custom-call(bf16[2,512,256]{2,1,0:T(8,128)(2,1)S(1)} %get-tuple-element.20.table_ref, bf16[2,64,256]{2,1,0:T(8,128)(2,1)S(1)} %get-tuple-element.24.refs_0_, bf16[2,64,256]{2,1,0:T(8,128)(2,1)S(1)} %collective-permute-done.7.refs_1_, bf16[2,64,256]{2,1,0:T(8,128)(2,1)S(1)} %collective-permute-done.8.refs_2_, ...), custom_call_target="tpu_custom_call" | custom-call | flops 268435456 | bytes 4194304 | tf_op jit(solution)/shard_map/transform_x_last/pallas_call | solution.py:343
  (25 shorter events, 1.6 us)
Async XLA Ops:
  0.0 11.3 %collective-permute-start = (bf16[2,128,1024]{2,1,0:T(8,128)(2,1)}, bf16[2,128,1024]{2,1,0:T(8,128)(2,1)S(1)}, u32[]{:S(2)}, u32[]{:S(2)}) collective-permute-start(bf16[2,128,1024]{2,1,0:T(8,128)(2,1)} %bitcast.6), channel_id=1, source_target_pairs={{0,4},{4,0},{8,12},{12,8},{16,20},{20,16},{24,28},{28,24},{1,5},{5... | collective-permute-start | bytes 1572872 | tf_op jit(solution)/shard_map/ppermute | solution.py:364
  1.5 6.9 %collective-permute-start.12 = (bf16[2,64,1024]{2,1,0:T(8,128)(2,1)S(1)}, bf16[2,64,1024]{2,1,0:T(8,128)(2,1)S(1)}, u32[]{:S(2)}, u32[]{:S(2)}) collective-permute-start(bf16[2,64,1024]{2,1,0:T(8,128)(2,1)S(1)} %get-tuple-element.29.refs_0_), channel_id=1, source_target_pairs={{0,8},{4,20},{8,0},{12,28},{16,24},{20,4},{24,16},{28,12},{1,9},{5... | collective-permute-start | bytes 786440 | tf_op jit(solution)/shard_map/ppermute | solution.py:364
  4.1 7.2 %collective-permute-start.3 = (bf16[2,64,1024]{2,1,0:T(8,128)(2,1)S(1)}, bf16[2,64,1024]{2,1,0:T(8,128)(2,1)S(1)}, u32[]{:S(2)}, u32[]{:S(2)}) collective-permute-start(bf16[2,64,1024]{2,1,0:T(8,128)(2,1)S(1)} %get-tuple-element.22.refs_0_), channel_id=1, source_target_pairs={{0,8},{4,20},{8,0},{12,28},{16,24},{20,4},{24,16},{28,12},{1,9},{5... | collective-permute-start | bytes 786440 | tf_op jit(solution)/shard_map/ppermute | solution.py:364
  8.4 4.9 %collective-permute-start.13 = (bf16[2,64,1024]{2,1,0:T(8,128)(2,1)S(1)}, bf16[2,64,1024]{2,1,0:T(8,128)(2,1)S(1)}, u32[]{:S(2)}, u32[]{:S(2)}) collective-permute-start(bf16[2,64,1024]{2,1,0:T(8,128)(2,1)S(1)} %collective-permute-done.12.refs_2_), channel_id=1, source_target_pairs={{0,4},{4,0},{8,12},{12,8},{16,20},{20,16},{24,28},{28,24},{1,5},{5... | collective-permute-start | bytes 786440 | tf_op jit(solution)/shard_map/ppermute | solution.py:364
  11.3 4.2 %collective-permute-start.4 = (bf16[2,64,1024]{2,1,0:T(8,128)(2,1)S(1)}, bf16[2,64,1024]{2,1,0:T(8,128)(2,1)S(1)}, u32[]{:S(2)}, u32[]{:S(2)}) collective-permute-start(bf16[2,64,1024]{2,1,0:T(8,128)(2,1)S(1)} %collective-permute-done.3.refs_2_), channel_id=1, source_target_pairs={{0,4},{4,0},{8,12},{12,8},{16,20},{20,16},{24,28},{28,24},{1,5},{5... | collective-permute-start | bytes 786440 | tf_op jit(solution)/shard_map/ppermute | solution.py:364
  11.3 6.4 %collective-permute-start.10 = (bf16[2,64,1024]{2,1,0:T(8,128)(2,1)S(1)}, bf16[2,64,1024]{2,1,0:T(8,128)(2,1)S(1)}, u32[]{:S(2)}, u32[]{:S(2)}) collective-permute-start(bf16[2,64,1024]{2,1,0:T(8,128)(2,1)S(1)} %get-tuple-element.35), channel_id=1, source_target_pairs={{0,8},{4,20},{8,0},{12,28},{16,24},{20,4},{24,16},{28,12},{1,9},{5... | collective-permute-start | bytes 786440 | tf_op jit(solution)/shard_map/ppermute | solution.py:364
  13.4 7.2 %collective-permute-start.14 = (bf16[2,64,1024]{2,1,0:T(8,128)(2,1)S(1)}, bf16[2,64,1024]{2,1,0:T(8,128)(2,1)S(1)}, u32[]{:S(2)}, u32[]{:S(2)}) collective-permute-start(bf16[2,64,1024]{2,1,0:T(8,128)(2,1)S(1)} %collective-permute-done.13.refs_3_), channel_id=1, source_target_pairs={{0,8},{4,20},{8,0},{12,28},{16,24},{20,4},{24,16},{28,12},{1,9},{5... | collective-permute-start | bytes 786440 | tf_op jit(solution)/shard_map/ppermute | solution.py:364
  13.5 9.9 %collective-permute-start.1 = (bf16[2,64,1024]{2,1,0:T(8,128)(2,1)S(1)}, bf16[2,64,1024]{2,1,0:T(8,128)(2,1)S(1)}, u32[]{:S(2)}, u32[]{:S(2)}) collective-permute-start(bf16[2,64,1024]{2,1,0:T(8,128)(2,1)S(1)} %get-tuple-element.36), channel_id=1, source_target_pairs={{0,8},{4,20},{8,0},{12,28},{16,24},{20,4},{24,16},{28,12},{1,9},{5... | collective-permute-start | bytes 786440 | tf_op jit(solution)/shard_map/ppermute | solution.py:364
  15.4 10.7 %collective-permute-start.5 = (bf16[2,64,1024]{2,1,0:T(8,128)(2,1)S(1)}, bf16[2,64,1024]{2,1,0:T(8,128)(2,1)S(1)}, u32[]{:S(2)}, u32[]{:S(2)}) collective-permute-start(bf16[2,64,1024]{2,1,0:T(8,128)(2,1)S(1)} %collective-permute-done.4.refs_3_), channel_id=1, source_target_pairs={{0,8},{4,20},{8,0},{12,28},{16,24},{20,4},{24,16},{28,12},{1,9},{5... | collective-permute-start | bytes 786440 | tf_op jit(solution)/shard_map/ppermute | solution.py:364
  17.7 12.2 %collective-permute-start.11 = (bf16[2,64,1024]{2,1,0:T(8,128)(2,1)S(1)}, bf16[2,64,1024]{2,1,0:T(8,128)(2,1)S(1)}, u32[]{:S(2)}, u32[]{:S(2)}) collective-permute-start(bf16[2,64,1024]{2,1,0:T(8,128)(2,1)S(1)} %collective-permute-done.10.refs_4_), channel_id=1, source_target_pairs={{0,4},{4,0},{8,12},{12,8},{16,20},{20,16},{24,28},{28,24},{1,5},{5... | collective-permute-start | bytes 786440 | tf_op jit(solution)/shard_map/ppermute | solution.py:364
  20.5 9.6 %collective-permute-start.15 = (bf16[2,64,1024]{2,1,0:T(8,128)(2,1)S(1)}, bf16[2,64,1024]{2,1,0:T(8,128)(2,1)S(1)}, u32[]{:S(2)}, u32[]{:S(2)}) collective-permute-start(bf16[2,64,1024]{2,1,0:T(8,128)(2,1)S(1)} %collective-permute-done.14.refs_1_), channel_id=1, source_target_pairs={{0,4},{4,0},{8,12},{12,8},{16,20},{20,16},{24,28},{28,24},{1,5},{5... | collective-permute-start | bytes 786440 | tf_op jit(solution)/shard_map/ppermute | solution.py:364
  23.4 14.6 %collective-permute-start.2 = (bf16[2,64,1024]{2,1,0:T(8,128)(2,1)S(1)}, bf16[2,64,1024]{2,1,0:T(8,128)(2,1)S(1)}, u32[]{:S(2)}, u32[]{:S(2)}) collective-permute-start(bf16[2,64,1024]{2,1,0:T(8,128)(2,1)S(1)} %collective-permute-done.1.refs_4_), channel_id=1, source_target_pairs={{0,4},{4,0},{8,12},{12,8},{16,20},{20,16},{24,28},{28,24},{1,5},{5... | collective-permute-start | bytes 786440 | tf_op jit(solution)/shard_map/ppermute | solution.py:364
  26.2 12.0 %collective-permute-start.6 = (bf16[2,64,1024]{2,1,0:T(8,128)(2,1)S(1)}, bf16[2,64,1024]{2,1,0:T(8,128)(2,1)S(1)}, u32[]{:S(2)}, u32[]{:S(2)}) collective-permute-start(bf16[2,64,1024]{2,1,0:T(8,128)(2,1)S(1)} %collective-permute-done.5.refs_1_), channel_id=1, source_target_pairs={{0,4},{4,0},{8,12},{12,8},{16,20},{20,16},{24,28},{28,24},{1,5},{5... | collective-permute-start | bytes 786440 | tf_op jit(solution)/shard_map/ppermute | solution.py:364
  31.1 9.1 %collective-permute-start.16 = (bf16[2,64,256]{2,1,0:T(8,128)(2,1)S(1)}, bf16[2,64,256]{2,1,0:T(8,128)(2,1)S(1)}, u32[]{:S(2)}, u32[]{:S(2)}) collective-permute-start(bf16[2,64,256]{2,1,0:T(8,128)(2,1)S(1)} %get-tuple-element.31), channel_id=1, source_target_pairs={{0,1},{1,2},{2,3},{3,0},{4,5},{5,6},{6,7},{7,4},{8,9},{9,10},{10,1... | collective-permute-start | bytes 196616 | tf_op jit(solution)/shard_map/ppermute | solution.py:385
  33.9 9.0 %collective-permute-start.17 = (bf16[2,64,256]{2,1,0:T(8,128)(2,1)S(1)}, bf16[2,64,256]{2,1,0:T(8,128)(2,1)S(1)}, u32[]{:S(2)}, u32[]{:S(2)}) collective-permute-start(bf16[2,64,256]{2,1,0:T(8,128)(2,1)S(1)} %get-tuple-element.32), channel_id=1, source_target_pairs={{0,2},{1,3},{2,0},{3,1},{4,7},{5,4},{6,5},{7,6},{8,10},{9,11},{10,... | collective-permute-start | bytes 196616 | tf_op jit(solution)/shard_map/ppermute | solution.py:385
  36.6 6.4 %collective-permute-start.18 = (bf16[2,64,256]{2,1,0:T(8,128)(2,1)S(1)}, bf16[2,64,256]{2,1,0:T(8,128)(2,1)S(1)}, u32[]{:S(2)}, u32[]{:S(2)}) collective-permute-start(bf16[2,64,256]{2,1,0:T(8,128)(2,1)S(1)} %get-tuple-element.33), channel_id=1, source_target_pairs={{0,3},{1,0},{2,1},{3,2},{4,6},{5,7},{6,4},{7,5},{8,11},{9,8},{10,9... | collective-permute-start | bytes 196616 | tf_op jit(solution)/shard_map/ppermute | solution.py:385
  39.1 6.3 %collective-permute-start.7 = (bf16[2,64,256]{2,1,0:T(8,128)(2,1)S(1)}, bf16[2,64,256]{2,1,0:T(8,128)(2,1)S(1)}, u32[]{:S(2)}, u32[]{:S(2)}) collective-permute-start(bf16[2,64,256]{2,1,0:T(8,128)(2,1)S(1)} %get-tuple-element.25), channel_id=1, source_target_pairs={{0,1},{1,2},{2,3},{3,0},{4,5},{5,6},{6,7},{7,4},{8,9},{9,10},{10,1... | collective-permute-start | bytes 196616 | tf_op jit(solution)/shard_map/ppermute | solution.py:385
  39.8 7.5 %collective-permute-start.8 = (bf16[2,64,256]{2,1,0:T(8,128)(2,1)S(1)}, bf16[2,64,256]{2,1,0:T(8,128)(2,1)S(1)}, u32[]{:S(2)}, u32[]{:S(2)}) collective-permute-start(bf16[2,64,256]{2,1,0:T(8,128)(2,1)S(1)} %get-tuple-element.26), channel_id=1, source_target_pairs={{0,2},{1,3},{2,0},{3,1},{4,7},{5,4},{6,5},{7,6},{8,10},{9,11},{10,... | collective-permute-start | bytes 196616 | tf_op jit(solution)/shard_map/ppermute | solution.py:385
  40.1 7.2 %collective-permute-start.9 = (bf16[2,64,256]{2,1,0:T(8,128)(2,1)S(1)}, bf16[2,64,256]{2,1,0:T(8,128)(2,1)S(1)}, u32[]{:S(2)}, u32[]{:S(2)}) collective-permute-start(bf16[2,64,256]{2,1,0:T(8,128)(2,1)S(1)} %get-tuple-element.27), channel_id=1, source_target_pairs={{0,3},{1,0},{2,1},{3,2},{4,6},{5,7},{6,4},{7,5},{8,11},{9,8},{10,9... | collective-permute-start | bytes 196616 | tf_op jit(solution)/shard_map/ppermute | solution.py:385

commit v6 on v3

--- a/solution.py
+++ b/solution.py
@@ -357,7 +357,7 @@
     own, green, contrast = spectra[0], green[0], contrast[0]
 
     swap = [(i, i ^ 1) for i in range(8)]
-    out = [(i, i ^ 2 if i % 2 == 0 else i ^ 4) for i in range(8)]
+    out = [(i, i ^ 4 if i % 2 == 0 else i ^ 2) for i in range(8)]
 
     def send(v, route):
         return lax.ppermute(v, "depth", route)
@@ -387,9 +387,9 @@
     for i, (start, size) in enumerate(parts):
         far_swap, across_swap = send(far[i], swap), send(across[i], swap)
         sources = [(owns[i], 0, 0), (own_swap, 0, start), (near[i], 0, 0), (near_swap[i], 0, 0), (far[i], 0, 0)]
-        total = early_sum(green, sources, layers([(0, 0), (1, 1), (2, 4), (5, 3), (3, 5)]), start, size)
+        total = early_sum(green, sources, layers([(0, 0), (1, 1), (4, 2), (3, 5), (5, 3)]), start, size)
         sources = [(far_swap, 0, 0), (across[i], 0, 0)]
-        total = early_sum(green, sources, layers([(4, 2), (7, 7)]), start, size, total)
+        total = early_sum(green, sources, layers([(2, 4), (7, 7)]), start, size, total)
         halves.append(finish_rows(green, total, [(across_swap, 0, 0)], layers([(6, 6)]), table_y, start, size, slabs))
     field = None
     for i, slab in enumerate(halves):

time: 48.6 us -> 48.6 us (level)
  no operation moved by 1% of the time
where the time goes in v6:
time: 48.6 us; the launch traced here: 48.5 us
  waiting for transfers between devices  21.7 us (45%)
  starting transfers between devices  17.4 us (36%)
  Pallas kernels  9.28 us (19%)
    ppermute x13, waiting for transfers between devices, send(): return lax.ppermute(v, 'depth', route)  17.7 us
    ppermute x6, starting transfers between devices, hop(): return lax.ppermute(v, ('depth', 'kslab'), pairs)  10 us
    ppermute x13, starting transfers between devices, send(): return lax.ppermute(v, 'depth', route)  7.36 us
    pallas_call x7, Pallas kernels, call(): pl.pallas_call(body, out_shape=[pltpu.VMEM(o.shape, o.dtype) for o in out...  4.07 us
    ppermute x6, waiting for transfers between devices, hop(): return lax.ppermute(v, ('depth', 'kslab'), pairs)  3.94 us
    pallas_call x1, Pallas kernels, prepare(): pl.pallas_call(body, out_shape=[pltpu.VMEM(o.shape, o.dtype) for o in out...  3.02 us
    pallas_call x1, Pallas kernels, transform_x(): pl.pallas_call(last_body, out_shape=struct((2, nx, wide), BF16), in_specs...  1.14 us
    pallas_call x1, Pallas kernels, split_rows(): pl.pallas_call(body, out_shape=[pltpu.VMEM((planes, size, ny), own.dtype)...  1.04 us
  transfers between devices with their start and end apart: 19, of which 8 were waited for; matrix products, arithmetic and copies ran while one was open for 0% of the time, Pallas kernels for 17%

profile of v6, /device:TPU:0, one launch (start us, length us, event | category | flops | bytes accessed | tf_op | source)
XLA Modules:
  0.0 48.5 jit_solution(9361327445517885138)
XLA Ops:
  0.0 0.5 %collective-permute-start = (bf16[2,128,1024]{2,1,0:T(8,128)(2,1)}, bf16[2,128,1024]{2,1,0:T(8,128)(2,1)S(1)}, u32[]{:S(2)}, u32[]{:S(2)}) collective-permute-start(bf16[2,128,1024]{2,1,0:T(8,128)(2,1)} %bitcast.6), channel_id=1, source_target_pairs={{0,4},{4,0},{8,12},{12,8},{16,20},{20,16},{24,28},{28,24},{1,5},{5... | collective-permute-start | bytes 1572872 | tf_op jit(solution)/shard_map/ppermute | solution.py:363
  0.5 1.0 %split_rows.1 = (bf16[2,64,1024]{2,1,0:T(8,128)(2,1)S(1)}, bf16[2,64,1024]{2,1,0:T(8,128)(2,1)S(1)}) custom-call(bf16[2,128,1024]{2,1,0:T(8,128)(2,1)} %bitcast.7), custom_call_target="tpu_custom_call" | custom-call | bytes 1048576 | tf_op jit(solution)/shard_map/split_rows/pallas_call | solution.py:129
  1.5 2.6 %collective-permute-start.12 = (bf16[2,64,1024]{2,1,0:T(8,128)(2,1)S(1)}, bf16[2,64,1024]{2,1,0:T(8,128)(2,1)S(1)}, u32[]{:S(2)}, u32[]{:S(2)}) collective-permute-start(bf16[2,64,1024]{2,1,0:T(8,128)(2,1)S(1)} %get-tuple-element.29.refs_0_), channel_id=1, source_target_pairs={{0,16},{4,12},{8,24},{12,4},{16,0},{20,28},{24,8},{28,20},{1,17},{... | collective-permute-start | bytes 786440 | tf_op jit(solution)/shard_map/ppermute | solution.py:363
  4.2 4.3 %collective-permute-done.12.refs_2_ = bf16[2,64,1024]{2,1,0:T(8,128)(2,1)S(1)} collective-permute-done((bf16[2,64,1024]{2,1,0:T(8,128)(2,1)S(1)}, bf16[2,64,1024]{2,1,0:T(8,128)(2,1)S(1)}, u32[]{:S(2)}, u32[]{:S(2)}) %collective-permute-start.12) | collective-permute-done | bytes 262176 | tf_op jit(solution)/shard_map/ppermute | solution.py:363
  8.5 2.8 %collective-permute-done.3.refs_2_ = bf16[2,64,1024]{2,1,0:T(8,128)(2,1)S(1)} collective-permute-done((bf16[2,64,1024]{2,1,0:T(8,128)(2,1)S(1)}, bf16[2,64,1024]{2,1,0:T(8,128)(2,1)S(1)}, u32[]{:S(2)}, u32[]{:S(2)}) %collective-permute-start.3) | collective-permute-done | bytes 262176 | tf_op jit(solution)/shard_map/ppermute | solution.py:363
  11.3 2.1 %collective-permute-start.10 = (bf16[2,64,1024]{2,1,0:T(8,128)(2,1)S(1)}, bf16[2,64,1024]{2,1,0:T(8,128)(2,1)S(1)}, u32[]{:S(2)}, u32[]{:S(2)}) collective-permute-start(bf16[2,64,1024]{2,1,0:T(8,128)(2,1)S(1)} %get-tuple-element.35), channel_id=1, source_target_pairs={{0,16},{4,12},{8,24},{12,4},{16,0},{20,28},{24,8},{28,20},{1,17},{... | collective-permute-start | bytes 786440 | tf_op jit(solution)/shard_map/ppermute | solution.py:363
  13.5 1.9 %collective-permute-start.1 = (bf16[2,64,1024]{2,1,0:T(8,128)(2,1)S(1)}, bf16[2,64,1024]{2,1,0:T(8,128)(2,1)S(1)}, u32[]{:S(2)}, u32[]{:S(2)}) collective-permute-start(bf16[2,64,1024]{2,1,0:T(8,128)(2,1)S(1)} %get-tuple-element.36), channel_id=1, source_target_pairs={{0,16},{4,12},{8,24},{12,4},{16,0},{20,28},{24,8},{28,20},{1,17},{... | collective-permute-start | bytes 786440 | tf_op jit(solution)/shard_map/ppermute | solution.py:363
  15.5 2.2 %collective-permute-done.10.refs_4_ = bf16[2,64,1024]{2,1,0:T(8,128)(2,1)S(1)} collective-permute-done((bf16[2,64,1024]{2,1,0:T(8,128)(2,1)S(1)}, bf16[2,64,1024]{2,1,0:T(8,128)(2,1)S(1)}, u32[]{:S(2)}, u32[]{:S(2)}) %collective-permute-start.10) | collective-permute-done | bytes 262176 | tf_op jit(solution)/shard_map/ppermute | solution.py:363
  17.8 2.8 %collective-permute-done.14.refs_1_ = bf16[2,64,1024]{2,1,0:T(8,128)(2,1)S(1)} collective-permute-done((bf16[2,64,1024]{2,1,0:T(8,128)(2,1)S(1)}, bf16[2,64,1024]{2,1,0:T(8,128)(2,1)S(1)}, u32[]{:S(2)}, u32[]{:S(2)}) %collective-permute-start.14) | collective-permute-done | bytes 262176 | tf_op jit(solution)/shard_map/ppermute | solution.py:363
  20.6 2.8 %collective-permute-done.1.refs_4_ = bf16[2,64,1024]{2,1,0:T(8,128)(2,1)S(1)} collective-permute-done((bf16[2,64,1024]{2,1,0:T(8,128)(2,1)S(1)}, bf16[2,64,1024]{2,1,0:T(8,128)(2,1)S(1)}, u32[]{:S(2)}, u32[]{:S(2)}) %collective-permute-start.1) | collective-permute-done | bytes 262176 | tf_op jit(solution)/shard_map/ppermute | solution.py:363
  23.4 2.8 %collective-permute-done.5.refs_1_ = bf16[2,64,1024]{2,1,0:T(8,128)(2,1)S(1)} collective-permute-done((bf16[2,64,1024]{2,1,0:T(8,128)(2,1)S(1)}, bf16[2,64,1024]{2,1,0:T(8,128)(2,1)S(1)}, u32[]{:S(2)}, u32[]{:S(2)}) %collective-permute-start.5) | collective-permute-done | bytes 262176 | tf_op jit(solution)/shard_map/ppermute | solution.py:363
  26.2 3.0 %prepare.1 = (bf16[2,1024,1024]{2,1,0:T(8,128)(2,1)S(1)}, bf16[2,512,256]{2,1,0:T(8,128)(2,1)S(1)}, bf16[2,512,256]{2,1,0:T(8,128)(2,1)S(1)}, bf16[8,2,128,1024]{3,2,1,0:T(8,128)(2,1)S(1)}, f32[512,256]{1,0:T(8,128)S(1)}) custom-call(bf16[8,2,128,1024]{3,2,1,0:T(8,128)(2,1)} %bitcast.4, f32[512,256]{1,0:T(8,128)} %bitcast.5), custom_call_target="tpu_custom_call" | custom-call | flops 8388608 | bytes 8388608 | tf_op jit(solution)/shard_map/prepare/pallas_call | solution.py:192
  29.2 0.7 %shard_map.40.refs_2_ = f32[2,64,1024]{2,1,0:T(8,128)S(1)} custom-call(bf16[8,2,128,1024]{3,2,1,0:T(8,128)(2,1)S(1)} %get-tuple-element.21.green_ref, bf16[2,64,1024]{2,1,0:T(8,128)(2,1)S(1)} %get-tuple-element.29.refs_0_, bf16[2,128,1024]{2,1,0:T(8,128)(2,1)S(1)} %collective-permute-done.refs_1_, bf16[2,64,1024]{2,1,0:T(8,128)(2,1)S(1)} %collective-permute-done.12.refs_2_, ...), custom_call_target="tpu_custom_call" | custom-call | flops 2621440 | bytes 6291456 | tf_op jit(solution)/shard_map/pallas_call | solution.py:65
  30.2 0.9 %shard_map.42 = (bf16[2,64,256]{2,1,0:T(8,128)(2,1)S(1)}, bf16[2,64,256]{2,1,0:T(8,128)(2,1)S(1)}, bf16[2,64,256]{2,1,0:T(8,128)(2,1)S(1)}, bf16[2,64,256]{2,1,0:T(8,128)(2,1)S(1)}) custom-call(bf16[8,2,128,1024]{3,2,1,0:T(8,128)(2,1)S(1)} %get-tuple-element.21.green_ref, f32[2,64,1024]{2,1,0:T(8,128)S(1)} %shard_map.41.total_ref, ...), custom_call_target="tpu_custom_call" | custom-call | flops 536870912 | bytes 9437184 | tf_op jit(solution)/shard_map/pallas_call | solution.py:65
  31.1 2.1 %collective-permute-start.16 = (bf16[2,64,256]{2,1,0:T(8,128)(2,1)S(1)}, bf16[2,64,256]{2,1,0:T(8,128)(2,1)S(1)}, u32[]{:S(2)}, u32[]{:S(2)}) collective-permute-start(bf16[2,64,256]{2,1,0:T(8,128)(2,1)S(1)} %get-tuple-element.31), channel_id=1, source_target_pairs={{0,1},{1,2},{2,3},{3,0},{4,5},{5,6},{6,7},{7,4},{8,9},{9,10},{10,1... | collective-permute-start | bytes 196616 | tf_op jit(solution)/shard_map/ppermute | solution.py:384
  33.2 0.7 %shard_map.37.refs_2_ = f32[2,64,1024]{2,1,0:T(8,128)S(1)} custom-call(bf16[8,2,128,1024]{3,2,1,0:T(8,128)(2,1)S(1)} %get-tuple-element.21.green_ref, bf16[2,64,1024]{2,1,0:T(8,128)(2,1)S(1)} %get-tuple-element.22.refs_0_, bf16[2,128,1024]{2,1,0:T(8,128)(2,1)S(1)} %collective-permute-done.refs_1_, bf16[2,64,1024]{2,1,0:T(8,128)(2,1)S(1)} %collective-permute-done.3.refs_2_, ...), custom_call_target="tpu_custom_call" | custom-call | flops 2621440 | bytes 6291456 | tf_op jit(solution)/shard_map/pallas_call | solution.py:65
  33.9 2.6 %collective-permute-start.17 = (bf16[2,64,256]{2,1,0:T(8,128)(2,1)S(1)}, bf16[2,64,256]{2,1,0:T(8,128)(2,1)S(1)}, u32[]{:S(2)}, u32[]{:S(2)}) collective-permute-start(bf16[2,64,256]{2,1,0:T(8,128)(2,1)S(1)} %get-tuple-element.32), channel_id=1, source_target_pairs={{0,2},{1,3},{2,0},{3,1},{4,7},{5,4},{6,5},{7,6},{8,10},{9,11},{10,... | collective-permute-start | bytes 196616 | tf_op jit(solution)/shard_map/ppermute | solution.py:384
  36.6 1.3 %collective-permute-start.18 = (bf16[2,64,256]{2,1,0:T(8,128)(2,1)S(1)}, bf16[2,64,256]{2,1,0:T(8,128)(2,1)S(1)}, u32[]{:S(2)}, u32[]{:S(2)}) collective-permute-start(bf16[2,64,256]{2,1,0:T(8,128)(2,1)S(1)} %get-tuple-element.33), channel_id=1, source_target_pairs={{0,3},{1,0},{2,1},{3,2},{4,6},{5,7},{6,4},{7,5},{8,11},{9,8},{10,9... | collective-permute-start | bytes 196616 | tf_op jit(solution)/shard_map/ppermute | solution.py:384
  38.2 0.9 %shard_map.39 = (bf16[2,64,256]{2,1,0:T(8,128)(2,1)S(1)}, bf16[2,64,256]{2,1,0:T(8,128)(2,1)S(1)}, bf16[2,64,256]{2,1,0:T(8,128)(2,1)S(1)}, bf16[2,64,256]{2,1,0:T(8,128)(2,1)S(1)}) custom-call(bf16[8,2,128,1024]{3,2,1,0:T(8,128)(2,1)S(1)} %get-tuple-element.21.green_ref, f32[2,64,1024]{2,1,0:T(8,128)S(1)} %shard_map.38.total_ref, ...), custom_call_target="tpu_custom_call" | custom-call | flops 536870912 | bytes 9437184 | tf_op jit(solution)/shard_map/pallas_call | solution.py:65
  39.1 0.7 %collective-permute-start.7 = (bf16[2,64,256]{2,1,0:T(8,128)(2,1)S(1)}, bf16[2,64,256]{2,1,0:T(8,128)(2,1)S(1)}, u32[]{:S(2)}, u32[]{:S(2)}) collective-permute-start(bf16[2,64,256]{2,1,0:T(8,128)(2,1)S(1)} %get-tuple-element.25), channel_id=1, source_target_pairs={{0,1},{1,2},{2,3},{3,0},{4,5},{5,6},{6,7},{7,4},{8,9},{9,10},{10,1... | collective-permute-start | bytes 196616 | tf_op jit(solution)/shard_map/ppermute | solution.py:384
  40.1 2.8 %collective-permute-start.9 = (bf16[2,64,256]{2,1,0:T(8,128)(2,1)S(1)}, bf16[2,64,256]{2,1,0:T(8,128)(2,1)S(1)}, u32[]{:S(2)}, u32[]{:S(2)}) collective-permute-start(bf16[2,64,256]{2,1,0:T(8,128)(2,1)S(1)} %get-tuple-element.27), channel_id=1, source_target_pairs={{0,3},{1,0},{2,1},{3,2},{4,6},{5,7},{6,4},{7,5},{8,11},{9,8},{10,9... | collective-permute-start | bytes 196616 | tf_op jit(solution)/shard_map/ppermute | solution.py:384
  43.4 2.0 %collective-permute-done.7.refs_1_ = bf16[2,64,256]{2,1,0:T(8,128)(2,1)S(1)} collective-permute-done((bf16[2,64,256]{2,1,0:T(8,128)(2,1)S(1)}, bf16[2,64,256]{2,1,0:T(8,128)(2,1)S(1)}, u32[]{:S(2)}, u32[]{:S(2)}) %collective-permute-start.7) | collective-permute-done | bytes 65568 | tf_op jit(solution)/shard_map/ppermute | solution.py:384
  45.4 1.9 %collective-permute-done.8.refs_2_ = bf16[2,64,256]{2,1,0:T(8,128)(2,1)S(1)} collective-permute-done((bf16[2,64,256]{2,1,0:T(8,128)(2,1)S(1)}, bf16[2,64,256]{2,1,0:T(8,128)(2,1)S(1)}, u32[]{:S(2)}, u32[]{:S(2)}) %collective-permute-start.8) | collective-permute-done | bytes 65568 | tf_op jit(solution)/shard_map/ppermute | solution.py:384
  47.3 1.1 %transform_x_last.1 = bf16[2,512,256]{2,1,0:T(8,128)(2,1)} custom-call(bf16[2,512,256]{2,1,0:T(8,128)(2,1)S(1)} %get-tuple-element.20.table_ref, bf16[2,64,256]{2,1,0:T(8,128)(2,1)S(1)} %get-tuple-element.24.refs_0_, bf16[2,64,256]{2,1,0:T(8,128)(2,1)S(1)} %collective-permute-done.7.refs_1_, bf16[2,64,256]{2,1,0:T(8,128)(2,1)S(1)} %collective-permute-done.8.refs_2_, ...), custom_call_target="tpu_custom_call" | custom-call | flops 268435456 | bytes 4194304 | tf_op jit(solution)/shard_map/transform_x_last/pallas_call | solution.py:342
  (25 shorter events, 1.6 us)
Async XLA Ops:
  0.0 11.3 %collective-permute-start = (bf16[2,128,1024]{2,1,0:T(8,128)(2,1)}, bf16[2,128,1024]{2,1,0:T(8,128)(2,1)S(1)}, u32[]{:S(2)}, u32[]{:S(2)}) collective-permute-start(bf16[2,128,1024]{2,1,0:T(8,128)(2,1)} %bitcast.6), channel_id=1, source_target_pairs={{0,4},{4,0},{8,12},{12,8},{16,20},{20,16},{24,28},{28,24},{1,5},{5... | collective-permute-start | bytes 1572872 | tf_op jit(solution)/shard_map/ppermute | solution.py:363
  1.5 6.9 %collective-permute-start.12 = (bf16[2,64,1024]{2,1,0:T(8,128)(2,1)S(1)}, bf16[2,64,1024]{2,1,0:T(8,128)(2,1)S(1)}, u32[]{:S(2)}, u32[]{:S(2)}) collective-permute-start(bf16[2,64,1024]{2,1,0:T(8,128)(2,1)S(1)} %get-tuple-element.29.refs_0_), channel_id=1, source_target_pairs={{0,16},{4,12},{8,24},{12,4},{16,0},{20,28},{24,8},{28,20},{1,17},{... | collective-permute-start | bytes 786440 | tf_op jit(solution)/shard_map/ppermute | solution.py:363
  4.1 7.2 %collective-permute-start.3 = (bf16[2,64,1024]{2,1,0:T(8,128)(2,1)S(1)}, bf16[2,64,1024]{2,1,0:T(8,128)(2,1)S(1)}, u32[]{:S(2)}, u32[]{:S(2)}) collective-permute-start(bf16[2,64,1024]{2,1,0:T(8,128)(2,1)S(1)} %get-tuple-element.22.refs_0_), channel_id=1, source_target_pairs={{0,16},{4,12},{8,24},{12,4},{16,0},{20,28},{24,8},{28,20},{1,17},{... | collective-permute-start | bytes 786440 | tf_op jit(solution)/shard_map/ppermute | solution.py:363
  8.5 4.9 %collective-permute-start.13 = (bf16[2,64,1024]{2,1,0:T(8,128)(2,1)S(1)}, bf16[2,64,1024]{2,1,0:T(8,128)(2,1)S(1)}, u32[]{:S(2)}, u32[]{:S(2)}) collective-permute-start(bf16[2,64,1024]{2,1,0:T(8,128)(2,1)S(1)} %collective-permute-done.12.refs_2_), channel_id=1, source_target_pairs={{0,4},{4,0},{8,12},{12,8},{16,20},{20,16},{24,28},{28,24},{1,5},{5... | collective-permute-start | bytes 786440 | tf_op jit(solution)/shard_map/ppermute | solution.py:363
  11.3 4.2 %collective-permute-start.4 = (bf16[2,64,1024]{2,1,0:T(8,128)(2,1)S(1)}, bf16[2,64,1024]{2,1,0:T(8,128)(2,1)S(1)}, u32[]{:S(2)}, u32[]{:S(2)}) collective-permute-start(bf16[2,64,1024]{2,1,0:T(8,128)(2,1)S(1)} %collective-permute-done.3.refs_2_), channel_id=1, source_target_pairs={{0,4},{4,0},{8,12},{12,8},{16,20},{20,16},{24,28},{28,24},{1,5},{5... | collective-permute-start | bytes 786440 | tf_op jit(solution)/shard_map/ppermute | solution.py:363
  11.3 6.4 %collective-permute-start.10 = (bf16[2,64,1024]{2,1,0:T(8,128)(2,1)S(1)}, bf16[2,64,1024]{2,1,0:T(8,128)(2,1)S(1)}, u32[]{:S(2)}, u32[]{:S(2)}) collective-permute-start(bf16[2,64,1024]{2,1,0:T(8,128)(2,1)S(1)} %get-tuple-element.35), channel_id=1, source_target_pairs={{0,16},{4,12},{8,24},{12,4},{16,0},{20,28},{24,8},{28,20},{1,17},{... | collective-permute-start | bytes 786440 | tf_op jit(solution)/shard_map/ppermute | solution.py:363
  13.4 7.2 %collective-permute-start.14 = (bf16[2,64,1024]{2,1,0:T(8,128)(2,1)S(1)}, bf16[2,64,1024]{2,1,0:T(8,128)(2,1)S(1)}, u32[]{:S(2)}, u32[]{:S(2)}) collective-permute-start(bf16[2,64,1024]{2,1,0:T(8,128)(2,1)S(1)} %collective-permute-done.13.refs_3_), channel_id=1, source_target_pairs={{0,16},{4,12},{8,24},{12,4},{16,0},{20,28},{24,8},{28,20},{1,17},{... | collective-permute-start | bytes 786440 | tf_op jit(solution)/shard_map/ppermute | solution.py:363
  13.5 9.9 %collective-permute-start.1 = (bf16[2,64,1024]{2,1,0:T(8,128)(2,1)S(1)}, bf16[2,64,1024]{2,1,0:T(8,128)(2,1)S(1)}, u32[]{:S(2)}, u32[]{:S(2)}) collective-permute-start(bf16[2,64,1024]{2,1,0:T(8,128)(2,1)S(1)} %get-tuple-element.36), channel_id=1, source_target_pairs={{0,16},{4,12},{8,24},{12,4},{16,0},{20,28},{24,8},{28,20},{1,17},{... | collective-permute-start | bytes 786440 | tf_op jit(solution)/shard_map/ppermute | solution.py:363
  15.4 10.7 %collective-permute-start.5 = (bf16[2,64,1024]{2,1,0:T(8,128)(2,1)S(1)}, bf16[2,64,1024]{2,1,0:T(8,128)(2,1)S(1)}, u32[]{:S(2)}, u32[]{:S(2)}) collective-permute-start(bf16[2,64,1024]{2,1,0:T(8,128)(2,1)S(1)} %collective-permute-done.4.refs_3_), channel_id=1, source_target_pairs={{0,16},{4,12},{8,24},{12,4},{16,0},{20,28},{24,8},{28,20},{1,17},{... | collective-permute-start | bytes 786440 | tf_op jit(solution)/shard_map/ppermute | solution.py:363
  17.8 12.2 %collective-permute-start.11 = (bf16[2,64,1024]{2,1,0:T(8,128)(2,1)S(1)}, bf16[2,64,1024]{2,1,0:T(8,128)(2,1)S(1)}, u32[]{:S(2)}, u32[]{:S(2)}) collective-permute-start(bf16[2,64,1024]{2,1,0:T(8,128)(2,1)S(1)} %collective-permute-done.10.refs_4_), channel_id=1, source_target_pairs={{0,4},{4,0},{8,12},{12,8},{16,20},{20,16},{24,28},{28,24},{1,5},{5... | collective-permute-start | bytes 786440 | tf_op jit(solution)/shard_map/ppermute | solution.py:363
  20.6 9.6 %collective-permute-start.15 = (bf16[2,64,1024]{2,1,0:T(8,128)(2,1)S(1)}, bf16[2,64,1024]{2,1,0:T(8,128)(2,1)S(1)}, u32[]{:S(2)}, u32[]{:S(2)}) collective-permute-start(bf16[2,64,1024]{2,1,0:T(8,128)(2,1)S(1)} %collective-permute-done.14.refs_1_), channel_id=1, source_target_pairs={{0,4},{4,0},{8,12},{12,8},{16,20},{20,16},{24,28},{28,24},{1,5},{5... | collective-permute-start | bytes 786440 | tf_op jit(solution)/shard_map/ppermute | solution.py:363
  23.4 14.6 %collective-permute-start.2 = (bf16[2,64,1024]{2,1,0:T(8,128)(2,1)S(1)}, bf16[2,64,1024]{2,1,0:T(8,128)(2,1)S(1)}, u32[]{:S(2)}, u32[]{:S(2)}) collective-permute-start(bf16[2,64,1024]{2,1,0:T(8,128)(2,1)S(1)} %collective-permute-done.1.refs_4_), channel_id=1, source_target_pairs={{0,4},{4,0},{8,12},{12,8},{16,20},{20,16},{24,28},{28,24},{1,5},{5... | collective-permute-start | bytes 786440 | tf_op jit(solution)/shard_map/ppermute | solution.py:363
  26.2 12.0 %collective-permute-start.6 = (bf16[2,64,1024]{2,1,0:T(8,128)(2,1)S(1)}, bf16[2,64,1024]{2,1,0:T(8,128)(2,1)S(1)}, u32[]{:S(2)}, u32[]{:S(2)}) collective-permute-start(bf16[2,64,1024]{2,1,0:T(8,128)(2,1)S(1)} %collective-permute-done.5.refs_1_), channel_id=1, source_target_pairs={{0,4},{4,0},{8,12},{12,8},{16,20},{20,16},{24,28},{28,24},{1,5},{5... | collective-permute-start | bytes 786440 | tf_op jit(solution)/shard_map/ppermute | solution.py:363
  31.1 9.0 %collective-permute-start.16 = (bf16[2,64,256]{2,1,0:T(8,128)(2,1)S(1)}, bf16[2,64,256]{2,1,0:T(8,128)(2,1)S(1)}, u32[]{:S(2)}, u32[]{:S(2)}) collective-permute-start(bf16[2,64,256]{2,1,0:T(8,128)(2,1)S(1)} %get-tuple-element.31), channel_id=1, source_target_pairs={{0,1},{1,2},{2,3},{3,0},{4,5},{5,6},{6,7},{7,4},{8,9},{9,10},{10,1... | collective-permute-start | bytes 196616 | tf_op jit(solution)/shard_map/ppermute | solution.py:384
  33.9 9.0 %collective-permute-start.17 = (bf16[2,64,256]{2,1,0:T(8,128)(2,1)S(1)}, bf16[2,64,256]{2,1,0:T(8,128)(2,1)S(1)}, u32[]{:S(2)}, u32[]{:S(2)}) collective-permute-start(bf16[2,64,256]{2,1,0:T(8,128)(2,1)S(1)} %get-tuple-element.32), channel_id=1, source_target_pairs={{0,2},{1,3},{2,0},{3,1},{4,7},{5,4},{6,5},{7,6},{8,10},{9,11},{10,... | collective-permute-start | bytes 196616 | tf_op jit(solution)/shard_map/ppermute | solution.py:384
  36.6 6.4 %collective-permute-start.18 = (bf16[2,64,256]{2,1,0:T(8,128)(2,1)S(1)}, bf16[2,64,256]{2,1,0:T(8,128)(2,1)S(1)}, u32[]{:S(2)}, u32[]{:S(2)}) collective-permute-start(bf16[2,64,256]{2,1,0:T(8,128)(2,1)S(1)} %get-tuple-element.33), channel_id=1, source_target_pairs={{0,3},{1,0},{2,1},{3,2},{4,6},{5,7},{6,4},{7,5},{8,11},{9,8},{10,9... | collective-permute-start | bytes 196616 | tf_op jit(solution)/shard_map/ppermute | solution.py:384
  39.1 6.3 %collective-permute-start.7 = (bf16[2,64,256]{2,1,0:T(8,128)(2,1)S(1)}, bf16[2,64,256]{2,1,0:T(8,128)(2,1)S(1)}, u32[]{:S(2)}, u32[]{:S(2)}) collective-permute-start(bf16[2,64,256]{2,1,0:T(8,128)(2,1)S(1)} %get-tuple-element.25), channel_id=1, source_target_pairs={{0,1},{1,2},{2,3},{3,0},{4,5},{5,6},{6,7},{7,4},{8,9},{9,10},{10,1... | collective-permute-start | bytes 196616 | tf_op jit(solution)/shard_map/ppermute | solution.py:384
  39.8 7.5 %collective-permute-start.8 = (bf16[2,64,256]{2,1,0:T(8,128)(2,1)S(1)}, bf16[2,64,256]{2,1,0:T(8,128)(2,1)S(1)}, u32[]{:S(2)}, u32[]{:S(2)}) collective-permute-start(bf16[2,64,256]{2,1,0:T(8,128)(2,1)S(1)} %get-tuple-element.26), channel_id=1, source_target_pairs={{0,2},{1,3},{2,0},{3,1},{4,7},{5,4},{6,5},{7,6},{8,10},{9,11},{10,... | collective-permute-start | bytes 196616 | tf_op jit(solution)/shard_map/ppermute | solution.py:384
  40.1 7.2 %collective-permute-start.9 = (bf16[2,64,256]{2,1,0:T(8,128)(2,1)S(1)}, bf16[2,64,256]{2,1,0:T(8,128)(2,1)S(1)}, u32[]{:S(2)}, u32[]{:S(2)}) collective-permute-start(bf16[2,64,256]{2,1,0:T(8,128)(2,1)S(1)} %get-tuple-element.27), channel_id=1, source_target_pairs={{0,3},{1,0},{2,1},{3,2},{4,6},{5,7},{6,4},{7,5},{8,11},{9,8},{10,9... | collective-permute-start | bytes 196616 | tf_op jit(solution)/shard_map/ppermute | solution.py:384
